TPU v7x, 32 devices: a whole 2x2x4 slice. The times are simulated.
32 devices in a mesh: task: 4 (over x, core), tensor: 4 (over z), dp: 2 (over y).
Axes of the slice: x: 2, y: 2, z: 4, core: 2. Of those that a mesh axis runs over, the one named last changes fastest.
Arguments:
- hidden: bfloat16 [1024, 4608], P(('task', 'dp')), may hold values from -6 to 6
- pre_gain: float32 [4608], replicated, may hold values from 0.1 to 1.9
- base_query: bfloat16 [4608, 512], P('dp', 'tensor'), may hold values from -0.09375 to 0.09375
- base_keyval: bfloat16 [2, 4608, 256], P(None, 'dp', 'tensor'), may hold values from -0.09375 to 0.09375
- base_output: bfloat16 [512, 4608], P('tensor', 'dp'), may hold values from -0.25 to 0.25
- delta_query: bfloat16 [4, 4608, 512], P('task', 'dp', 'tensor'), may hold values from -0.046875 to 0.046875
- delta_keyval: bfloat16 [4, 2, 4608, 256], P('task', None, 'dp', 'tensor'), may hold values from -0.046875 to 0.046875
- delta_output: bfloat16 [4, 512, 4608], P('task', 'tensor', 'dp'), may hold values from -0.125 to 0.125
- trim_query: int32 [4, 72, 8], P('task', 'dp', 'tensor'), may hold values 0 or 1
- trim_keyval: int32 [4, 2, 72, 4], P('task', None, 'dp', 'tensor'), may hold values 0 or 1
- trim_output: int32 [4, 8, 72], P('task', 'tensor', 'dp'), may hold values 0 or 1
- sign_query: int32 [72, 8], P('dp', 'tensor'), may hold values from 0 to 1
- sign_keyval: int32 [2, 72, 4], P(None, 'dp', 'tensor'), may hold values from 0 to 1
- sign_output: int32 [8, 72], P('tensor', 'dp'), may hold values from 0 to 1
- post_gain: float32 [4608], replicated, may hold values from 0.1 to 1.9
- final_gain: float32 [4608], replicated, may hold values from 0.1 to 1.9
- unembedding: bfloat16 [28672, 4608], P(('task', 'tensor', 'dp')), may hold values from -0.375 to 0.375
- targets: int32 [1024], replicated, may hold values from 0 to 28671
- loss_mask: int32 [1024], replicated, may hold values 0 or 1
Outputs:
- token_loss: float32 [1024], P(('task', 'dp'))
- summary: float32 [2], replicated
All inputs are finite; a program needn't handle non-finite values. No bound on the sum of `trim_query` or of `trim_keyval` or of `trim_output` on one device may be relied on, other than what follows from the above.
Results may differ from a plain program's by a relative error of at most 0.0045.
Values may be sent and summed in bfloat16 or wider, within the bound.
No kernel may reach another device: no remote copies, remote signals or barrier semaphores. Data moves between devices by JAX's collectives and lax.ppermute only.
A program may use at most 128 MiB of HBM per device.

v0:
```python
import functools

import jax
import jax.numpy as jnp
from jax import lax
from jax.experimental import pallas as pl
from jax.experimental.pallas import tpu as pltpu
from jax.sharding import PartitionSpec as P


BLK = 64
LANES = 128

EPSILON = 1e-06
QUERY_SCALE = 1.0 / 12.0
ROPE_BASE = 10000.0
SCORE_CAP = 50.0
LOGIT_CAP = 30.0


VMEM = pl.BlockSpec(memory_space=pltpu.VMEM)
SMEM = pl.BlockSpec(memory_space=pltpu.SMEM)


def kernel_call(body, inputs, in_specs, outputs, scratch=(), flops=1, transcendentals=0):
    moved = sum(a.size * a.dtype.itemsize for a in inputs)
    moved += sum(int(jnp.dtype(o.dtype).itemsize) * o.size for o in outputs)
    return pl.pallas_call(
        body,
        out_shape=outputs,
        in_specs=in_specs,
        out_specs=[VMEM] * len(outputs),
        scratch_shapes=list(scratch),
        cost_estimate=pl.CostEstimate(
            flops=flops, bytes_accessed=moved, transcendentals=transcendentals
        ),
    )(*inputs)


def shape_of(dims, dtype):
    return jax.ShapeDtypeStruct(tuple(dims), dtype)


def swap(block, axis, mask):
    count = lax.axis_size(axis)
    return lax.ppermute(block, axis, [(i, i ^ mask) for i in range(count)])


def swap_two(block, task_mask, dp_mask):
    tasks, halves = lax.axis_size("task"), lax.axis_size("dp")
    route = []
    for t in range(tasks):
        for d in range(halves):
            route.append((t * halves + d, (t ^ task_mask) * halves + (d ^ dp_mask)))
    return lax.ppermute(block, ("task", "dp"), route)


def gather_group(block):
    tasks, halves = lax.axis_size("task"), lax.axis_size("dp")
    near = [(0, 0, block)]
    for tm in range(0, tasks, 2):
        for dm in range(halves):
            if tm or dm:
                if not dm:
                    got = swap(block, "task", tm)
                elif not tm:
                    got = swap(block, "dp", dm)
                else:
                    got = swap_two(block, tm, dm)
                near.append((tm, dm, got))
    return near + [(tm ^ 1, dm, swap(b, "task", 1)) for tm, dm, b in near]


def after(values, earlier):
    count = len(values)
    return list(lax.optimization_barrier(tuple(values) + tuple(earlier))[:count])


def total_over(value, axis):
    count = lax.axis_size(axis)
    if count <= 4:
        parts = [swap(value, axis, m) for m in range(1, count)]
        for part in parts:
            value = value + part
        return value
    step = 1
    while step < count:
        value = value + swap(value, axis, step)
        step *= 2
    return value


def total_over_group(value):
    tasks, halves = lax.axis_size("task"), lax.axis_size("dp")
    parts = []
    for tm in range(0, tasks, 2):
        for dm in range(halves):
            if tm or dm:
                parts.append(swap_two(value, tm, dm))
    for part in parts:
        value = value + part
    return value + swap(value, "task", 1)


def block_code(trim, sign):
    return (trim * (2 * sign - 1)).astype(jnp.float32)


def transpose_columns(source, out_ref):
    for c in range(out_ref.shape[0] // LANES):
        out_ref[c * LANES : (c + 1) * LANES, :] = source(c).astype(jnp.float32).T


def keyval_tile(ref, c):
    both = ref[:, :, c * LANES : (c + 1) * LANES]
    return both.reshape(2 * both.shape[1], LANES)


def trim_input_body(tasks, place, tq, tkv, sq, skv, dq, dkv, *rest):
    outs, turned = rest[:-1], rest[-1]
    me = place[0]
    transpose_columns(lambda c: keyval_tile(dkv.at[0], c), turned)
    rows = outs[0].shape[0]
    blocks = rows // BLK
    low = lax.broadcasted_iota(jnp.int32, (BLK, LANES), 1) < BLK
    for j in range(tasks):
        first = (me ^ j) * blocks
        for r in range(blocks):
            b = first + r
            at = pl.ds(pl.multiple_of(b * BLK, BLK), BLK)
            here = slice(r * BLK, (r + 1) * BLK)
            code = jnp.where(
                low, block_code(tq[0, 0, b], sq[0, b]), block_code(tq[0, 1, b], sq[1, b])
            )
            d = dq[0, at, :].astype(jnp.float32)
            outs[j][here, :LANES] = jnp.where(d * code > 0, d, 0.0).astype(jnp.bfloat16)
            code = jnp.where(
                low, block_code(tkv[0, 0, 0, b], skv[0, 0, b]), block_code(tkv[0, 1, 0, b], skv[1, 0, b])
            )
            d = turned[at, :]
            outs[j][here, LANES:] = jnp.where(d * code > 0, d, 0.0).astype(jnp.bfloat16)


def trim_output_body(tasks, place, to, so, do, *outs):
    me = place[0]
    rows, width = outs[0].shape
    low = lax.broadcasted_iota(jnp.int32, (rows, LANES), 1) < BLK
    for j in range(tasks):
        first = (me ^ j) * rows
        at = pl.ds(pl.multiple_of(first, rows), rows)
        b = first // BLK
        for c in range(width // LANES):
            cols = slice(c * LANES, (c + 1) * LANES)
            code = jnp.where(
                low,
                block_code(to[0, b, 2 * c], so[b, 2 * c]),
                block_code(to[0, b, 2 * c + 1], so[b, 2 * c + 1]),
            )
            d = do[0, at, cols].astype(jnp.float32)
            outs[j][:, cols] = jnp.where(d * code > 0, d, 0.0).astype(jnp.bfloat16)


def base_input_body(place, bq, bkv, out, turned):
    transpose_columns(lambda c: keyval_tile(bkv, c), turned)
    rows = out.shape[0]
    at = pl.ds(pl.multiple_of(place[0] * rows, BLK), rows)
    out[:, :LANES] = bq[at, :]
    out[:, LANES:] = turned[at, :].astype(jnp.bfloat16)


def merged(base, parts, gain=1.0):
    total = jnp.zeros(base.shape, jnp.float32)
    count = jnp.zeros(base.shape, jnp.float32)
    for part in parts:
        value = part.astype(jnp.float32)
        total = total + value
        count = count + jnp.where(value != 0, 1.0, 0.0)
    value = base.astype(jnp.float32) + total / jnp.maximum(count, 1.0)
    return (value * gain).astype(jnp.bfloat16)


def merge_input_body(base, *refs):
    out = refs[-1]
    step = BLK
    for r in range(out.shape[0] // step):
        at = slice(r * step, (r + 1) * step)
        out[at, :] = merged(base[at, :], [p[at, :] for p in refs[:-1]])


def merge_output_body(place, gain, base, *refs):
    out = refs[-1]
    rows, width = out.shape
    start = place[1] * width
    at = pl.ds(pl.multiple_of(place[0] * rows, rows), rows)
    step = 4 * LANES
    for c in range(0, width, step):
        cols = slice(c, min(c + step, width))
        size = min(c + step, width) - c
        factor = gain[0:1, pl.ds(pl.multiple_of(start + c, LANES), size)]
        out[:, cols] = merged(base[at, cols], [p[:, cols] for p in refs[:-1]], factor)


def turn(values, cosine, sine):
    return values * cosine + pltpu.roll(values, values.shape[-1] // 2, 1) * sine


def project_body(masks, tasks, place, normed, cosine, sine, *refs):
    pieces, q_out, kv_out = refs[:-2], refs[-2], refs[-1]
    total = jnp.zeros((q_out.shape[0], 2 * LANES), jnp.float32)
    for (tm, dm), piece in zip(masks, pieces):
        block = (place[1] ^ dm) * tasks + (place[0] ^ tm)
        total = total + jnp.dot(normed[block], piece[...], preferred_element_type=jnp.float32)
    q = turn(total[:, :LANES], cosine[...], sine[...])
    q_out[...] = (q * QUERY_SCALE).astype(jnp.bfloat16)
    kv_out[...] = total[:, LANES:].astype(jnp.bfloat16)


def join_body(place, cosine, sine, own, other, out):
    mine, theirs = own[...].astype(jnp.float32), other[...].astype(jnp.float32)
    even = place[2] % 2 == 0
    first = jnp.where(even, mine, theirs)
    second = jnp.where(even, theirs, mine)
    low = lax.broadcasted_iota(jnp.int32, first.shape, 1) < LANES // 2
    keys = jnp.where(low, first, pltpu.roll(second, LANES // 2, 1))
    values = jnp.where(low, pltpu.roll(first, LANES // 2, 1), second)
    out[:, :LANES] = turn(keys, cosine[...], sine[...]).astype(jnp.bfloat16)
    out[:, LANES:] = values.astype(jnp.bfloat16)


def attend_body(masks, halves, place, q_ref, *refs):
    pieces, out = refs[:-1], refs[-1]
    rows = q_ref.shape[0]
    q = q_ref[...]
    mine = place[0] * halves + place[1]
    row = lax.broadcasted_iota(jnp.int32, (rows, rows), 0)
    col = lax.broadcasted_iota(jnp.int32, (rows, rows), 1)
    top = jnp.zeros((rows, LANES), jnp.float32)
    bottom = jnp.zeros((rows, 1), jnp.float32)
    for (tm, dm), piece in zip(masks, pieces):
        theirs = (place[0] ^ tm) * halves + (place[1] ^ dm)
        scores = lax.dot_general(
            q, piece[:, :LANES], (((1,), (1,)), ((), ())), preferred_element_type=jnp.float32
        )
        capped = SCORE_CAP * jnp.tanh(scores / SCORE_CAP)
        allowed = col + theirs * rows <= row + mine * rows
        weights = jnp.where(allowed, jnp.exp(capped), 0.0)
        bottom = bottom + jnp.sum(weights, axis=1, keepdims=True)
        top = top + jnp.dot(
            weights.astype(jnp.bfloat16), piece[:, LANES:], preferred_element_type=jnp.float32
        )
    out[...] = (top / bottom).astype(jnp.bfloat16)


def output_body(masks, place, attention, *refs):
    pieces, out, whole = refs[:-2], refs[-2], refs[-1]
    for (tm, dm), piece in zip(masks, pieces):
        whole[place[1] ^ dm, place[0] ^ tm] = piece[...]
    halves, tasks, rows, width = whole.shape
    for h in range(halves):
        weight = whole[h].reshape(tasks * rows, width)
        out[:, h * width : (h + 1) * width] = jnp.dot(
            attention[...], weight, preferred_element_type=jnp.float32
        ).astype(jnp.bfloat16)


def heads_body(masks, place, *refs):
    parts, out = refs[:-1], refs[-1]
    for m, part in zip(masks, parts):
        out[:, pl.ds(pl.multiple_of((place[2] ^ m) * LANES, LANES), LANES)] = part[...]


def assemble_body(labels, place, *refs):
    pieces, plain = refs[:-1], refs[-1]
    rows, half = plain.shape[2], pieces[0].shape[1]
    for (tm, dm, first), piece in zip(labels, pieces):
        h, t = place[1] ^ dm, place[0] ^ tm
        cols = pl.ds(pl.multiple_of(h * half, LANES), half)
        for m in range(piece.shape[0] // rows):
            plain[place[2] ^ (first + m), t, :, cols] = piece[m * rows : (m + 1) * rows, :]


def statistics_body(attention, weight, hidden, to_plain, to_post, out):
    rows, width = hidden.shape
    step = width // 4
    squares = jnp.zeros((rows, 1), jnp.float32)
    parts = []
    for c in range(0, width, step):
        p = jnp.dot(
            attention[...], weight[:, c : c + step], preferred_element_type=jnp.float32
        )
        plain = p * to_plain[0:1, c : c + step]
        squares = squares + jnp.sum(plain * plain, axis=1, keepdims=True)
        parts.append(p)
    inner = lax.rsqrt(squares / width + EPSILON)
    squares = jnp.zeros((rows, 1), jnp.float32)
    for i, p in enumerate(parts):
        cols = slice(i * step, (i + 1) * step)
        stream = hidden[:, cols].astype(jnp.float32) + p * inner * to_post[0:1, cols]
        squares = squares + jnp.sum(stream * stream, axis=1, keepdims=True)
    outer = lax.rsqrt(squares / width + EPSILON)
    lane = lax.broadcasted_iota(jnp.int32, (rows, LANES), 1)
    table = jnp.where(lane == 0, inner, jnp.where(lane == 1, outer, 0.0))
    out[...] = table.T[: out.shape[0], :]


def contract_body(count, table, *refs):
    left, out, total = refs[:count], refs[count], refs[count + 1]
    step = pl.program_id(0)
    rows = [ref[...] for ref in left]
    product = lax.dot_general(
        jnp.concatenate(rows, axis=0) if count > 1 else rows[0],
        table[...],
        (((1,), (1,)), ((), ())),
        preferred_element_type=jnp.float32,
    )

    @pl.when(step == 0)
    def _():
        total[...] = product

    @pl.when(step > 0)
    def _():
        total[...] += product

    @pl.when(step == pl.num_programs(0) - 1)
    def _():
        out[...] = total[...].astype(out.dtype)


def contract(left, table, dtype):
    width = table.shape[1]
    step = width // 4 if width % (4 * LANES) == 0 else width
    rows = sum(block.shape[0] for block in left)
    vocab = table.shape[0]
    return pl.pallas_call(
        functools.partial(contract_body, len(left)),
        out_shape=shape_of((rows, vocab), dtype),
        grid=(width // step,),
        in_specs=[pl.BlockSpec((vocab, step), lambda k: (0, k))]
        + [pl.BlockSpec((block.shape[0], step), lambda k: (0, k)) for block in left],
        out_specs=pl.BlockSpec((rows, vocab), lambda k: (0, 0)),
        scratch_shapes=[pltpu.VMEM((rows, vocab), jnp.float32)],
        name="contract",
        cost_estimate=pl.CostEstimate(
            flops=2 * rows * width * vocab,
            bytes_accessed=2 * (rows + vocab) * width + 4 * rows * vocab,
            transcendentals=0,
        ),
    )(table, *left)


def score_body(masks, halves, place, targets, mixed, *refs):
    count = len(masks)
    attention, stats = refs[:count], refs[count : 2 * count]
    near, far, out = refs[2 * count :]
    rows = attention[0].shape[0]
    vocab = mixed.shape[1]
    first_id = place[3]
    lane = lax.broadcasted_iota(jnp.int32, (rows, LANES), 1)
    for n, (tm, dm) in enumerate(masks):
        group = (place[0] ^ tm) * halves + (place[1] ^ dm)
        table = stats[n][...].T
        wanted = jnp.broadcast_to(targets[pl.ds(group, 1), :], (8, rows)).T
        inner, outer, wanted = table[:, 0:1], table[:, 1:2], wanted[:, 0:1]
        base = far if tm > 1 else near
        start = (halves * (tm % 2) + dm) * rows
        sums = jnp.zeros((rows, LANES), jnp.float32)
        hits = jnp.zeros((rows, LANES), jnp.float32)
        product = jnp.dot(attention[n][...], mixed[...], preferred_element_type=jnp.float32)
        for v in range(vocab // LANES):
            cols = slice(v * LANES, (v + 1) * LANES)
            logits = outer * (base[start : start + rows, cols] + inner * product[:, cols])
            capped = LOGIT_CAP * jnp.tanh(logits / LOGIT_CAP)
            sums = sums + jnp.exp(capped)
            hits = hits + jnp.where(lane + (first_id + v * LANES) == wanted, capped, 0.0)
        for kind, value in ((0, sums), (1, hits)):
            out[kind, pl.ds(group, 1), :] = jnp.sum(value.T, axis=0, keepdims=True)


def loss_body(halves, place, mask, first, second, own, summary):
    both = first[...] + second[...]
    counted = mask[...].astype(jnp.float32)
    losses = (jnp.log(both[0]) - both[1]) * counted
    at = pl.ds(place[0] * halves + place[1], 1)
    sumexp = first[0, at, :] + second[0, at, :]
    target = first[1, at, :] + second[1, at, :]
    own[...] = (jnp.log(sumexp) - target) * mask[at, :].astype(jnp.float32)
    summary[0] = jnp.sum(losses)
    summary[1] = jnp.sum(counted)


def rms_norm(values, gain):
    scale = lax.rsqrt(jnp.mean(values * values, axis=-1, keepdims=True) + EPSILON)
    return values * scale * gain


def general_tail(
    place, masks, attention, piece_out, hidden, post_gain, final_gain, unembedding, targets, loss_mask
):
    bf16, f32 = jnp.bfloat16, jnp.float32
    tasks = lax.axis_size("task")
    tensors = lax.axis_size("tensor")
    halves = lax.axis_size("dp")
    task, dp, tensor = lax.axis_index("task"), lax.axis_index("dp"), lax.axis_index("tensor")
    row_count, width = hidden.shape
    out_rows, half = piece_out.shape
    residual = hidden.astype(f32)
    group_index = task * halves + dp
    pieces_out = gather_group(piece_out)
    partial_value = kernel_call(
        functools.partial(output_body, masks),
        [place, attention] + [b for _, _, b in pieces_out],
        [SMEM] + [VMEM] * (1 + len(masks)),
        [shape_of((row_count, width), bf16)],
        [pltpu.VMEM((halves, tasks, out_rows, half), bf16)],
        flops=2 * row_count * width * LANES,
    )[0]

    span_rows = row_count // tensors
    share_rows = lax.psum_scatter(partial_value, "tensor", scatter_dimension=0, tiled=True).astype(f32)
    own_stream = lax.dynamic_slice_in_dim(residual, tensor * span_rows, span_rows, 0)
    stream = own_stream + rms_norm(share_rows, post_gain)
    final = rms_norm(stream, final_gain).astype(bf16)
    every_rows = lax.all_gather(final, ("task", "tensor", "dp"), axis=0, tiled=True)

    def order(values):
        return jnp.transpose(
            values.reshape(tasks, halves, tensors, span_rows), (0, 2, 1, 3)
        ).reshape(-1)

    ordered_targets, ordered_mask = order(targets), order(loss_mask)
    logits = lax.dot_general(
        every_rows, unembedding, (((1,), (1,)), ((), ())), preferred_element_type=f32
    )
    capped = LOGIT_CAP * jnp.tanh(logits / LOGIT_CAP)
    vocab_ids = lax.axis_index(("task", "tensor", "dp")) * unembedding.shape[0] + jnp.arange(
        unembedding.shape[0], dtype=jnp.int32
    )
    local_sumexp = jnp.sum(jnp.exp(capped), axis=1)
    local_target = jnp.sum(
        jnp.where(ordered_targets[:, None] == vocab_ids[None, :], capped, 0.0), axis=1
    )
    both = jnp.stack([local_sumexp, local_target])
    both = total_over_group(total_over(both, "tensor"))
    sumexp, target_logit = both[0], both[1]
    counted = ordered_mask.astype(f32)
    losses = (jnp.log(sumexp) - target_logit) * counted
    summary = jnp.stack([jnp.sum(losses), jnp.sum(counted)])
    losses = jnp.transpose(
        losses.reshape(tasks, tensors, halves, span_rows), (0, 2, 1, 3)
    ).reshape(-1)
    own_losses = lax.dynamic_slice_in_dim(losses, group_index * row_count, row_count, 0)
    return (own_losses, summary)


def exchange_hidden(hidden, kept, tensor):
    tensors = lax.axis_size("tensor")
    rows = hidden.shape[0] // tensors
    cut = hidden.shape[0] // 2
    hidden = after([hidden], [kept])[0]
    share = lax.dynamic_slice_in_dim(hidden, tensor * rows, rows, 0)
    top, bottom = hidden[:cut], hidden[cut:]
    dp_top = swap(top, "dp", 1)
    by_task = swap(share, "task", 2)
    dp_bottom = swap(bottom, "dp", 1)
    task_all = jnp.zeros_like(hidden)
    for m in range(tensors):
        block = swap(by_task, "tensor", m) if m else by_task
        task_all = lax.dynamic_update_slice_in_dim(task_all, block, (tensor ^ m) * rows, 0)
    both_top = swap(dp_top, "task", 2)
    both_bottom = swap(task_all[cut:], "dp", 1)

    def paired(blocks):
        return blocks + [swap(block, "task", 1) for block in blocks]

    return paired([hidden, dp_top, dp_bottom]), paired([task_all, both_top, both_bottom])


def split_tail(
    where,
    attention,
    piece_out,
    inverse_gains,
    far_rows,
    near,
    hidden,
    unembedding,
    targets,
    loss_mask,
):
    bf16, f32 = jnp.bfloat16, jnp.float32
    tasks = lax.axis_size("task")
    tensors = lax.axis_size("tensor")
    halves = lax.axis_size("dp")
    row_count, width = hidden.shape
    out_rows, _ = piece_out.shape
    groups = tasks * halves
    vocab = unembedding.shape[0]
    place = where
    to_plain, to_post = inverse_gains

    column = jnp.concatenate([piece_out] + [swap(piece_out, "tensor", m) for m in range(1, tensors)], axis=0)
    by_task, by_dp = swap(column, "task", 2), swap(column, "dp", 1)
    cut = column.shape[0] // 2
    parts = [
        (0, 0, 0, column),
        (2, 0, 0, by_task),
        (0, 1, 0, by_dp),
        (2, 1, 0, swap(by_dp[:cut], "task", 2)),
        (2, 1, cut // out_rows, swap(by_task[cut:], "dp", 1)),
    ]
    parts += [(tm ^ 1, dm, first, swap(b, "task", 1)) for tm, dm, first, b in parts]
    plain = kernel_call(
        functools.partial(assemble_body, [part[:3] for part in parts]),
        [place] + [part[3] for part in parts],
        [SMEM] + [VMEM] * len(parts),
        [shape_of((tensors, tasks, out_rows, width), bf16)],
    )[0]
    features = tensors * tasks * out_rows
    plain = plain.reshape(features, width)
    mixed = contract([plain], unembedding, bf16)

    heads = kernel_call(
        functools.partial(heads_body, list(range(tensors))),
        [place, attention] + [swap(attention, "tensor", m) for m in range(1, tensors)],
        [SMEM] + [VMEM] * tensors,
        [shape_of((row_count, features), bf16)],
    )[0]
    stats = kernel_call(
        statistics_body,
        [heads, plain, hidden, to_plain, to_post],
        [VMEM] * 5,
        [shape_of((8, row_count), f32)],
        flops=2 * row_count * features * width,
    )[0]
    every_heads = gather_group(heads)
    far = contract(far_rows, unembedding, f32)
    every_stats = gather_group(stats)
    both = kernel_call(
        functools.partial(score_body, [(tm, dm) for tm, dm, _ in every_heads], halves),
        [where, targets.reshape(groups, row_count), mixed]
        + [b for _, _, b in every_heads]
        + [b for _, _, b in every_stats]
        + [near, far],
        [SMEM] + [VMEM] * (4 + 2 * groups),
        [shape_of((2, groups, row_count), f32)],
        flops=2 * groups * row_count * features * vocab,
        transcendentals=2 * groups * row_count * vocab,
    )[0]
    both = total_over(both, "tensor")
    parts = [swap_two(both, tm, dm) for tm in range(0, tasks, 2) for dm in range(halves) if tm or dm]
    for part in parts:
        both = both + part
    own, summary = pl.pallas_call(
        functools.partial(loss_body, halves),
        out_shape=[shape_of((1, row_count), f32), shape_of((2,), f32)],
        in_specs=[SMEM] + [VMEM] * 3,
        out_specs=[VMEM, SMEM],
        name="loss",
    )(place, loss_mask.reshape(groups, row_count), both, swap(both, "task", 1))
    return own.reshape(row_count), summary


def on_device(
    hidden,
    pre_gain,
    base_query,
    base_keyval,
    base_output,
    delta_query,
    delta_keyval,
    delta_output,
    trim_query,
    trim_keyval,
    trim_output,
    sign_query,
    sign_keyval,
    sign_output,
    post_gain,
    final_gain,
    unembedding,
    targets,
    loss_mask,
):
    bf16, f32 = jnp.bfloat16, jnp.float32
    tasks = lax.axis_size("task")
    tensors = lax.axis_size("tensor")
    halves = lax.axis_size("dp")
    task, dp, tensor = lax.axis_index("task"), lax.axis_index("dp"), lax.axis_index("tensor")
    place = jnp.stack([task, dp, tensor]).astype(jnp.int32)
    row_count, width = hidden.shape
    half = base_query.shape[0]
    quarter = half // tasks
    out_rows = base_output.shape[0] // tasks

    kept_in = kernel_call(
        functools.partial(trim_input_body, tasks),
        [
            place,
            jnp.swapaxes(trim_query, 1, 2),
            jnp.swapaxes(trim_keyval, 2, 3),
            sign_query.T,
            jnp.swapaxes(sign_keyval, 1, 2),
            delta_query,
            jnp.swapaxes(delta_keyval, 2, 3),
        ],
        [SMEM] * 5 + [VMEM] * 2,
        [shape_of((quarter, 2 * LANES), bf16)] * tasks,
        [pltpu.VMEM((half, LANES), f32)],
    )
    got_in = [kept_in[0]] + [swap(kept_in[j], "task", j) for j in range(1, tasks)]
    kept_out = kernel_call(
        functools.partial(trim_output_body, tasks),
        [place, trim_output, sign_output, delta_output],
        [SMEM] * 3 + [VMEM],
        [shape_of((out_rows, half), bf16)] * tasks,
    )
    base_in = kernel_call(
        base_input_body,
        [place, base_query, jnp.swapaxes(base_keyval, 1, 2)],
        [SMEM] + [VMEM] * 2,
        [shape_of((quarter, 2 * LANES), bf16)],
        [pltpu.VMEM((half, LANES), f32)],
    )[0]

    residual = hidden.astype(f32)
    normed = rms_norm(residual, pre_gain).astype(bf16)
    blocks = width // quarter
    normed = jnp.transpose(normed.reshape(row_count, blocks, quarter), (1, 0, 2))
    group_index = task * halves + dp
    query_positions = group_index * row_count + jnp.arange(row_count, dtype=jnp.int32)
    half_head = LANES // 2
    frequencies = jnp.exp(
        -jnp.log(ROPE_BASE) * 2.0 * jnp.arange(half_head, dtype=jnp.int32).astype(f32) / LANES
    )
    angles = query_positions.astype(f32)[:, None] * frequencies[None, :]
    cosine, sine = jnp.cos(angles), jnp.sin(angles)
    cosine = jnp.concatenate([cosine, cosine], axis=1)
    sine = jnp.concatenate([-sine, sine], axis=1)

    gathered_bytes = tensors * base_output.shape[0] * width * base_output.dtype.itemsize
    low_rank = gathered_bytes <= 6 * 2**20
    where = jnp.concatenate(
        [place, (lax.axis_index(("task", "tensor", "dp")) * unembedding.shape[0]).astype(jnp.int32)[None]]
    )
    if low_rank:
        weight_gain = (post_gain * final_gain)[None, :]
        rows = [weight_gain, 1.0 / weight_gain, (1.0 / final_gain)[None, :], where]
    else:
        rows = [jnp.ones((1, width), f32), where]
    tied = after(list(got_in) + rows, [])
    got_in, rows = tied[:tasks], tied[tasks:]
    weight_gain, where = rows[0], rows[-1]
    piece_in = kernel_call(
        merge_input_body,
        [base_in] + got_in,
        [VMEM] * (1 + tasks),
        [shape_of((quarter, 2 * LANES), bf16)],
    )[0]
    pieces_in = gather_group(piece_in)
    masks = [(tm, dm) for tm, dm, _ in pieces_in]

    kept_out = after(kept_out, [piece_in])
    got_out = [kept_out[0]] + [swap(kept_out[j], "task", j) for j in range(1, tasks)]
    got_out = after(got_out, [b for _, _, b in pieces_in[1:4]])
    if low_rank:
        scaled = (hidden.astype(f32) * final_gain).astype(bf16)
        near_rows, far_rows = exchange_hidden(scaled, kept_in[0], tensor)
        near_rows = after(near_rows, [piece_in])
        near = contract(near_rows, unembedding, f32)
    piece_out = kernel_call(
        merge_output_body,
        [place, weight_gain, base_output] + got_out,
        [SMEM] + [VMEM] * (2 + tasks),
        [shape_of((out_rows, half), bf16)],
    )[0]

    queries, keyval = kernel_call(
        functools.partial(project_body, masks, tasks),
        [place, normed, cosine, sine] + [b for _, _, b in pieces_in],
        [SMEM] + [VMEM] * (3 + len(masks)),
        [shape_of((row_count, LANES), bf16)] * 2,
        flops=2 * row_count * width * 2 * LANES,
    )
    other = swap(keyval, "tensor", 1)
    joined = kernel_call(
        join_body,
        [place, cosine, sine, keyval, other],
        [SMEM] + [VMEM] * 4,
        [shape_of((row_count, 2 * LANES), bf16)],
    )[0]
    every_keyval = gather_group(joined)
    if low_rank:
        queries = after([queries], [near])[0]
    attention = kernel_call(
        functools.partial(attend_body, masks, halves),
        [place, queries] + [b for _, _, b in every_keyval],
        [SMEM] + [VMEM] * (1 + len(masks)),
        [shape_of((row_count, LANES), bf16)],
        flops=4 * row_count * row_count * LANES * len(masks),
        transcendentals=2 * row_count * row_count * len(masks),
    )[0]
    if not low_rank:
        return general_tail(
            place, masks, attention, piece_out, hidden, post_gain, final_gain, unembedding, targets, loss_mask
        )
    return split_tail(
        where,
        attention,
        piece_out,
        rows[1:3],
        far_rows,
        near,
        hidden,
        unembedding,
        targets,
        loss_mask,
    )


def solution(mesh):
    return jax.shard_map(
        on_device,
        mesh=mesh,
        in_specs=(
            P(("task", "dp"), None),
            P(),
            P("dp", "tensor"),
            P(None, "dp", "tensor"),
            P("tensor", "dp"),
            P("task", "dp", "tensor"),
            P("task", None, "dp", "tensor"),
            P("task", "tensor", "dp"),
            P("task", "dp", "tensor"),
            P("task", None, "dp", "tensor"),
            P("task", "tensor", "dp"),
            P("dp", "tensor"),
            P(None, "dp", "tensor"),
            P("tensor", "dp"),
            P(),
            P(),
            P(("task", "tensor", "dp"), None),
            P(),
            P(),
        ),
        out_specs=(P(("task", "dp")), P()),
        check_vma=False,
    )
```

profile of v0, /device:TPU:0, one launch (start us, length us, event | category | flops | bytes accessed | tf_op | source)
XLA Modules:
  0.0 217.0 jit_solution(7112550141392295694)
XLA Ops:
  1.3 2.6 %shard_map.194 = (bf16[576,256]{1,0:T(8,128)(2,1)}, bf16[576,256]{1,0:T(8,128)(2,1)}, bf16[576,256]{1,0:T(8,128)(2,1)}, bf16[576,256]{1,0:T(8,128)(2,1)}) custom-call(s32[3]{0:T(128)} %pad_add_fusion.place, s32[1,2,36]{2,1,0:T(2,128)} %bitcast.28, s32[1,2,1,36]{3,2,1,0:T(1,128)} %bitcast.29, s32[2,36]{1,0:T(2,128)} %bitcast.30, s32[2,1,36]{2,1,0:T(1,128)} %bitcast.31, ...), custom_call_target="tpu_custom_call" | custom-call | flops 1 | bytes 2360460 | tf_op jit(solution)/shard_map/pallas_call | solution.py:28
  4.4 2.5 %collective-permute-start.1 = (bf16[576,256]{1,0:T(8,128)(2,1)}, bf16[576,256]{1,0:T(8,128)(2,1)}, u32[]{:S(2)}, u32[]{:S(2)}) collective-permute-start(bf16[576,256]{1,0:T(8,128)(2,1)} %get-tuple-element.40), channel_id=1, source_target_pairs={{0,16},{8,24},{16,0},{24,8},{1,17},{9,25},{17,1},{25,9},{2,18},{10... | collective-permute-start | bytes 884744 | tf_op jit(solution)/shard_map/ppermute | solution.py:46
  7.3 2.2 %shard_map.196.base = bf16[576,256]{1,0:T(8,128)(2,1)} custom-call(s32[3]{0:T(128)} %pad_add_fusion.place, bf16[2304,128]{1,0:T(8,128)(2,1)} %bq.1, bf16[2,64,2304]{2,1,0:T(8,128)(2,1)} %bitcast.25), custom_call_target="tpu_custom_call" | custom-call | flops 1 | bytes 1474572 | tf_op jit(solution)/shard_map/pallas_call | solution.py:28
  13.4 1.7 collective-permute-done.1.refs_2_
  15.0 6.0 %collective-permute-done.2.refs_3_ = bf16[576,256]{1,0:T(8,128)(2,1)} collective-permute-done((bf16[576,256]{1,0:T(8,128)(2,1)}, bf16[576,256]{1,0:T(8,128)(2,1)}, u32[]{:S(2)}, u32[]{:S(2)}) %collective-permute-start.2) | collective-permute-done | bytes 294944 | tf_op jit(solution)/shard_map/ppermute | solution.py:46
  21.0 2.5 %shard_map.197.refs_0_ = bf16[576,256]{1,0:T(8,128)(2,1)} custom-call(bf16[576,256]{1,0:T(8,128)(2,1)} %shard_map.196.base, bf16[576,256]{1,0:T(8,128)(2,1)} %get-tuple-element.48.refs_0_, bf16[576,256]{1,0:T(8,128)(2,1)} %collective-permute-done.refs_1_, bf16[576,256]{1,0:T(8,128)(2,1)} %collective-permute-done.1.refs_2_, ...), custom_call_target="tpu_custom_call" | custom-call | flops 1 | bytes 1769472 | tf_op jit(solution)/shard_map/pallas_call | solution.py:28
  23.5 1.5 collective-permute-start.6
  25.0 1.5 collective-permute-start.7
  27.7 1.5 collective-permute-start.55
  29.2 2.2 %shard_map.195 = (bf16[32,2304]{1,0:T(8,128)(2,1)}, bf16[32,2304]{1,0:T(8,128)(2,1)}, bf16[32,2304]{1,0:T(8,128)(2,1)}, bf16[32,2304]{1,0:T(8,128)(2,1)}) custom-call(s32[3]{0:T(128)} %pad_add_fusion.place, s32[1,2,36]{2,1,0:T(2,128)} %to.1, s32[2,36]{1,0:T(2,128)} %so.1, bf16[1,128,2304]{2,1,0:T(8,128)(2,1)} %do.1), custom_call_target="tpu_custom_call" | custom-call | flops 1 | bytes 1180236 | tf_op jit(solution)/shard_map/pallas_call | solution.py:28
  32.2 1.4 copy.27
  35.2 6.3 %collective-permute-done.8.refs_3_ = bf16[576,256]{1,0:T(8,128)(2,1)} collective-permute-done((bf16[576,256]{1,0:T(8,128)(2,1)}, bf16[576,256]{1,0:T(8,128)(2,1)}, u32[]{:S(2)}, u32[]{:S(2)}) %collective-permute-start.8) | collective-permute-done | bytes 294944 | tf_op jit(solution)/shard_map/ppermute | solution.py:55
  43.1 1.5 collective-permute-start.4
  45.4 3.3 %shard_map.200 = (bf16[128,128]{1,0:T(8,128)(2,1)}, bf16[128,128]{1,0:T(8,128)(2,1)}) custom-call(s32[3]{0:T(128)} %pad_add_fusion.place, bf16[8,128,576]{2,1,0:T(8,128)(2,1)} %bitcast.22, f32[128,128]{1,0:T(8,128)} %get-tuple-element.84.cosine, f32[128,128]{1,0:T(8,128)} %get-tuple-element.85.sine, bf16[576,256]{1,0:T(8,128)(2,1)} %shard_map.197.refs_0_, ...), custom_call_target="tpu_custom_call" | custom-call | flops 301989888 | bytes 3735564 | tf_op jit(solution)/shard_map/pallas_call | solution.py:28
  48.6 1.6 collective-permute-start.30
  51.1 1.5 collective-permute-start.25
  53.6 2.6 %collective-permute-start.57 = (bf16[32,4608]{1,0:T(8,128)(2,1)}, bf16[32,4608]{1,0:T(8,128)(2,1)}, u32[]{:S(2)}, u32[]{:S(2)}) collective-permute-start(bf16[32,4608]{1,0:T(8,128)(2,1)} %collective-permute-done.55), channel_id=1, source_target_pairs={{0,4},{2,6},{4,0},{6,2},{1,5},{3,7},{5,1},{7,3},{8,12},{10,14},{12... | collective-permute-start | bytes 884744 | tf_op jit(solution)/shard_map/ppermute | solution.py:46
  56.2 1.7 collective-permute-start.58
  59.0 2.1 shard_map.198
  61.1 1.7 shard_map.201.refs_0_
  62.8 4.8 %collective-permute-done.25.refs_1_ = bf16[64,4608]{1,0:T(8,128)(2,1)} collective-permute-done((bf16[64,4608]{1,0:T(8,128)(2,1)}, bf16[64,4608]{1,0:T(8,128)(2,1)}, u32[]{:S(2)}, u32[]{:S(2)}) %collective-permute-start.25) | collective-permute-done | bytes 589856 | tf_op jit(solution)/shard_map/ppermute | solution.py:46
  67.6 12.0 %collective-permute-done.26.refs_2_ = bf16[64,4608]{1,0:T(8,128)(2,1)} collective-permute-done((bf16[64,4608]{1,0:T(8,128)(2,1)S(1)}, bf16[64,4608]{1,0:T(8,128)(2,1)}, u32[]{:S(2)}, u32[]{:S(2)}) %collective-permute-start.26) | collective-permute-done | bytes 589856 | tf_op jit(solution)/shard_map/ppermute | solution.py:46
  79.6 2.5 %collective-permute-start.11 = (bf16[32,2304]{1,0:T(8,128)(2,1)}, bf16[32,2304]{1,0:T(8,128)(2,1)S(1)}, u32[]{:S(2)}, u32[]{:S(2)}) collective-permute-start(bf16[32,2304]{1,0:T(8,128)(2,1)} %shard_map.198), channel_id=1, source_target_pairs={{0,6},{2,4},{4,2},{6,0},{1,7},{3,5},{5,3},{7,1},{8,14},{10,12},{12... | collective-permute-start | bytes 442376 | tf_op jit(solution)/shard_map/ppermute | solution.py:46
  82.2 1.8 collective-permute-start.9
  84.0 1.5 collective-permute-start.31
  86.5 1.9 collective-permute-done.11
  88.4 7.0 %collective-permute-done.10 = bf16[32,2304]{1,0:T(8,128)(2,1)S(1)} collective-permute-done((bf16[32,2304]{1,0:T(8,128)(2,1)}, bf16[32,2304]{1,0:T(8,128)(2,1)S(1)}, u32[]{:S(2)}, u32[]{:S(2)}) %collective-permute-start.10) | collective-permute-done | bytes 147488 | tf_op jit(solution)/shard_map/ppermute | solution.py:46
  95.4 1.6 collective-permute-start.32
  100.1 2.3 %collective-permute-done.33.refs_3_ = bf16[128,256]{1,0:T(8,128)(2,1)S(1)} collective-permute-done((bf16[128,256]{1,0:T(8,128)(2,1)}, bf16[128,256]{1,0:T(8,128)(2,1)S(1)}, u32[]{:S(2)}, u32[]{:S(2)}) %collective-permute-start.33) | collective-permute-done | bytes 65568 | tf_op jit(solution)/shard_map/ppermute | solution.py:55
  102.6 1.6 collective-permute-start.59
  109.1 10.2 %contract.4.refs_16_ = f32[512,896]{1,0:T(8,128)} custom-call(bf16[896,4608]{1,0:T(8,128)(2,1)} %table.5, bf16[128,4608]{1,0:T(8,128)(2,1)} %copy-done.1, bf16[64,4608]{1,0:T(8,128)(2,1)} %collective-permute-done.25.refs_1_, bf16[64,4608]{1,0:T(8,128)(2,1)} %collective-permute-done.26.refs_2_, bf16[128,4608]{1,0:T(8,128)(2,1)} %copy-done.47, ...), custom_call_target="tpu_custom_call" | custom-call | flops 4227858432 | bytes 14811136 | tf_op jit(solution)/shard_map/contract/pallas_call | solution.py:335
  119.3 2.3 %shard_map.202.refs_0_ = bf16[128,128]{1,0:T(8,128)(2,1)} custom-call(s32[3]{0:T(128)} %pad_add_fusion.place, bf16[128,128]{1,0:T(8,128)(2,1)} %get-tuple-element.68.q_ref, bf16[128,256]{1,0:T(8,128)(2,1)} %shard_map.201.refs_0_, bf16[128,256]{1,0:T(8,128)(2,1)} %copy-done.27, bf16[128,256]{1,0:T(8,128)(2,1)} %copy-done.28, bf16[128,256]{1,0:T(8,128)(2,1)} %copy-done.29, ...), custom_call_target="tpu_custom_call" | custom-call | flops 67108864 | bytes 589836 | tf_op jit(solution)/shard_map/pallas_call | solution.py:28
  121.8 9.4 %collective-permute-done.12.refs_1_ = bf16[128,2304]{1,0:T(8,128)(2,1)S(1)} collective-permute-done((bf16[128,2304]{1,0:T(8,128)(2,1)S(1)}, bf16[128,2304]{1,0:T(8,128)(2,1)S(1)}, u32[]{:S(2)}, u32[]{:S(2)}) %collective-permute-start.12) | collective-permute-done | bytes 589856 | tf_op jit(solution)/shard_map/ppermute | solution.py:46
  131.2 3.0 %collective-permute-start.40 = (bf16[128,128]{1,0:T(8,128)(2,1)}, bf16[128,128]{1,0:T(8,128)(2,1)S(1)}, u32[]{:S(2)}, u32[]{:S(2)}) collective-permute-start(bf16[128,128]{1,0:T(8,128)(2,1)} %shard_map.202.refs_0_), channel_id=1, source_target_pairs={{0,6},{2,4},{4,2},{6,0},{1,7},{3,5},{5,3},{7,1},{8,14},{10,12},{12... | collective-permute-start | bytes 98312 | tf_op jit(solution)/shard_map/ppermute | solution.py:46
  134.4 2.5 %collective-permute-done.39.refs_2_ = bf16[128,128]{1,0:T(8,128)(2,1)S(1)} collective-permute-done((bf16[128,128]{1,0:T(8,128)(2,1)}, bf16[128,128]{1,0:T(8,128)(2,1)S(1)}, u32[]{:S(2)}, u32[]{:S(2)}) %collective-permute-start.39) | collective-permute-done | bytes 32800 | tf_op jit(solution)/shard_map/ppermute | solution.py:46
  136.9 2.0 collective-permute-start.14
  139.0 5.0 %collective-permute-done.14.refs_3_ = bf16[64,2304]{1,0:T(8,128)(2,1)} collective-permute-done((bf16[64,2304]{1,0:T(8,128)(2,1)S(1)}, bf16[64,2304]{1,0:T(8,128)(2,1)}, u32[]{:S(2)}, u32[]{:S(2)}) %collective-permute-start.14) | collective-permute-done | bytes 294944 | tf_op jit(solution)/shard_map/ppermute | solution.py:46
  144.0 1.7 collective-permute-done.15.refs_4_
  145.9 1.5 shard_map.203.attention.refs_0_
  149.2 4.2 %collective-permute-done.41.refs_1_ = bf16[128,512]{1,0:T(8,128)(2,1)S(1)} collective-permute-done((bf16[128,512]{1,0:T(8,128)(2,1)}, bf16[128,512]{1,0:T(8,128)(2,1)S(1)}, u32[]{:S(2)}, u32[]{:S(2)}) %collective-permute-start.41) | collective-permute-done | bytes 131104 | tf_op jit(solution)/shard_map/ppermute | solution.py:46
  157.7 4.8 %shard_map.199 = bf16[4,4,32,4608]{3,2,1,0:T(8,128)(2,1)} custom-call(s32[4]{0:T(128)} %pad_add_fusion.1.place, bf16[128,2304]{1,0:T(8,128)(2,1)} %copy-done.3, bf16[128,2304]{1,0:T(8,128)(2,1)} %copy-done.4, bf16[128,2304]{1,0:T(8,128)(2,1)} %copy-done.5, bf16[64,2304]{1,0:T(8,128)(2,1)} %collective-permute-done.14.refs_3_, ...), custom_call_target="tpu_custom_call" | custom-call | flops 1 | bytes 9437200 | tf_op jit(solution)/shard_map/pallas_call | solution.py:28
  162.4 5.0 %shard_map.204.refs_8_ = f32[8,128]{1,0:T(8,128)} custom-call(bf16[128,512]{1,0:T(8,128)(2,1)} %shard_map.203.attention.refs_0_, bf16[512,4608]{1,0:T(8,128)(2,1)} %bitcast.20, bf16[128,4608]{1,0:T(8,128)(2,1)} %hidden.1, f32[1,4608]{1,0:T(1,128)} %div.27.to_plain, f32[1,4608]{1,0:T(1,128)} %broadcast_in_dim.18.to_post), custom_call_target="tpu_custom_call" | custom-call | flops 603979776 | bytes 6070272 | tf_op jit(solution)/shard_map/pallas_call | solution.py:28
  171.6 10.2 %contract.5.refs_17_ = f32[512,896]{1,0:T(8,128)} custom-call(bf16[896,4608]{1,0:T(8,128)(2,1)} %table.5, bf16[128,4608]{1,0:T(8,128)(2,1)} %copy-done.2, bf16[64,4608]{1,0:T(8,128)(2,1)} %collective-permute-done.59.refs_1_, bf16[64,4608]{1,0:T(8,128)(2,1)} %collective-permute-done.60.refs_2_, bf16[128,4608]{1,0:T(8,128)(2,1)} %collective-permute-done.61.refs_3_, ...), custom_call_target="tpu_custom_call" | custom-call | flops 4227858432 | bytes 14811136 | tf_op jit(solution)/shard_map/contract/pallas_call | solution.py:335
  183.1 9.8 %contract.3.mixed = bf16[512,896]{1,0:T(8,128)(2,1)} custom-call(bf16[896,4608]{1,0:T(8,128)(2,1)} %table.5, bf16[512,4608]{1,0:T(8,128)(2,1)} %bitcast.21), custom_call_target="tpu_custom_call" | custom-call | flops 4227858432 | bytes 14811136 | tf_op jit(solution)/shard_map/contract/pallas_call | solution.py:335
  193.7 5.7 %shard_map.205 = f32[2,8,128]{2,1,0:T(8,128)} custom-call(s32[4]{0:T(128)} %pad_add_fusion.1.place, s32[8,128]{1,0:T(8,128)} %bitcast.26, bf16[512,896]{1,0:T(8,128)(2,1)} %contract.3.mixed, bf16[128,512]{1,0:T(8,128)(2,1)} %shard_map.203.attention.refs_0_, bf16[128,512]{1,0:T(8,128)(2,1)} %copy-done.21, bf16[128,512]{1,0:T(8,128)(2,1)} %collective-permute-done.42.refs_2_, ...), custom_call_target="tpu_custom_call" | custom-call | flops 939524096 | bytes 5681168 | tf_op jit(solution)/shard_map/pallas_call | solution.py:28
  199.4 2.2 %collective-permute-start.66 = (f32[2,8,128]{2,1,0:T(8,128)}, f32[2,8,128]{2,1,0:T(8,128)S(1)}, u32[]{:S(2)}, u32[]{:S(2)}) collective-permute-start(f32[2,8,128]{2,1,0:T(8,128)} %shard_map.205), channel_id=1, source_target_pairs={{0,6},{2,4},{4,2},{6,0},{1,7},{3,5},{5,3},{7,1},{8,14},{10,12},{12... | collective-permute-start | bytes 24584 | tf_op jit(solution)/shard_map/ppermute | solution.py:46
  202.1 1.7 collective-permute-start.64
  207.1 1.6 collective-permute-start.69
  (240 shorter events, 47.6 us)
Async XLA Ops:
  3.9 9.5 %collective-permute-start = (bf16[576,256]{1,0:T(8,128)(2,1)}, bf16[576,256]{1,0:T(8,128)(2,1)}, u32[]{:S(2)}, u32[]{:S(2)}) collective-permute-start(bf16[576,256]{1,0:T(8,128)(2,1)} %get-tuple-element.39), channel_id=1, source_target_pairs={{0,8},{8,0},{16,24},{24,16},{1,9},{9,1},{17,25},{25,17},{2,10},{10... | collective-permute-start | bytes 884744 | tf_op jit(solution)/shard_map/ppermute | solution.py:46
  4.4 10.7 %collective-permute-start.1 = (bf16[576,256]{1,0:T(8,128)(2,1)}, bf16[576,256]{1,0:T(8,128)(2,1)}, u32[]{:S(2)}, u32[]{:S(2)}) collective-permute-start(bf16[576,256]{1,0:T(8,128)(2,1)} %get-tuple-element.40), channel_id=1, source_target_pairs={{0,16},{8,24},{16,0},{24,8},{1,17},{9,25},{17,1},{25,9},{2,18},{10... | collective-permute-start | bytes 884744 | tf_op jit(solution)/shard_map/ppermute | solution.py:46
  6.9 14.1 %collective-permute-start.2 = (bf16[576,256]{1,0:T(8,128)(2,1)}, bf16[576,256]{1,0:T(8,128)(2,1)}, u32[]{:S(2)}, u32[]{:S(2)}) collective-permute-start(bf16[576,256]{1,0:T(8,128)(2,1)} %get-tuple-element.41), channel_id=1, source_target_pairs={{0,24},{8,16},{16,8},{24,0},{1,25},{9,17},{17,9},{25,1},{2,26},{10... | collective-permute-start | bytes 884744 | tf_op jit(solution)/shard_map/ppermute | solution.py:46
  23.5 10.2 %collective-permute-start.6 = (bf16[576,256]{1,0:T(8,128)(2,1)}, bf16[576,256]{1,0:T(8,128)(2,1)}, u32[]{:S(2)}, u32[]{:S(2)}) collective-permute-start(bf16[576,256]{1,0:T(8,128)(2,1)} %shard_map.197.refs_0_), channel_id=1, source_target_pairs={{0,1},{1,0},{2,3},{3,2},{4,5},{5,4},{6,7},{7,6},{8,9},{9,8},{10,11... | collective-permute-start | bytes 884744 | tf_op jit(solution)/shard_map/ppermute | solution.py:46
  25.0 10.2 %collective-permute-start.7 = (bf16[576,256]{1,0:T(8,128)(2,1)}, bf16[576,256]{1,0:T(8,128)(2,1)}, u32[]{:S(2)}, u32[]{:S(2)}) collective-permute-start(bf16[576,256]{1,0:T(8,128)(2,1)} %shard_map.197.refs_0_), channel_id=1, source_target_pairs={{0,16},{8,24},{16,0},{24,8},{1,17},{9,25},{17,1},{25,9},{2,18},{10... | collective-permute-start | bytes 884744 | tf_op jit(solution)/shard_map/ppermute | solution.py:46
  26.5 15.0 %collective-permute-start.8 = (bf16[576,256]{1,0:T(8,128)(2,1)}, bf16[576,256]{1,0:T(8,128)(2,1)}, u32[]{:S(2)}, u32[]{:S(2)}) collective-permute-start(bf16[576,256]{1,0:T(8,128)(2,1)} %shard_map.197.refs_0_), channel_id=1, source_target_pairs={{0,17},{1,16},{8,25},{9,24},{16,1},{17,0},{24,9},{25,8},{2,19},{3,... | collective-permute-start | bytes 884744 | tf_op jit(solution)/shard_map/ppermute | solution.py:55
  27.7 23.3 %collective-permute-start.55 = (bf16[32,4608]{1,0:T(8,128)(2,1)}, bf16[32,4608]{1,0:T(8,128)(2,1)}, u32[]{:S(2)}, u32[]{:S(2)}) collective-permute-start(bf16[32,4608]{1,0:T(8,128)(2,1)} %constant_dynamic-slice_fusion), channel_id=1, source_target_pairs={{0,16},{8,24},{16,0},{24,8},{1,17},{9,25},{17,1},{25,9},{2,18},{10... | collective-permute-start | bytes 884744 | tf_op jit(solution)/shard_map/ppermute | solution.py:46
  33.6 8.9 %collective-permute-start.21 = (bf16[576,256]{1,0:T(8,128)(2,1)S(1)}, bf16[576,256]{1,0:T(8,128)(2,1)S(1)}, u32[]{:S(2)}, u32[]{:S(2)}) collective-permute-start(bf16[576,256]{1,0:T(8,128)(2,1)S(1)} %copy-done.6), channel_id=1, source_target_pairs={{0,8},{8,0},{16,24},{24,16},{1,9},{9,1},{17,25},{25,17},{2,10},{10... | collective-permute-start | bytes 884744 | tf_op jit(solution)/shard_map/ppermute | solution.py:46
  33.7 9.3 %collective-permute-start.22 = (bf16[576,256]{1,0:T(8,128)(2,1)}, bf16[576,256]{1,0:T(8,128)(2,1)S(1)}, u32[]{:S(2)}, u32[]{:S(2)}) collective-permute-start(bf16[576,256]{1,0:T(8,128)(2,1)} %collective-permute-done.6.refs_1_), channel_id=1, source_target_pairs={{0,8},{8,0},{16,24},{24,16},{1,9},{9,1},{17,25},{25,17},{2,10},{10... | collective-permute-start | bytes 884744 | tf_op jit(solution)/shard_map/ppermute | solution.py:46
  35.2 9.3 %collective-permute-start.23 = (bf16[576,256]{1,0:T(8,128)(2,1)}, bf16[576,256]{1,0:T(8,128)(2,1)S(1)}, u32[]{:S(2)}, u32[]{:S(2)}) collective-permute-start(bf16[576,256]{1,0:T(8,128)(2,1)} %collective-permute-done.7.refs_2_), channel_id=1, source_target_pairs={{0,8},{8,0},{16,24},{24,16},{1,9},{9,1},{17,25},{25,17},{2,10},{10... | collective-permute-start | bytes 884744 | tf_op jit(solution)/shard_map/ppermute | solution.py:46
  42.5 10.1 %collective-permute-start.3 = (bf16[32,2304]{1,0:T(8,128)(2,1)}, bf16[32,2304]{1,0:T(8,128)(2,1)S(1)}, u32[]{:S(2)}, u32[]{:S(2)}) collective-permute-start(bf16[32,2304]{1,0:T(8,128)(2,1)} %get-tuple-element.53), channel_id=1, source_target_pairs={{0,8},{8,0},{16,24},{24,16},{1,9},{9,1},{17,25},{25,17},{2,10},{10... | collective-permute-start | bytes 442376 | tf_op jit(solution)/shard_map/ppermute | solution.py:46
  43.1 10.1 %collective-permute-start.4 = (bf16[32,2304]{1,0:T(8,128)(2,1)}, bf16[32,2304]{1,0:T(8,128)(2,1)S(1)}, u32[]{:S(2)}, u32[]{:S(2)}) collective-permute-start(bf16[32,2304]{1,0:T(8,128)(2,1)} %get-tuple-element.54), channel_id=1, source_target_pairs={{0,16},{8,24},{16,0},{24,8},{1,17},{9,25},{17,1},{25,9},{2,18},{10... | collective-permute-start | bytes 442376 | tf_op jit(solution)/shard_map/ppermute | solution.py:46
  44.5 9.0 %collective-permute-start.5 = (bf16[32,2304]{1,0:T(8,128)(2,1)S(1)}, bf16[32,2304]{1,0:T(8,128)(2,1)S(1)}, u32[]{:S(2)}, u32[]{:S(2)}) collective-permute-start(bf16[32,2304]{1,0:T(8,128)(2,1)S(1)} %copy-done.50), channel_id=1, source_target_pairs={{0,24},{8,16},{16,8},{24,0},{1,25},{9,17},{17,9},{25,1},{2,26},{10... | collective-permute-start | bytes 442376 | tf_op jit(solution)/shard_map/ppermute | solution.py:46
  51.1 16.5 %collective-permute-start.25 = (bf16[64,4608]{1,0:T(8,128)(2,1)}, bf16[64,4608]{1,0:T(8,128)(2,1)}, u32[]{:S(2)}, u32[]{:S(2)}) collective-permute-start(bf16[64,4608]{1,0:T(8,128)(2,1)} %get-tuple-element.77), channel_id=1, source_target_pairs={{0,1},{1,0},{2,3},{3,2},{4,5},{5,4},{6,7},{7,6},{8,9},{9,8},{10,11... | collective-permute-start | bytes 1769480 | tf_op jit(solution)/shard_map/ppermute | solution.py:46
  52.6 27.0 %collective-permute-start.26 = (bf16[64,4608]{1,0:T(8,128)(2,1)S(1)}, bf16[64,4608]{1,0:T(8,128)(2,1)}, u32[]{:S(2)}, u32[]{:S(2)}) collective-permute-start(bf16[64,4608]{1,0:T(8,128)(2,1)S(1)} %get-tuple-element.76), channel_id=1, source_target_pairs={{0,1},{1,0},{2,3},{3,2},{4,5},{5,4},{6,7},{7,6},{8,9},{9,8},{10,11... | collective-permute-start | bytes 1769480 | tf_op jit(solution)/shard_map/ppermute | solution.py:46
  53.1 29.0 %collective-permute-start.56 = (bf16[32,4608]{1,0:T(8,128)(2,1)}, bf16[32,4608]{1,0:T(8,128)(2,1)}, u32[]{:S(2)}, u32[]{:S(2)}) collective-permute-start(bf16[32,4608]{1,0:T(8,128)(2,1)} %collective-permute-done.55), channel_id=1, source_target_pairs={{0,2},{2,0},{4,6},{6,4},{1,3},{3,1},{5,7},{7,5},{8,10},{10,8},{12,... | collective-permute-start | bytes 884744 | tf_op jit(solution)/shard_map/ppermute | solution.py:46
  53.6 28.6 %collective-permute-start.57 = (bf16[32,4608]{1,0:T(8,128)(2,1)}, bf16[32,4608]{1,0:T(8,128)(2,1)}, u32[]{:S(2)}, u32[]{:S(2)}) collective-permute-start(bf16[32,4608]{1,0:T(8,128)(2,1)} %collective-permute-done.55), channel_id=1, source_target_pairs={{0,4},{2,6},{4,0},{6,2},{1,5},{3,7},{5,1},{7,3},{8,12},{10,14},{12... | collective-permute-start | bytes 884744 | tf_op jit(solution)/shard_map/ppermute | solution.py:46
  56.2 27.8 %collective-permute-start.58 = (bf16[32,4608]{1,0:T(8,128)(2,1)}, bf16[32,4608]{1,0:T(8,128)(2,1)S(1)}, u32[]{:S(2)}, u32[]{:S(2)}) collective-permute-start(bf16[32,4608]{1,0:T(8,128)(2,1)} %collective-permute-done.55), channel_id=1, source_target_pairs={{0,6},{2,4},{4,2},{6,0},{1,7},{3,5},{5,3},{7,1},{8,14},{10,12},{12... | collective-permute-start | bytes 884744 | tf_op jit(solution)/shard_map/ppermute | solution.py:46
  67.6 37.7 %collective-permute-start.27 = (bf16[128,4608]{1,0:T(8,128)(2,1)S(1)}, bf16[128,4608]{1,0:T(8,128)(2,1)S(1)}, u32[]{:S(2)}, u32[]{:S(2)}) collective-permute-start(bf16[128,4608]{1,0:T(8,128)(2,1)S(1)} %get-tuple-element.62.refs_0_), channel_id=1, source_target_pairs={{0,8},{8,0},{16,24},{24,16},{1,9},{9,1},{17,25},{25,17},{2,10},{10... | collective-permute-start | bytes 3538952 | tf_op jit(solution)/shard_map/ppermute | solution.py:46
  79.6 8.8 %collective-permute-start.11 = (bf16[32,2304]{1,0:T(8,128)(2,1)}, bf16[32,2304]{1,0:T(8,128)(2,1)S(1)}, u32[]{:S(2)}, u32[]{:S(2)}) collective-permute-start(bf16[32,2304]{1,0:T(8,128)(2,1)} %shard_map.198), channel_id=1, source_target_pairs={{0,6},{2,4},{4,2},{6,0},{1,7},{3,5},{5,3},{7,1},{8,14},{10,12},{12... | collective-permute-start | bytes 442376 | tf_op jit(solution)/shard_map/ppermute | solution.py:46
  82.1 13.3 %collective-permute-start.10 = (bf16[32,2304]{1,0:T(8,128)(2,1)}, bf16[32,2304]{1,0:T(8,128)(2,1)S(1)}, u32[]{:S(2)}, u32[]{:S(2)}) collective-permute-start(bf16[32,2304]{1,0:T(8,128)(2,1)} %shard_map.198), channel_id=1, source_target_pairs={{0,4},{2,6},{4,0},{6,2},{1,5},{3,7},{5,1},{7,3},{8,12},{10,14},{12... | collective-permute-start | bytes 442376 | tf_op jit(solution)/shard_map/ppermute | solution.py:46
  82.2 13.2 %collective-permute-start.9 = (bf16[32,2304]{1,0:T(8,128)(2,1)}, bf16[32,2304]{1,0:T(8,128)(2,1)S(1)}, u32[]{:S(2)}, u32[]{:S(2)}) collective-permute-start(bf16[32,2304]{1,0:T(8,128)(2,1)} %shard_map.198), channel_id=1, source_target_pairs={{0,2},{2,0},{4,6},{6,4},{1,3},{3,1},{5,7},{7,5},{8,10},{10,8},{12,... | collective-permute-start | bytes 442376 | tf_op jit(solution)/shard_map/ppermute | solution.py:46
  84.0 13.0 %collective-permute-start.31 = (bf16[128,256]{1,0:T(8,128)(2,1)}, bf16[128,256]{1,0:T(8,128)(2,1)S(1)}, u32[]{:S(2)}, u32[]{:S(2)}) collective-permute-start(bf16[128,256]{1,0:T(8,128)(2,1)} %shard_map.201.refs_0_), channel_id=1, source_target_pairs={{0,1},{1,0},{2,3},{3,2},{4,5},{5,4},{6,7},{7,6},{8,9},{9,8},{10,11... | collective-permute-start | bytes 196616 | tf_op jit(solution)/shard_map/ppermute | solution.py:46
  88.4 17.7 %collective-permute-start.28 = (bf16[64,4608]{1,0:T(8,128)(2,1)}, bf16[64,4608]{1,0:T(8,128)(2,1)S(1)}, u32[]{:S(2)}, u32[]{:S(2)}) collective-permute-start(bf16[64,4608]{1,0:T(8,128)(2,1)} %collective-permute-done.25.refs_1_), channel_id=1, source_target_pairs={{0,8},{8,0},{16,24},{24,16},{1,9},{9,1},{17,25},{25,17},{2,10},{10... | collective-permute-start | bytes 1769480 | tf_op jit(solution)/shard_map/ppermute | solution.py:46
  95.4 10.7 %collective-permute-start.29 = (bf16[64,4608]{1,0:T(8,128)(2,1)}, bf16[64,4608]{1,0:T(8,128)(2,1)S(1)}, u32[]{:S(2)}, u32[]{:S(2)}) collective-permute-start(bf16[64,4608]{1,0:T(8,128)(2,1)} %collective-permute-done.26.refs_2_), channel_id=1, source_target_pairs={{0,8},{8,0},{16,24},{24,16},{1,9},{9,1},{17,25},{25,17},{2,10},{10... | collective-permute-start | bytes 1769480 | tf_op jit(solution)/shard_map/ppermute | solution.py:46
  102.6 19.0 %collective-permute-start.59 = (bf16[64,4608]{1,0:T(8,128)(2,1)}, bf16[64,4608]{1,0:T(8,128)(2,1)}, u32[]{:S(2)}, u32[]{:S(2)}) collective-permute-start(bf16[64,4608]{1,0:T(8,128)(2,1)} %collective-permute-done.25.refs_1_), channel_id=1, source_target_pairs={{0,16},{8,24},{16,0},{24,8},{1,17},{9,25},{17,1},{25,9},{2,18},{10... | collective-permute-start | bytes 1769480 | tf_op jit(solution)/shard_map/ppermute | solution.py:46
  104.2 27.0 %collective-permute-start.12 = (bf16[128,2304]{1,0:T(8,128)(2,1)S(1)}, bf16[128,2304]{1,0:T(8,128)(2,1)S(1)}, u32[]{:S(2)}, u32[]{:S(2)}) collective-permute-start(bf16[128,2304]{1,0:T(8,128)(2,1)S(1)} %pad_maximum_fusion.refs_0_), channel_id=1, source_target_pairs={{0,16},{8,24},{16,0},{24,8},{1,17},{9,25},{17,1},{25,9},{2,18},{10... | collective-permute-start | bytes 1769480 | tf_op jit(solution)/shard_map/ppermute | solution.py:46
  105.3 25.9 %collective-permute-start.13 = (bf16[128,2304]{1,0:T(8,128)(2,1)S(1)}, bf16[128,2304]{1,0:T(8,128)(2,1)S(1)}, u32[]{:S(2)}, u32[]{:S(2)}) collective-permute-start(bf16[128,2304]{1,0:T(8,128)(2,1)S(1)} %pad_maximum_fusion.refs_0_), channel_id=1, source_target_pairs={{0,1},{1,0},{2,3},{3,2},{4,5},{5,4},{6,7},{7,6},{8,9},{9,8},{10,11... | collective-permute-start | bytes 1769480 | tf_op jit(solution)/shard_map/ppermute | solution.py:46
  107.6 39.8 %collective-permute-start.60 = (bf16[64,4608]{1,0:T(8,128)(2,1)}, bf16[64,4608]{1,0:T(8,128)(2,1)}, u32[]{:S(2)}, u32[]{:S(2)}) collective-permute-start(bf16[64,4608]{1,0:T(8,128)(2,1)} %slice.22), channel_id=1, source_target_pairs={{0,1},{1,0},{2,3},{3,2},{4,5},{5,4},{6,7},{7,6},{8,9},{9,8},{10,11... | collective-permute-start | bytes 1769480 | tf_op jit(solution)/shard_map/ppermute | solution.py:46
  109.0 39.0 %collective-permute-start.16 = (bf16[128,2304]{1,0:T(8,128)(2,1)S(1)}, bf16[128,2304]{1,0:T(8,128)(2,1)S(1)}, u32[]{:S(2)}, u32[]{:S(2)}) collective-permute-start(bf16[128,2304]{1,0:T(8,128)(2,1)S(1)} %pad_maximum_fusion.refs_0_), channel_id=1, source_target_pairs={{0,8},{8,0},{16,24},{24,16},{1,9},{9,1},{17,25},{25,17},{2,10},{10... | collective-permute-start | bytes 1769480 | tf_op jit(solution)/shard_map/ppermute | solution.py:46
  121.6 12.7 %collective-permute-start.38 = (bf16[128,128]{1,0:T(8,128)(2,1)}, bf16[128,128]{1,0:T(8,128)(2,1)S(1)}, u32[]{:S(2)}, u32[]{:S(2)}) collective-permute-start(bf16[128,128]{1,0:T(8,128)(2,1)} %shard_map.202.refs_0_), channel_id=1, source_target_pairs={{0,2},{2,0},{4,6},{6,4},{1,3},{3,1},{5,7},{7,5},{8,10},{10,8},{12,... | collective-permute-start | bytes 98312 | tf_op jit(solution)/shard_map/ppermute | solution.py:46
  134.4 33.8 %collective-permute-start.61 = (bf16[128,4608]{1,0:T(8,128)(2,1)S(1)}, bf16[128,4608]{1,0:T(8,128)(2,1)}, u32[]{:S(2)}, u32[]{:S(2)}) collective-permute-start(bf16[128,4608]{1,0:T(8,128)(2,1)S(1)} %constant_dynamic-update-slice_fusion.refs_0_), channel_id=1, source_target_pairs={{0,8},{8,0},{16,24},{24,16},{1,9},{9,1},{17,25},{25,17},{2,10},{10... | collective-permute-start | bytes 3538952 | tf_op jit(solution)/shard_map/ppermute | solution.py:46
  144.0 10.1 %collective-permute-start.19 = (bf16[64,2304]{1,0:T(8,128)(2,1)}, bf16[64,2304]{1,0:T(8,128)(2,1)}, u32[]{:S(2)}, u32[]{:S(2)}) collective-permute-start(bf16[64,2304]{1,0:T(8,128)(2,1)} %collective-permute-done.14.refs_3_), channel_id=1, source_target_pairs={{0,8},{8,0},{16,24},{24,16},{1,9},{9,1},{17,25},{25,17},{2,10},{10... | collective-permute-start | bytes 884744 | tf_op jit(solution)/shard_map/ppermute | solution.py:46
  145.8 8.9 %collective-permute-start.20 = (bf16[64,2304]{1,0:T(8,128)(2,1)}, bf16[64,2304]{1,0:T(8,128)(2,1)}, u32[]{:S(2)}, u32[]{:S(2)}) collective-permute-start(bf16[64,2304]{1,0:T(8,128)(2,1)} %collective-permute-done.15.refs_4_), channel_id=1, source_target_pairs={{0,8},{8,0},{16,24},{24,16},{1,9},{9,1},{17,25},{25,17},{2,10},{10... | collective-permute-start | bytes 884744 | tf_op jit(solution)/shard_map/ppermute | solution.py:46
  154.1 14.9 %collective-permute-start.62 = (bf16[64,4608]{1,0:T(8,128)(2,1)}, bf16[64,4608]{1,0:T(8,128)(2,1)}, u32[]{:S(2)}, u32[]{:S(2)}) collective-permute-start(bf16[64,4608]{1,0:T(8,128)(2,1)} %collective-permute-done.59.refs_1_), channel_id=1, source_target_pairs={{0,8},{8,0},{16,24},{24,16},{1,9},{9,1},{17,25},{25,17},{2,10},{10... | collective-permute-start | bytes 1769480 | tf_op jit(solution)/shard_map/ppermute | solution.py:46
  154.7 15.7 %collective-permute-start.63 = (bf16[64,4608]{1,0:T(8,128)(2,1)}, bf16[64,4608]{1,0:T(8,128)(2,1)}, u32[]{:S(2)}, u32[]{:S(2)}) collective-permute-start(bf16[64,4608]{1,0:T(8,128)(2,1)} %collective-permute-done.60.refs_2_), channel_id=1, source_target_pairs={{0,8},{8,0},{16,24},{24,16},{1,9},{9,1},{17,25},{25,17},{2,10},{10... | collective-permute-start | bytes 1769480 | tf_op jit(solution)/shard_map/ppermute | solution.py:46
  155.5 12.0 %collective-permute-start.43 = (bf16[128,512]{1,0:T(8,128)(2,1)}, bf16[128,512]{1,0:T(8,128)(2,1)}, u32[]{:S(2)}, u32[]{:S(2)}) collective-permute-start(bf16[128,512]{1,0:T(8,128)(2,1)} %shard_map.203.attention.refs_0_), channel_id=1, source_target_pairs={{0,17},{1,16},{8,25},{9,24},{16,1},{17,0},{24,9},{25,8},{2,19},{3,... | collective-permute-start | bytes 393224 | tf_op jit(solution)/shard_map/ppermute | solution.py:55
  157.6 10.4 %collective-permute-start.44 = (bf16[128,512]{1,0:T(8,128)(2,1)}, bf16[128,512]{1,0:T(8,128)(2,1)}, u32[]{:S(2)}, u32[]{:S(2)}) collective-permute-start(bf16[128,512]{1,0:T(8,128)(2,1)} %shard_map.203.attention.refs_0_), channel_id=1, source_target_pairs={{0,8},{8,0},{16,24},{24,16},{1,9},{9,1},{17,25},{25,17},{2,10},{10... | collective-permute-start | bytes 393224 | tf_op jit(solution)/shard_map/ppermute | solution.py:46
  167.5 14.4 %collective-permute-start.45 = (bf16[128,512]{1,0:T(8,128)(2,1)S(1)}, bf16[128,512]{1,0:T(8,128)(2,1)S(1)}, u32[]{:S(2)}, u32[]{:S(2)}) collective-permute-start(bf16[128,512]{1,0:T(8,128)(2,1)S(1)} %copy-done.22), channel_id=1, source_target_pairs={{0,8},{8,0},{16,24},{24,16},{1,9},{9,1},{17,25},{25,17},{2,10},{10... | collective-permute-start | bytes 393224 | tf_op jit(solution)/shard_map/ppermute | solution.py:46
  168.0 13.9 %collective-permute-start.46 = (bf16[128,512]{1,0:T(8,128)(2,1)}, bf16[128,512]{1,0:T(8,128)(2,1)S(1)}, u32[]{:S(2)}, u32[]{:S(2)}) collective-permute-start(bf16[128,512]{1,0:T(8,128)(2,1)} %collective-permute-done.42.refs_2_), channel_id=1, source_target_pairs={{0,8},{8,0},{16,24},{24,16},{1,9},{9,1},{17,25},{25,17},{2,10},{10... | collective-permute-start | bytes 393224 | tf_op jit(solution)/shard_map/ppermute | solution.py:46
  168.1 14.4 %collective-permute-start.48 = (f32[8,128]{1,0:T(8,128)}, f32[8,128]{1,0:T(8,128)S(1)}, u32[]{:S(2)}, u32[]{:S(2)}) collective-permute-start(f32[8,128]{1,0:T(8,128)} %shard_map.204.refs_8_), channel_id=1, source_target_pairs={{0,1},{1,0},{2,3},{3,2},{4,5},{5,4},{6,7},{7,6},{8,9},{9,8},{10,11... | collective-permute-start | bytes 12296 | tf_op jit(solution)/shard_map/ppermute | solution.py:46
  169.0 13.6 %collective-permute-start.49 = (f32[8,128]{1,0:T(8,128)}, f32[8,128]{1,0:T(8,128)S(1)}, u32[]{:S(2)}, u32[]{:S(2)}) collective-permute-start(f32[8,128]{1,0:T(8,128)} %shard_map.204.refs_8_), channel_id=1, source_target_pairs={{0,16},{8,24},{16,0},{24,8},{1,17},{9,25},{17,1},{25,9},{2,18},{10... | collective-permute-start | bytes 12296 | tf_op jit(solution)/shard_map/ppermute | solution.py:46
  170.3 12.7 %collective-permute-start.50 = (f32[8,128]{1,0:T(8,128)}, f32[8,128]{1,0:T(8,128)S(1)}, u32[]{:S(2)}, u32[]{:S(2)}) collective-permute-start(f32[8,128]{1,0:T(8,128)} %shard_map.204.refs_8_), channel_id=1, source_target_pairs={{0,17},{1,16},{8,25},{9,24},{16,1},{17,0},{24,9},{25,8},{2,19},{3,... | collective-permute-start | bytes 12296 | tf_op jit(solution)/shard_map/ppermute | solution.py:55
  181.9 11.1 %collective-permute-start.47 = (bf16[128,512]{1,0:T(8,128)(2,1)}, bf16[128,512]{1,0:T(8,128)(2,1)S(1)}, u32[]{:S(2)}, u32[]{:S(2)}) collective-permute-start(bf16[128,512]{1,0:T(8,128)(2,1)} %collective-permute-done.43.refs_3_), channel_id=1, source_target_pairs={{0,8},{8,0},{16,24},{24,16},{1,9},{9,1},{17,25},{25,17},{2,10},{10... | collective-permute-start | bytes 393224 | tf_op jit(solution)/shard_map/ppermute | solution.py:46
  182.0 11.1 %collective-permute-start.51 = (f32[8,128]{1,0:T(8,128)S(1)}, f32[8,128]{1,0:T(8,128)S(1)}, u32[]{:S(2)}, u32[]{:S(2)}) collective-permute-start(f32[8,128]{1,0:T(8,128)S(1)} %copy-done.38), channel_id=1, source_target_pairs={{0,8},{8,0},{16,24},{24,16},{1,9},{9,1},{17,25},{25,17},{2,10},{10... | collective-permute-start | bytes 12296 | tf_op jit(solution)/shard_map/ppermute | solution.py:46
  182.5 10.5 %collective-permute-start.52 = (f32[8,128]{1,0:T(8,128)S(1)}, f32[8,128]{1,0:T(8,128)S(1)}, u32[]{:S(2)}, u32[]{:S(2)}) collective-permute-start(f32[8,128]{1,0:T(8,128)S(1)} %collective-permute-done.48.refs_9_), channel_id=1, source_target_pairs={{0,8},{8,0},{16,24},{24,16},{1,9},{9,1},{17,25},{25,17},{2,10},{10... | collective-permute-start | bytes 12296 | tf_op jit(solution)/shard_map/ppermute | solution.py:46
  182.6 10.5 %collective-permute-start.53 = (f32[8,128]{1,0:T(8,128)S(1)}, f32[8,128]{1,0:T(8,128)S(1)}, u32[]{:S(2)}, u32[]{:S(2)}) collective-permute-start(f32[8,128]{1,0:T(8,128)S(1)} %collective-permute-done.49.refs_10_), channel_id=1, source_target_pairs={{0,8},{8,0},{16,24},{24,16},{1,9},{9,1},{17,25},{25,17},{2,10},{10... | collective-permute-start | bytes 12296 | tf_op jit(solution)/shard_map/ppermute | solution.py:46
  183.0 10.0 %collective-permute-start.54 = (f32[8,128]{1,0:T(8,128)S(1)}, f32[8,128]{1,0:T(8,128)S(1)}, u32[]{:S(2)}, u32[]{:S(2)}) collective-permute-start(f32[8,128]{1,0:T(8,128)S(1)} %collective-permute-done.50.refs_11_), channel_id=1, source_target_pairs={{0,8},{8,0},{16,24},{24,16},{1,9},{9,1},{17,25},{25,17},{2,10},{10... | collective-permute-start | bytes 12296 | tf_op jit(solution)/shard_map/ppermute | solution.py:46
  (74 other events, 561.3 us)
where the time goes:
time: 218 us; the launch traced here: 217 us
  waiting for transfers between devices  74.3 us (34%)
  Pallas kernels  67.7 us (31%)
  starting transfers between devices  55.6 us (26%)
  local copies, waits for them, and re-layouts  13.3 us (6%)
  other arithmetic  4.61 us (2%)
    ppermute x64, waiting for transfers between devices, swap(): return lax.ppermute(block, axis, [(i, i ^ mask) for i in range(count)])  62.6 us
    ppermute x64, starting transfers between devices, swap(): return lax.ppermute(block, axis, [(i, i ^ mask) for i in range(count)])  47.6 us
    pallas_call x12, Pallas kernels, kernel_call(): pl.pallas_call(body, out_shape=outputs, in_specs=in_specs, out_specs=[VME...  36 us
    pallas_call x3, Pallas kernels, contract(): pl.pallas_call(functools.partial(contract_body, len(left)), out_shape=sha...  30.3 us
    ppermute x7, waiting for transfers between devices, swap_two(): return lax.ppermute(block, ('task', 'dp'), route)  11.7 us
    ppermute x7, starting transfers between devices, swap_two(): return lax.ppermute(block, ('task', 'dp'), route)  7.98 us
  transfers between devices with their start and end apart: 71, of which 22 were waited for; matrix products, arithmetic and copies ran while one was open for 6% of the time, Pallas kernels for 26%

commit v1 on v0

--- a/solution.py
+++ b/solution.py
@@ -8,6 +8,8 @@
 from jax.sharding import PartitionSpec as P
 
 
+TASK, TENSOR, DP = "task", "tensor", "dp"
+
 BLK = 64
 LANES = 128
 
@@ -17,6 +19,9 @@
 SCORE_CAP = 50.0
 LOGIT_CAP = 30.0
 
+
+KERNEL_VMEM = 20 * 2**20
+CONTRACT_VMEM = 28 * 2**20
 
 VMEM = pl.BlockSpec(memory_space=pltpu.VMEM)
 SMEM = pl.BlockSpec(memory_space=pltpu.SMEM)
@@ -31,6 +36,7 @@
         in_specs=in_specs,
         out_specs=[VMEM] * len(outputs),
         scratch_shapes=list(scratch),
+        compiler_params=pltpu.CompilerParams(vmem_limit_bytes=KERNEL_VMEM),
         cost_estimate=pl.CostEstimate(
             flops=flops, bytes_accessed=moved, transcendentals=transcendentals
         ),
@@ -47,28 +53,28 @@
 
 
 def swap_two(block, task_mask, dp_mask):
-    tasks, halves = lax.axis_size("task"), lax.axis_size("dp")
+    tasks, halves = lax.axis_size(TASK), lax.axis_size(DP)
     route = []
     for t in range(tasks):
         for d in range(halves):
             route.append((t * halves + d, (t ^ task_mask) * halves + (d ^ dp_mask)))
-    return lax.ppermute(block, ("task", "dp"), route)
+    return lax.ppermute(block, (TASK, DP), route)
 
 
 def gather_group(block):
-    tasks, halves = lax.axis_size("task"), lax.axis_size("dp")
+    tasks, halves = lax.axis_size(TASK), lax.axis_size(DP)
     near = [(0, 0, block)]
     for tm in range(0, tasks, 2):
         for dm in range(halves):
             if tm or dm:
                 if not dm:
-                    got = swap(block, "task", tm)
+                    got = swap(block, TASK, tm)
                 elif not tm:
-                    got = swap(block, "dp", dm)
+                    got = swap(block, DP, dm)
                 else:
                     got = swap_two(block, tm, dm)
                 near.append((tm, dm, got))
-    return near + [(tm ^ 1, dm, swap(b, "task", 1)) for tm, dm, b in near]
+    return near + [(tm ^ 1, dm, swap(b, TASK, 1)) for tm, dm, b in near]
 
 
 def after(values, earlier):
@@ -91,7 +97,7 @@
 
 
 def total_over_group(value):
-    tasks, halves = lax.axis_size("task"), lax.axis_size("dp")
+    tasks, halves = lax.axis_size(TASK), lax.axis_size(DP)
     parts = []
     for tm in range(0, tasks, 2):
         for dm in range(halves):
@@ -99,7 +105,7 @@
                 parts.append(swap_two(value, tm, dm))
     for part in parts:
         value = value + part
-    return value + swap(value, "task", 1)
+    return value + swap(value, TASK, 1)
 
 
 def block_code(trim, sign):
@@ -303,28 +309,27 @@
     out[...] = table.T[: out.shape[0], :]
 
 
-def contract_body(count, table, *refs):
-    left, out, total = refs[:count], refs[count], refs[count + 1]
-    step = pl.program_id(0)
-    rows = [ref[...] for ref in left]
-    product = lax.dot_general(
-        jnp.concatenate(rows, axis=0) if count > 1 else rows[0],
-        table[...],
-        (((1,), (1,)), ((), ())),
-        preferred_element_type=jnp.float32,
-    )
-
-    @pl.when(step == 0)
-    def _():
-        total[...] = product
-
-    @pl.when(step > 0)
-    def _():
-        total[...] += product
-
-    @pl.when(step == pl.num_programs(0) - 1)
-    def _():
-        out[...] = total[...].astype(out.dtype)
+def contract_body(step, table, *refs):
+    left, out, total = refs[:-2], refs[-2], refs[-1]
+
+    def add(k, first):
+        cols = pl.ds(pl.multiple_of(k * step, LANES), step)
+        rows = [ref[:, cols] for ref in left]
+        product = lax.dot_general(
+            jnp.concatenate(rows, axis=0) if len(rows) > 1 else rows[0],
+            table[:, cols],
+            (((1,), (1,)), ((), ())),
+            preferred_element_type=jnp.float32,
+        )
+        total[...] = product if first else total[...] + product
+
+    add(0, True)
+
+    @pl.loop(1, table.shape[1] // step)
+    def _(k):
+        add(k, False)
+
+    out[...] = total[...].astype(out.dtype)
 
 
 def contract(left, table, dtype):
@@ -333,14 +338,12 @@
     rows = sum(block.shape[0] for block in left)
     vocab = table.shape[0]
     return pl.pallas_call(
-        functools.partial(contract_body, len(left)),
+        functools.partial(contract_body, step),
         out_shape=shape_of((rows, vocab), dtype),
-        grid=(width // step,),
-        in_specs=[pl.BlockSpec((vocab, step), lambda k: (0, k))]
-        + [pl.BlockSpec((block.shape[0], step), lambda k: (0, k)) for block in left],
-        out_specs=pl.BlockSpec((rows, vocab), lambda k: (0, 0)),
+        in_specs=[VMEM] * (1 + len(left)),
+        out_specs=VMEM,
         scratch_shapes=[pltpu.VMEM((rows, vocab), jnp.float32)],
-        name="contract",
+        compiler_params=pltpu.CompilerParams(vmem_limit_bytes=CONTRACT_VMEM),
         cost_estimate=pl.CostEstimate(
             flops=2 * rows * width * vocab,
             bytes_accessed=2 * (rows + vocab) * width + 4 * rows * vocab,
@@ -349,27 +352,60 @@
     )(table, *left)
 
 
-def score_body(masks, halves, place, targets, mixed, *refs):
+def score_body(masks, halves, shares, place, targets, mixed, *refs):
     count = len(masks)
     attention, stats = refs[:count], refs[count : 2 * count]
-    near, far, out = refs[2 * count :]
+    first, early, late, out = refs[2 * count :]
     rows = attention[0].shape[0]
+    cut = rows // 2
+    share = rows // shares
     vocab = mixed.shape[1]
     first_id = place[3]
+    z = place[2]
+    side = z // (shares // 2)
     lane = lax.broadcasted_iota(jnp.int32, (rows, LANES), 1)
+    late_rows = cut + rows + cut
+
+    def halves_of(mine, rest):
+        top = jnp.where(side == 0, mine, rest)
+        bottom = jnp.where(side == 0, rest, mine)
+        return jnp.concatenate([top, bottom], axis=0)
+
+    def by_share(start, natural, cols):
+        found = []
+        for s in natural:
+            at = pl.multiple_of(start + (z ^ s) * share, share)
+            found.append(late[pl.ds(at, share), cols])
+        return jnp.concatenate(found, axis=0)
+
     for n, (tm, dm) in enumerate(masks):
         group = (place[0] ^ tm) * halves + (place[1] ^ dm)
         table = stats[n][...].T
         wanted = jnp.broadcast_to(targets[pl.ds(group, 1), :], (8, rows)).T
         inner, outer, wanted = table[:, 0:1], table[:, 1:2], wanted[:, 0:1]
-        base = far if tm > 1 else near
-        start = (halves * (tm % 2) + dm) * rows
+        core = tm % 2
+        own = core * rows
+        far = core * late_rows
         sums = jnp.zeros((rows, LANES), jnp.float32)
         hits = jnp.zeros((rows, LANES), jnp.float32)
         product = jnp.dot(attention[n][...], mixed[...], preferred_element_type=jnp.float32)
         for v in range(vocab // LANES):
             cols = slice(v * LANES, (v + 1) * LANES)
-            logits = outer * (base[start : start + rows, cols] + inner * product[:, cols])
+            if tm < 2 and not dm:
+                plain = first[own : own + rows, cols]
+            elif tm < 2:
+                plain = halves_of(early[own : own + cut, cols], early[own + cut : own + rows, cols])
+            elif not dm:
+                plain = by_share(far + cut, range(shares), cols)
+            else:
+                count_rest = shares // 2
+                rest = by_share(
+                    far + rows,
+                    [(1 - side) * count_rest + i for i in range(count_rest)],
+                    cols,
+                )
+                plain = halves_of(late[far : far + cut, cols], rest)
+            logits = outer * (plain + inner * product[:, cols])
             capped = LOGIT_CAP * jnp.tanh(logits / LOGIT_CAP)
             sums = sums + jnp.exp(capped)
             hits = hits + jnp.where(lane + (first_id + v * LANES) == wanted, capped, 0.0)
@@ -398,10 +434,10 @@
     place, masks, attention, piece_out, hidden, post_gain, final_gain, unembedding, targets, loss_mask
 ):
     bf16, f32 = jnp.bfloat16, jnp.float32
-    tasks = lax.axis_size("task")
-    tensors = lax.axis_size("tensor")
-    halves = lax.axis_size("dp")
-    task, dp, tensor = lax.axis_index("task"), lax.axis_index("dp"), lax.axis_index("tensor")
+    tasks = lax.axis_size(TASK)
+    tensors = lax.axis_size(TENSOR)
+    halves = lax.axis_size(DP)
+    task, dp, tensor = lax.axis_index(TASK), lax.axis_index(DP), lax.axis_index(TENSOR)
     row_count, width = hidden.shape
     out_rows, half = piece_out.shape
     residual = hidden.astype(f32)
@@ -417,11 +453,11 @@
     )[0]
 
     span_rows = row_count // tensors
-    share_rows = lax.psum_scatter(partial_value, "tensor", scatter_dimension=0, tiled=True).astype(f32)
+    share_rows = lax.psum_scatter(partial_value, TENSOR, scatter_dimension=0, tiled=True).astype(f32)
     own_stream = lax.dynamic_slice_in_dim(residual, tensor * span_rows, span_rows, 0)
     stream = own_stream + rms_norm(share_rows, post_gain)
     final = rms_norm(stream, final_gain).astype(bf16)
-    every_rows = lax.all_gather(final, ("task", "tensor", "dp"), axis=0, tiled=True)
+    every_rows = lax.all_gather(final, (TASK, TENSOR, DP), axis=0, tiled=True)
 
     def order(values):
         return jnp.transpose(
@@ -433,7 +469,7 @@
         every_rows, unembedding, (((1,), (1,)), ((), ())), preferred_element_type=f32
     )
     capped = LOGIT_CAP * jnp.tanh(logits / LOGIT_CAP)
-    vocab_ids = lax.axis_index(("task", "tensor", "dp")) * unembedding.shape[0] + jnp.arange(
+    vocab_ids = lax.axis_index((TASK, TENSOR, DP)) * unembedding.shape[0] + jnp.arange(
         unembedding.shape[0], dtype=jnp.int32
     )
     local_sumexp = jnp.sum(jnp.exp(capped), axis=1)
@@ -441,7 +477,7 @@
         jnp.where(ordered_targets[:, None] == vocab_ids[None, :], capped, 0.0), axis=1
     )
     both = jnp.stack([local_sumexp, local_target])
-    both = total_over_group(total_over(both, "tensor"))
+    both = total_over_group(total_over(both, TENSOR))
     sumexp, target_logit = both[0], both[1]
     counted = ordered_mask.astype(f32)
     losses = (jnp.log(sumexp) - target_logit) * counted
@@ -453,27 +489,26 @@
     return (own_losses, summary)
 
 
-def exchange_hidden(hidden, kept, tensor):
-    tensors = lax.axis_size("tensor")
+def paired(blocks):
+    return blocks + [swap(block, TASK, 1) for block in blocks]
+
+
+def send_hidden(hidden, kept, tensor):
+    tensors = lax.axis_size(TENSOR)
     rows = hidden.shape[0] // tensors
     cut = hidden.shape[0] // 2
     hidden = after([hidden], [kept])[0]
+    side = tensor // (tensors // 2)
     share = lax.dynamic_slice_in_dim(hidden, tensor * rows, rows, 0)
-    top, bottom = hidden[:cut], hidden[cut:]
-    dp_top = swap(top, "dp", 1)
-    by_task = swap(share, "task", 2)
-    dp_bottom = swap(bottom, "dp", 1)
-    task_all = jnp.zeros_like(hidden)
-    for m in range(tensors):
-        block = swap(by_task, "tensor", m) if m else by_task
-        task_all = lax.dynamic_update_slice_in_dim(task_all, block, (tensor ^ m) * rows, 0)
-    both_top = swap(dp_top, "task", 2)
-    both_bottom = swap(task_all[cut:], "dp", 1)
-
-    def paired(blocks):
-        return blocks + [swap(block, "task", 1) for block in blocks]
-
-    return paired([hidden, dp_top, dp_bottom]), paired([task_all, both_top, both_bottom])
+    mine = lax.dynamic_slice_in_dim(hidden, side * cut, cut, 0)
+    rest = lax.dynamic_slice_in_dim(hidden, (1 - side) * cut, cut, 0)
+    dp_mine = swap(mine, DP, 1)
+    by_task = swap(share, TASK, 2)
+    dp_rest = swap(rest, DP, 1)
+    both_mine = swap(dp_mine, TASK, 2)
+    shares = [by_task] + [swap(by_task, TENSOR, m) for m in range(1, tensors)]
+    both_rest = [swap(shares[m], DP, 1) for m in range(tensors // 2, tensors)]
+    return [hidden, dp_mine, dp_rest], [both_mine], shares + both_rest
 
 
 def split_tail(
@@ -481,17 +516,17 @@
     attention,
     piece_out,
     inverse_gains,
-    far_rows,
-    near,
+    late_rows,
+    base,
     hidden,
     unembedding,
     targets,
     loss_mask,
 ):
     bf16, f32 = jnp.bfloat16, jnp.float32
-    tasks = lax.axis_size("task")
-    tensors = lax.axis_size("tensor")
-    halves = lax.axis_size("dp")
+    tasks = lax.axis_size(TASK)
+    tensors = lax.axis_size(TENSOR)
+    halves = lax.axis_size(DP)
     row_count, width = hidden.shape
     out_rows, _ = piece_out.shape
     groups = tasks * halves
@@ -499,33 +534,37 @@
     place = where
     to_plain, to_post = inverse_gains
 
-    column = jnp.concatenate([piece_out] + [swap(piece_out, "tensor", m) for m in range(1, tensors)], axis=0)
-    by_task, by_dp = swap(column, "task", 2), swap(column, "dp", 1)
+    features = tensors * tasks * out_rows
+    received = after([swap(attention, TENSOR, m) for m in range(1, tensors)], base[1:])
+    heads = kernel_call(
+        functools.partial(heads_body, list(range(tensors))),
+        [place, attention] + received,
+        [SMEM] + [VMEM] * tensors,
+        [shape_of((row_count, features), bf16)],
+    )[0]
+    late = contract(paired(after(late_rows, [attention])), unembedding, f32)
+    column = jnp.concatenate([piece_out] + [swap(piece_out, TENSOR, m) for m in range(1, tensors)], axis=0)
+    by_task, by_dp = swap(column, TASK, 2), swap(column, DP, 1)
     cut = column.shape[0] // 2
     parts = [
         (0, 0, 0, column),
         (2, 0, 0, by_task),
         (0, 1, 0, by_dp),
-        (2, 1, 0, swap(by_dp[:cut], "task", 2)),
-        (2, 1, cut // out_rows, swap(by_task[cut:], "dp", 1)),
+        (2, 1, 0, swap(by_dp[:cut], TASK, 2)),
+        (2, 1, cut // out_rows, swap(by_task[cut:], DP, 1)),
     ]
-    parts += [(tm ^ 1, dm, first, swap(b, "task", 1)) for tm, dm, first, b in parts]
+    parts += [(tm ^ 1, dm, first, swap(b, TASK, 1)) for tm, dm, first, b in parts]
+    tied = after([part[3] for part in parts[3:5]], [late])
+    parts[3:5] = [part[:3] + (block,) for part, block in zip(parts[3:5], tied)]
     plain = kernel_call(
         functools.partial(assemble_body, [part[:3] for part in parts]),
         [place] + [part[3] for part in parts],
         [SMEM] + [VMEM] * len(parts),
         [shape_of((tensors, tasks, out_rows, width), bf16)],
     )[0]
-    features = tensors * tasks * out_rows
     plain = plain.reshape(features, width)
     mixed = contract([plain], unembedding, bf16)
 
-    heads = kernel_call(
-        functools.partial(heads_body, list(range(tensors))),
-        [place, attention] + [swap(attention, "tensor", m) for m in range(1, tensors)],
-        [SMEM] + [VMEM] * tensors,
-        [shape_of((row_count, features), bf16)],
-    )[0]
     stats = kernel_call(
         statistics_body,
         [heads, plain, hidden, to_plain, to_post],
@@ -534,20 +573,19 @@
         flops=2 * row_count * features * width,
     )[0]
     every_heads = gather_group(heads)
-    far = contract(far_rows, unembedding, f32)
     every_stats = gather_group(stats)
     both = kernel_call(
-        functools.partial(score_body, [(tm, dm) for tm, dm, _ in every_heads], halves),
+        functools.partial(score_body, [(tm, dm) for tm, dm, _ in every_heads], halves, tensors),
         [where, targets.reshape(groups, row_count), mixed]
         + [b for _, _, b in every_heads]
         + [b for _, _, b in every_stats]
-        + [near, far],
-        [SMEM] + [VMEM] * (4 + 2 * groups),
+        + base + [late],
+        [SMEM] + [VMEM] * (5 + 2 * groups),
         [shape_of((2, groups, row_count), f32)],
         flops=2 * groups * row_count * features * vocab,
         transcendentals=2 * groups * row_count * vocab,
     )[0]
-    both = total_over(both, "tensor")
+    both = total_over(both, TENSOR)
     parts = [swap_two(both, tm, dm) for tm in range(0, tasks, 2) for dm in range(halves) if tm or dm]
     for part in parts:
         both = both + part
@@ -557,7 +595,7 @@
         in_specs=[SMEM] + [VMEM] * 3,
         out_specs=[VMEM, SMEM],
         name="loss",
-    )(place, loss_mask.reshape(groups, row_count), both, swap(both, "task", 1))
+    )(place, loss_mask.reshape(groups, row_count), both, swap(both, TASK, 1))
     return own.reshape(row_count), summary
 
 
@@ -583,10 +621,10 @@
     loss_mask,
 ):
     bf16, f32 = jnp.bfloat16, jnp.float32
-    tasks = lax.axis_size("task")
-    tensors = lax.axis_size("tensor")
-    halves = lax.axis_size("dp")
-    task, dp, tensor = lax.axis_index("task"), lax.axis_index("dp"), lax.axis_index("tensor")
+    tasks = lax.axis_size(TASK)
+    tensors = lax.axis_size(TENSOR)
+    halves = lax.axis_size(DP)
+    task, dp, tensor = lax.axis_index(TASK), lax.axis_index(DP), lax.axis_index(TENSOR)
     place = jnp.stack([task, dp, tensor]).astype(jnp.int32)
     row_count, width = hidden.shape
     half = base_query.shape[0]
@@ -608,7 +646,7 @@
         [shape_of((quarter, 2 * LANES), bf16)] * tasks,
         [pltpu.VMEM((half, LANES), f32)],
     )
-    got_in = [kept_in[0]] + [swap(kept_in[j], "task", j) for j in range(1, tasks)]
+    got_in = [kept_in[0]] + [swap(kept_in[j], TASK, j) for j in range(1, tasks)]
     kept_out = kernel_call(
         functools.partial(trim_output_body, tasks),
         [place, trim_output, sign_output, delta_output],
@@ -623,11 +661,11 @@
         [pltpu.VMEM((half, LANES), f32)],
     )[0]
 
-    residual = hidden.astype(f32)
-    normed = rms_norm(residual, pre_gain).astype(bf16)
+    early_hidden, early_place = after([hidden, place], [kept_in[0]])
+    normed = rms_norm(early_hidden.astype(f32), pre_gain).astype(bf16)
     blocks = width // quarter
     normed = jnp.transpose(normed.reshape(row_count, blocks, quarter), (1, 0, 2))
-    group_index = task * halves + dp
+    group_index = early_place[0] * halves + early_place[1]
     query_positions = group_index * row_count + jnp.arange(row_count, dtype=jnp.int32)
     half_head = LANES // 2
     frequencies = jnp.exp(
@@ -639,16 +677,16 @@
     sine = jnp.concatenate([-sine, sine], axis=1)
 
     gathered_bytes = tensors * base_output.shape[0] * width * base_output.dtype.itemsize
-    low_rank = gathered_bytes <= 6 * 2**20
+    low_rank = gathered_bytes <= 6 * 2**20 and tensors in (2, 4)
     where = jnp.concatenate(
-        [place, (lax.axis_index(("task", "tensor", "dp")) * unembedding.shape[0]).astype(jnp.int32)[None]]
+        [place, (lax.axis_index((TASK, TENSOR, DP)) * unembedding.shape[0]).astype(jnp.int32)[None]]
     )
     if low_rank:
         weight_gain = (post_gain * final_gain)[None, :]
         rows = [weight_gain, 1.0 / weight_gain, (1.0 / final_gain)[None, :], where]
     else:
         rows = [jnp.ones((1, width), f32), where]
-    tied = after(list(got_in) + rows, [])
+    tied = after(list(got_in) + rows, [normed, cosine, sine])
     got_in, rows = tied[:tasks], tied[tasks:]
     weight_gain, where = rows[0], rows[-1]
     piece_in = kernel_call(
@@ -661,13 +699,13 @@
     masks = [(tm, dm) for tm, dm, _ in pieces_in]
 
     kept_out = after(kept_out, [piece_in])
-    got_out = [kept_out[0]] + [swap(kept_out[j], "task", j) for j in range(1, tasks)]
+    got_out = [kept_out[0]] + [swap(kept_out[j], TASK, j) for j in range(1, tasks)]
     got_out = after(got_out, [b for _, _, b in pieces_in[1:4]])
     if low_rank:
         scaled = (hidden.astype(f32) * final_gain).astype(bf16)
-        near_rows, far_rows = exchange_hidden(scaled, kept_in[0], tensor)
-        near_rows = after(near_rows, [piece_in])
-        near = contract(near_rows, unembedding, f32)
+        early_rows, middle_rows, late_rows = send_hidden(scaled, kept_in[0], tensor)
+        base = [contract(paired(early_rows[:1]), unembedding, f32)]
+        base.append(contract(paired(early_rows[1:]), unembedding, f32))
     piece_out = kernel_call(
         merge_output_body,
         [place, weight_gain, base_output] + got_out,
@@ -682,7 +720,7 @@
         [shape_of((row_count, LANES), bf16)] * 2,
         flops=2 * row_count * width * 2 * LANES,
     )
-    other = swap(keyval, "tensor", 1)
+    other = swap(keyval, TENSOR, 1)
     joined = kernel_call(
         join_body,
         [place, cosine, sine, keyval, other],
@@ -690,8 +728,6 @@
         [shape_of((row_count, 2 * LANES), bf16)],
     )[0]
     every_keyval = gather_group(joined)
-    if low_rank:
-        queries = after([queries], [near])[0]
     attention = kernel_call(
         functools.partial(attend_body, masks, halves),
         [place, queries] + [b for _, _, b in every_keyval],
@@ -709,8 +745,8 @@
         attention,
         piece_out,
         rows[1:3],
-        far_rows,
-        near,
+        middle_rows + late_rows,
+        base,
         hidden,
         unembedding,
         targets,
@@ -723,26 +759,26 @@
         on_device,
         mesh=mesh,
         in_specs=(
-            P(("task", "dp"), None),
+            P((TASK, DP), None),
             P(),
-            P("dp", "tensor"),
-            P(None, "dp", "tensor"),
-            P("tensor", "dp"),
-            P("task", "dp", "tensor"),
-            P("task", None, "dp", "tensor"),
-            P("task", "tensor", "dp"),
-            P("task", "dp", "tensor"),
-            P("task", None, "dp", "tensor"),
-            P("task", "tensor", "dp"),
-            P("dp", "tensor"),
-            P(None, "dp", "tensor"),
-            P("tensor", "dp"),
+            P(DP, TENSOR),
+            P(None, DP, TENSOR),
+            P(TENSOR, DP),
+            P(TASK, DP, TENSOR),
+            P(TASK, None, DP, TENSOR),
+            P(TASK, TENSOR, DP),
+            P(TASK, DP, TENSOR),
+            P(TASK, None, DP, TENSOR),
+            P(TASK, TENSOR, DP),
+            P(DP, TENSOR),
+            P(None, DP, TENSOR),
+            P(TENSOR, DP),
             P(),
             P(),
-            P(("task", "tensor", "dp"), None),
+            P((TASK, TENSOR, DP), None),
             P(),
             P(),
         ),
-        out_specs=(P(("task", "dp")), P()),
+        out_specs=(P((TASK, DP)), P()),
         check_vma=False,
     )

time: 218 us -> 202 us (0.927)
  Pallas kernels: 67.7 us -> 38.2 us
  local copies, waits for them, and re-layouts: 13.3 us -> 18.9 us
  waiting for transfers between devices: 74.3 us -> 78.8 us
  other arithmetic: 4.61 us -> 6.95 us
    pallas_call x12, Pallas kernels: 36 us -> 16.2 us  [kernel_call(): pl.pallas_call(body, out_shape=outputs, in_specs=in_specs, out_specs=[VME...]
    ppermute x64 -> x69, waiting for transfers between devices: 62.6 us -> 75 us  [swap(): return lax.ppermute(block, axis, [(i, i ^ mask) for i in range(count)])]
    pallas_call x3 -> x4, Pallas kernels: 30.3 us -> 20.6 us  [contract(): pl.pallas_call(functools.partial(contract_body, step), out_shape=shape_of...]
    unnamed x102 -> x70, local copies, waits for them, and re-layouts: 3.52 us -> 11.7 us
    ppermute x7, waiting for transfers between devices: 11.7 us -> 3.78 us  [swap_two(): return lax.ppermute(block, (TASK, DP), route)]
    dynamic_update_slice x4 -> x0, local copies, waits for them, and re-layouts: 2.98 us -> none  [exchange_hidden(): lax.dynamic_update_slice_in_dim(task_all, block, (tensor ^ m) * rows, 0)]
    convert_element_type x0 -> x1, other arithmetic: none -> 2.8 us  [on_device(): normed = rms_norm(early_hidden.astype(f32), pre_gain).astype(bf16)]
    ppermute x64 -> x69, starting transfers between devices: 47.6 us -> 48.8 us  [swap(): return lax.ppermute(block, axis, [(i, i ^ mask) for i in range(count)])]
  transfers between devices with their start and end apart: 71 -> 76, of which waited for: 22 -> 24; matrix products, arithmetic and copies ran while one was open for 6% -> 7% of each run, Pallas kernels for 26% -> 16%
where the time goes in v1:
time: 202 us
  waiting for transfers between devices  78.8 us (39%)
  starting transfers between devices  56.1 us (28%)
  Pallas kernels  38.2 us (19%)
  local copies, waits for them, and re-layouts  18.9 us (9%)
  other arithmetic  6.95 us (3%)
  between operations  2.56 us (1%)
    ppermute x69, waiting for transfers between devices, swap(): return lax.ppermute(block, axis, [(i, i ^ mask) for i in range(count)])  75 us
    ppermute x69, starting transfers between devices, swap(): return lax.ppermute(block, axis, [(i, i ^ mask) for i in range(count)])  48.8 us
    pallas_call x4, Pallas kernels, contract(): pl.pallas_call(functools.partial(contract_body, step), out_shape=shape_of...  20.6 us
    pallas_call x12, Pallas kernels, kernel_call(): pl.pallas_call(body, out_shape=outputs, in_specs=in_specs, out_specs=[VME...  16.2 us
    unnamed x70, local copies, waits for them, and re-layouts  11.7 us
    ppermute x7, starting transfers between devices, swap_two(): return lax.ppermute(block, (TASK, DP), route)  7.34 us
  transfers between devices with their start and end apart: 76, of which 24 were waited for; matrix products, arithmetic and copies ran while one was open for 7% of the time, Pallas kernels for 16%

profile of v1, /device:TPU:0, one launch (start us, length us, event | category | flops | bytes accessed | tf_op | source)
XLA Modules:
  0.0 201.6 jit_solution(2321545486775896970)
XLA Ops:
  5.7 1.9 shard_map.194
  8.1 2.5 %collective-permute-start.1 = (bf16[576,256]{1,0:T(8,128)(2,1)}, bf16[576,256]{1,0:T(8,128)(2,1)}, u32[]{:S(2)}, u32[]{:S(2)}) collective-permute-start(bf16[576,256]{1,0:T(8,128)(2,1)} %get-tuple-element.47), channel_id=1, source_target_pairs={{0,16},{8,24},{16,0},{24,8},{1,17},{9,25},{17,1},{25,9},{2,18},{10... | collective-permute-start | bytes 884744 | tf_op jit(solution)/shard_map/ppermute | solution.py:52
  11.6 1.7 collective-permute-start.18
  16.7 2.0 fusion
  19.7 2.8 %fusion.2 = bf16[128,4608]{0,1:T(8,128)(2,1)} fusion(bf16[128,4608]{0,1:T(8,128)(2,1)S(1)} %copy-done.21, f32[4608]{0:T(1024)S(1)} %copy-done.31, f32[128]{0:T(128)S(1)} %add_rsqrt_fusion), kind=kLoop, calls=%fused_computation.4 | loop fusion | flops 2359296 | bytes 2378240 | tf_op jit(solution)/shard_map/convert_element_type | solution.py:665
  26.2 1.6 shard_map.195
  28.5 2.5 %copy.26 = bf16[128,8,576]{2,0,1:T(8,128)(2,1)} copy(bf16[128,8,576]{0,2,1:T(8,128)(2,1)} %bitcast.33) | data formatting | bytes 2359296 | tf_op jit(solution)/shard_map/reshape | solution.py:667
  32.9 1.6 shard_map.197.refs_0_
  35.0 1.8 collective-permute-start.6
  36.7 1.5 collective-permute-start.7
  38.5 3.1 %collective-permute-done.4.refs_2_ = bf16[32,2304]{1,0:T(8,128)(2,1)S(1)} collective-permute-done((bf16[32,2304]{1,0:T(8,128)(2,1)}, bf16[32,2304]{1,0:T(8,128)(2,1)S(1)}, u32[]{:S(2)}, u32[]{:S(2)}) %collective-permute-start.4) | collective-permute-done | bytes 147488 | tf_op jit(solution)/shard_map/ppermute | solution.py:52
  41.7 14.6 %collective-permute-done.5.refs_3_ = bf16[32,2304]{1,0:T(8,128)(2,1)S(1)} collective-permute-done((bf16[32,2304]{1,0:T(8,128)(2,1)}, bf16[32,2304]{1,0:T(8,128)(2,1)S(1)}, u32[]{:S(2)}, u32[]{:S(2)}) %collective-permute-start.5) | collective-permute-done | bytes 147488 | tf_op jit(solution)/shard_map/ppermute | solution.py:52
  56.3 1.5 collective-permute-start.16
  60.0 2.6 %collective-permute-start.20 = (bf16[32,4608]{1,0:T(8,128)(2,1)}, bf16[32,4608]{1,0:T(8,128)(2,1)S(1)}, u32[]{:S(2)}, u32[]{:S(2)}) collective-permute-start(bf16[32,4608]{1,0:T(8,128)(2,1)} %collective-permute-done.18.refs_1_), channel_id=1, source_target_pairs={{0,4},{2,6},{4,0},{6,2},{1,5},{3,7},{5,1},{7,3},{8,12},{10,14},{12... | collective-permute-start | bytes 884744 | tf_op jit(solution)/shard_map/ppermute | solution.py:52
  62.5 1.4 collective-permute-start.21
  65.4 7.2 %collective-permute-done.16.refs_0_ = bf16[64,4608]{1,0:T(8,128)(2,1)S(1)} collective-permute-done((bf16[64,4608]{1,0:T(8,128)(2,1)S(1)}, bf16[64,4608]{1,0:T(8,128)(2,1)S(1)}, u32[]{:S(2)}, u32[]{:S(2)}) %collective-permute-start.16) | collective-permute-done | bytes 589856 | tf_op jit(solution)/shard_map/ppermute | solution.py:52
  72.5 1.6 collective-permute-start.28
  74.9 10.3 %collective-permute-done.28.other = bf16[128,128]{1,0:T(8,128)(2,1)S(1)} collective-permute-done((bf16[128,128]{1,0:T(8,128)(2,1)S(1)}, bf16[128,128]{1,0:T(8,128)(2,1)S(1)}, u32[]{:S(2)}, u32[]{:S(2)}) %collective-permute-start.28) | collective-permute-done | bytes 32800 | tf_op jit(solution)/shard_map/ppermute | solution.py:52
  87.1 1.6 collective-permute-start.29
  89.2 1.4 collective-permute-start.31
  90.7 4.8 %collective-permute-done.10 = bf16[32,2304]{1,0:T(8,128)(2,1)S(1)} collective-permute-done((bf16[32,2304]{1,0:T(8,128)(2,1)S(1)}, bf16[32,2304]{1,0:T(8,128)(2,1)S(1)}, u32[]{:S(2)}, u32[]{:S(2)}) %collective-permute-start.10) | collective-permute-done | bytes 147488 | tf_op jit(solution)/shard_map/ppermute | solution.py:52
  95.4 1.5 collective-permute-start.22
  98.2 3.5 %collective-permute-start.11 = (bf16[32,2304]{1,0:T(8,128)(2,1)S(1)}, bf16[32,2304]{1,0:T(8,128)(2,1)S(1)}, u32[]{:S(2)}, u32[]{:S(2)}) collective-permute-start(bf16[32,2304]{1,0:T(8,128)(2,1)S(1)} %shard_map.198), channel_id=1, source_target_pairs={{0,6},{2,4},{4,2},{6,0},{1,7},{3,5},{5,3},{7,1},{8,14},{10,12},{12... | collective-permute-start | bytes 442376 | tf_op jit(solution)/shard_map/ppermute | solution.py:52
  103.0 3.8 %collective-permute-done.11 = bf16[32,2304]{1,0:T(8,128)(2,1)S(1)} collective-permute-done((bf16[32,2304]{1,0:T(8,128)(2,1)S(1)}, bf16[32,2304]{1,0:T(8,128)(2,1)S(1)}, u32[]{:S(2)}, u32[]{:S(2)}) %collective-permute-start.11) | collective-permute-done | bytes 147488 | tf_op jit(solution)/shard_map/ppermute | solution.py:52
  106.8 1.7 collective-permute-start.48
  109.3 1.6 collective-permute-start.49
  111.9 2.2 %collective-permute-done.49.refs_2_ = bf16[128,128]{1,0:T(8,128)(2,1)S(1)} collective-permute-done((bf16[128,128]{1,0:T(8,128)(2,1)S(1)}, bf16[128,128]{1,0:T(8,128)(2,1)S(1)}, u32[]{:S(2)}, u32[]{:S(2)}) %collective-permute-start.49) | collective-permute-done | bytes 32800 | tf_op jit(solution)/shard_map/ppermute | solution.py:52
  114.1 1.9 collective-permute-start.50
  116.0 3.8 %collective-permute-done.50.refs_3_ = bf16[128,128]{1,0:T(8,128)(2,1)S(1)} collective-permute-done((bf16[128,128]{1,0:T(8,128)(2,1)S(1)}, bf16[128,128]{1,0:T(8,128)(2,1)S(1)}, u32[]{:S(2)}, u32[]{:S(2)}) %collective-permute-start.50) | collective-permute-done | bytes 32800 | tf_op jit(solution)/shard_map/ppermute | solution.py:52
  121.1 3.3 %copy-done = bf16[896,4608]{1,0:T(8,128)(2,1)S(1)} copy-done((bf16[896,4608]{1,0:T(8,128)(2,1)S(1)}, bf16[896,4608]{1,0:T(8,128)(2,1)}, u32[]{:S(2)}) %copy-start) | copy-done | bytes 8257560
  124.4 3.6 %shard_map.205.refs_17_ = f32[256,896]{1,0:T(8,128)S(1)} custom-call(bf16[896,4608]{1,0:T(8,128)(2,1)S(1)} %copy-done, bf16[64,4608]{1,0:T(8,128)(2,1)S(1)} %collective-permute-done.16.refs_0_, bf16[64,4608]{1,0:T(8,128)(2,1)S(1)} %collective-permute-done.51.refs_1_, bf16[64,4608]{1,0:T(8,128)(2,1)S(1)} %collective-permute-done.52.refs_2_, ...), custom_call_target="tpu_custom_call" | custom-call | flops 2113929216 | bytes 11534336 | tf_op jit(solution)/shard_map/pallas_call | solution.py:340
  130.0 1.5 collective-permute-start.55
  131.4 4.0 %collective-permute-done.54.refs_1_ = bf16[128,512]{1,0:T(8,128)(2,1)S(1)} collective-permute-done((bf16[128,512]{1,0:T(8,128)(2,1)S(1)}, bf16[128,512]{1,0:T(8,128)(2,1)S(1)}, u32[]{:S(2)}, u32[]{:S(2)}) %collective-permute-start.54) | collective-permute-done | bytes 131104 | tf_op jit(solution)/shard_map/ppermute | solution.py:52
  135.5 4.4 %collective-permute-done.55.refs_2_ = bf16[128,512]{1,0:T(8,128)(2,1)S(1)} collective-permute-done((bf16[128,512]{1,0:T(8,128)(2,1)S(1)}, bf16[128,512]{1,0:T(8,128)(2,1)S(1)}, u32[]{:S(2)}, u32[]{:S(2)}) %collective-permute-start.55) | collective-permute-done | bytes 131104 | tf_op jit(solution)/shard_map/ppermute | solution.py:52
  143.4 7.7 %collective-permute-done.14.refs_3_ = bf16[64,2304]{1,0:T(8,128)(2,1)S(1)} collective-permute-done((bf16[64,2304]{1,0:T(8,128)(2,1)S(1)}, bf16[64,2304]{1,0:T(8,128)(2,1)S(1)}, u32[]{:S(2)}, u32[]{:S(2)}) %collective-permute-start.14) | collective-permute-done | bytes 294944 | tf_op jit(solution)/shard_map/ppermute | solution.py:52
  153.9 7.3 %shard_map.202.refs_18_ = f32[512,896]{1,0:T(8,128)S(1)} custom-call(bf16[896,4608]{1,0:T(8,128)(2,1)S(1)} %copy-done, bf16[64,4608]{1,0:T(8,128)(2,1)S(1)} %collective-permute-done.17.refs_0_, bf16[32,4608]{1,0:T(8,128)(2,1)} %collective-permute-done.18.refs_1_, bf16[32,4608]{1,0:T(8,128)(2,1)S(1)} %collective-permute-done.19.refs_2_, ...), custom_call_target="tpu_custom_call" | custom-call | flops 4227858432 | bytes 14811136 | tf_op jit(solution)/shard_map/pallas_call | solution.py:340
  162.7 1.7 shard_map.207.refs_8_
  167.9 3.6 %shard_map.208.refs_16_ = f32[256,896]{1,0:T(8,128)S(1)} custom-call(bf16[896,4608]{1,0:T(8,128)(2,1)S(1)} %bitcast.22, bf16[128,4608]{1,0:T(8,128)(2,1)S(1)} %multiply_convert_fusion.refs_0_, bf16[128,4608]{1,0:T(8,128)(2,1)S(1)} %collective-permute-done.68.refs_1_), custom_call_target="tpu_custom_call" | custom-call | flops 2113929216 | bytes 11534336 | tf_op jit(solution)/shard_map/pallas_call | solution.py:340
  172.6 6.1 %shard_map.204.mixed = bf16[512,896]{1,0:T(8,128)(2,1)S(1)} custom-call(bf16[896,4608]{1,0:T(8,128)(2,1)S(1)} %bitcast.22, bf16[512,4608]{1,0:T(8,128)(2,1)S(1)} %bitcast.24), custom_call_target="tpu_custom_call" | custom-call | flops 4227858432 | bytes 14811136 | tf_op jit(solution)/shard_map/pallas_call | solution.py:340
  178.8 3.4 %shard_map.209 = f32[2,8,128]{2,1,0:T(8,128)S(1)} custom-call(s32[4]{0:T(128)S(1)} %pad_add_fusion.1.place, s32[8,128]{1,0:T(8,128)S(1)} %bitcast.28, bf16[512,896]{1,0:T(8,128)(2,1)S(1)} %shard_map.204.mixed, bf16[128,512]{1,0:T(8,128)(2,1)S(1)} %shard_map.206.attention.refs_0_, bf16[128,512]{1,0:T(8,128)(2,1)S(1)} %collective-permute-done.54.refs_1_, ...), custom_call_target="tpu_custom_call" | custom-call | flops 939524096 | bytes 5681168 | tf_op jit(solution)/shard_map/pallas_call | solution.py:33
  182.2 1.8 collective-permute-start.69
  184.0 1.5 collective-permute-start.70
  186.7 2.0 collective-permute-done.70
  188.7 2.3 %collective-permute-done.71 = f32[2,8,128]{2,1,0:T(8,128)S(1)} collective-permute-done((f32[2,8,128]{2,1,0:T(8,128)S(1)}, f32[2,8,128]{2,1,0:T(8,128)S(1)}, u32[]{:S(2)}, u32[]{:S(2)}) %collective-permute-start.71) | collective-permute-done | bytes 8224 | tf_op jit(solution)/shard_map/ppermute | solution.py:52
  191.0 1.5 collective-permute-start.72
  194.6 1.5 collective-permute-done.73
  196.1 2.1 %collective-permute-done.74 = f32[2,8,128]{2,1,0:T(8,128)S(1)} collective-permute-done((f32[2,8,128]{2,1,0:T(8,128)S(1)}, f32[2,8,128]{2,1,0:T(8,128)S(1)}, u32[]{:S(2)}, u32[]{:S(2)}) %collective-permute-start.74) | collective-permute-done | bytes 8224 | tf_op jit(solution)/shard_map/ppermute | solution.py:61
  200.0 1.4 loss.1
  (216 shorter events, 48.4 us)
Async XLA Ops:
  7.6 25.3 %collective-permute-start = (bf16[576,256]{1,0:T(8,128)(2,1)}, bf16[576,256]{1,0:T(8,128)(2,1)}, u32[]{:S(2)}, u32[]{:S(2)}) collective-permute-start(bf16[576,256]{1,0:T(8,128)(2,1)} %get-tuple-element.46), channel_id=1, source_target_pairs={{0,8},{8,0},{16,24},{24,16},{1,9},{9,1},{17,25},{25,17},{2,10},{10... | collective-permute-start | bytes 884744 | tf_op jit(solution)/shard_map/ppermute | solution.py:52
  8.1 24.9 %collective-permute-start.1 = (bf16[576,256]{1,0:T(8,128)(2,1)}, bf16[576,256]{1,0:T(8,128)(2,1)}, u32[]{:S(2)}, u32[]{:S(2)}) collective-permute-start(bf16[576,256]{1,0:T(8,128)(2,1)} %get-tuple-element.47), channel_id=1, source_target_pairs={{0,16},{8,24},{16,0},{24,8},{1,17},{9,25},{17,1},{25,9},{2,18},{10... | collective-permute-start | bytes 884744 | tf_op jit(solution)/shard_map/ppermute | solution.py:52
  10.5 22.4 %collective-permute-start.2 = (bf16[576,256]{1,0:T(8,128)(2,1)}, bf16[576,256]{1,0:T(8,128)(2,1)}, u32[]{:S(2)}, u32[]{:S(2)}) collective-permute-start(bf16[576,256]{1,0:T(8,128)(2,1)} %get-tuple-element.48), channel_id=1, source_target_pairs={{0,24},{8,16},{16,8},{24,0},{1,25},{9,17},{17,9},{25,1},{2,26},{10... | collective-permute-start | bytes 884744 | tf_op jit(solution)/shard_map/ppermute | solution.py:52
  11.6 26.6 %collective-permute-start.18 = (bf16[32,4608]{1,0:T(8,128)(2,1)}, bf16[32,4608]{1,0:T(8,128)(2,1)}, u32[]{:S(2)}, u32[]{:S(2)}) collective-permute-start(bf16[32,4608]{1,0:T(8,128)(2,1)} %constant_dynamic-slice_fusion.1), channel_id=1, source_target_pairs={{0,16},{8,24},{16,0},{24,8},{1,17},{9,25},{17,1},{25,9},{2,18},{10... | collective-permute-start | bytes 884744 | tf_op jit(solution)/shard_map/ppermute | solution.py:52
  34.6 7.0 %collective-permute-start.4 = (bf16[32,2304]{1,0:T(8,128)(2,1)}, bf16[32,2304]{1,0:T(8,128)(2,1)S(1)}, u32[]{:S(2)}, u32[]{:S(2)}) collective-permute-start(bf16[32,2304]{1,0:T(8,128)(2,1)} %get-tuple-element.63), channel_id=1, source_target_pairs={{0,16},{8,24},{16,0},{24,8},{1,17},{9,25},{17,1},{25,9},{2,18},{10... | collective-permute-start | bytes 442376 | tf_op jit(solution)/shard_map/ppermute | solution.py:52
  35.0 22.9 %collective-permute-start.6 = (bf16[576,256]{1,0:T(8,128)(2,1)S(1)}, bf16[576,256]{1,0:T(8,128)(2,1)S(1)}, u32[]{:S(2)}, u32[]{:S(2)}) collective-permute-start(bf16[576,256]{1,0:T(8,128)(2,1)S(1)} %shard_map.197.refs_0_), channel_id=1, source_target_pairs={{0,1},{1,0},{2,3},{3,2},{4,5},{5,4},{6,7},{7,6},{8,9},{9,8},{10,11... | collective-permute-start | bytes 884744 | tf_op jit(solution)/shard_map/ppermute | solution.py:52
  36.7 21.6 %collective-permute-start.7 = (bf16[576,256]{1,0:T(8,128)(2,1)S(1)}, bf16[576,256]{1,0:T(8,128)(2,1)S(1)}, u32[]{:S(2)}, u32[]{:S(2)}) collective-permute-start(bf16[576,256]{1,0:T(8,128)(2,1)S(1)} %shard_map.197.refs_0_), channel_id=1, source_target_pairs={{0,16},{8,24},{16,0},{24,8},{1,17},{9,25},{17,1},{25,9},{2,18},{10... | collective-permute-start | bytes 884744 | tf_op jit(solution)/shard_map/ppermute | solution.py:52
  38.2 20.1 %collective-permute-start.8 = (bf16[576,256]{1,0:T(8,128)(2,1)S(1)}, bf16[576,256]{1,0:T(8,128)(2,1)S(1)}, u32[]{:S(2)}, u32[]{:S(2)}) collective-permute-start(bf16[576,256]{1,0:T(8,128)(2,1)S(1)} %shard_map.197.refs_0_), channel_id=1, source_target_pairs={{0,17},{1,16},{8,25},{9,24},{16,1},{17,0},{24,9},{25,8},{2,19},{3,... | collective-permute-start | bytes 884744 | tf_op jit(solution)/shard_map/ppermute | solution.py:61
  38.5 20.4 %collective-permute-start.24 = (bf16[576,256]{1,0:T(8,128)(2,1)S(1)}, bf16[576,256]{1,0:T(8,128)(2,1)S(1)}, u32[]{:S(2)}, u32[]{:S(2)}) collective-permute-start(bf16[576,256]{1,0:T(8,128)(2,1)S(1)} %shard_map.197.refs_0_), channel_id=1, source_target_pairs={{0,8},{8,0},{16,24},{24,16},{1,9},{9,1},{17,25},{25,17},{2,10},{10... | collective-permute-start | bytes 884744 | tf_op jit(solution)/shard_map/ppermute | solution.py:52
  41.6 14.7 %collective-permute-start.5 = (bf16[32,2304]{1,0:T(8,128)(2,1)}, bf16[32,2304]{1,0:T(8,128)(2,1)S(1)}, u32[]{:S(2)}, u32[]{:S(2)}) collective-permute-start(bf16[32,2304]{1,0:T(8,128)(2,1)} %copy-done.20), channel_id=1, source_target_pairs={{0,24},{8,16},{16,8},{24,0},{1,25},{9,17},{17,9},{25,1},{2,26},{10... | collective-permute-start | bytes 442376 | tf_op jit(solution)/shard_map/ppermute | solution.py:52
  56.3 16.2 %collective-permute-start.16 = (bf16[64,4608]{1,0:T(8,128)(2,1)S(1)}, bf16[64,4608]{1,0:T(8,128)(2,1)S(1)}, u32[]{:S(2)}, u32[]{:S(2)}) collective-permute-start(bf16[64,4608]{1,0:T(8,128)(2,1)S(1)} %get-tuple-element.91), channel_id=1, source_target_pairs={{0,1},{1,0},{2,3},{3,2},{4,5},{5,4},{6,7},{7,6},{8,9},{9,8},{10,11... | collective-permute-start | bytes 1769480 | tf_op jit(solution)/shard_map/ppermute | solution.py:52
  57.9 29.3 %collective-permute-start.51 = (bf16[64,4608]{1,0:T(8,128)(2,1)S(1)}, bf16[64,4608]{1,0:T(8,128)(2,1)S(1)}, u32[]{:S(2)}, u32[]{:S(2)}) collective-permute-start(bf16[64,4608]{1,0:T(8,128)(2,1)S(1)} %get-tuple-element.90), channel_id=1, source_target_pairs={{0,1},{1,0},{2,3},{3,2},{4,5},{5,4},{6,7},{7,6},{8,9},{9,8},{10,11... | collective-permute-start | bytes 1769480 | tf_op jit(solution)/shard_map/ppermute | solution.py:52
  60.0 28.8 %collective-permute-start.20 = (bf16[32,4608]{1,0:T(8,128)(2,1)}, bf16[32,4608]{1,0:T(8,128)(2,1)S(1)}, u32[]{:S(2)}, u32[]{:S(2)}) collective-permute-start(bf16[32,4608]{1,0:T(8,128)(2,1)} %collective-permute-done.18.refs_1_), channel_id=1, source_target_pairs={{0,4},{2,6},{4,0},{6,2},{1,5},{3,7},{5,1},{7,3},{8,12},{10,14},{12... | collective-permute-start | bytes 884744 | tf_op jit(solution)/shard_map/ppermute | solution.py:52
  62.5 26.7 %collective-permute-start.21 = (bf16[32,4608]{1,0:T(8,128)(2,1)}, bf16[32,4608]{1,0:T(8,128)(2,1)S(1)}, u32[]{:S(2)}, u32[]{:S(2)}) collective-permute-start(bf16[32,4608]{1,0:T(8,128)(2,1)} %collective-permute-done.18.refs_1_), channel_id=1, source_target_pairs={{0,6},{2,4},{4,2},{6,0},{1,7},{3,5},{5,3},{7,1},{8,14},{10,12},{12... | collective-permute-start | bytes 884744 | tf_op jit(solution)/shard_map/ppermute | solution.py:52
  64.0 26.7 %collective-permute-start.19 = (bf16[32,4608]{1,0:T(8,128)(2,1)}, bf16[32,4608]{1,0:T(8,128)(2,1)S(1)}, u32[]{:S(2)}, u32[]{:S(2)}) collective-permute-start(bf16[32,4608]{1,0:T(8,128)(2,1)} %collective-permute-done.18.refs_1_), channel_id=1, source_target_pairs={{0,2},{2,0},{4,6},{6,4},{1,3},{3,1},{5,7},{7,5},{8,10},{10,8},{12,... | collective-permute-start | bytes 884744 | tf_op jit(solution)/shard_map/ppermute | solution.py:52
  72.5 12.7 %collective-permute-start.28 = (bf16[128,128]{1,0:T(8,128)(2,1)S(1)}, bf16[128,128]{1,0:T(8,128)(2,1)S(1)}, u32[]{:S(2)}, u32[]{:S(2)}) collective-permute-start(bf16[128,128]{1,0:T(8,128)(2,1)S(1)} %get-tuple-element.71.own), channel_id=1, source_target_pairs={{0,2},{2,0},{4,6},{6,4},{1,3},{3,1},{5,7},{7,5},{8,10},{10,8},{12,... | collective-permute-start | bytes 98312 | tf_op jit(solution)/shard_map/ppermute | solution.py:52
  85.2 10.2 %collective-permute-start.10 = (bf16[32,2304]{1,0:T(8,128)(2,1)S(1)}, bf16[32,2304]{1,0:T(8,128)(2,1)S(1)}, u32[]{:S(2)}, u32[]{:S(2)}) collective-permute-start(bf16[32,2304]{1,0:T(8,128)(2,1)S(1)} %shard_map.198), channel_id=1, source_target_pairs={{0,4},{2,6},{4,0},{6,2},{1,5},{3,7},{5,1},{7,3},{8,12},{10,14},{12... | collective-permute-start | bytes 442376 | tf_op jit(solution)/shard_map/ppermute | solution.py:52
  87.1 9.8 %collective-permute-start.29 = (bf16[128,256]{1,0:T(8,128)(2,1)S(1)}, bf16[128,256]{1,0:T(8,128)(2,1)S(1)}, u32[]{:S(2)}, u32[]{:S(2)}) collective-permute-start(bf16[128,256]{1,0:T(8,128)(2,1)S(1)} %shard_map.200.refs_0_), channel_id=1, source_target_pairs={{0,1},{1,0},{2,3},{3,2},{4,5},{5,4},{6,7},{7,6},{8,9},{9,8},{10,11... | collective-permute-start | bytes 196616 | tf_op jit(solution)/shard_map/ppermute | solution.py:52
  88.7 8.3 %collective-permute-start.30 = (bf16[128,256]{1,0:T(8,128)(2,1)S(1)}, bf16[128,256]{1,0:T(8,128)(2,1)S(1)}, u32[]{:S(2)}, u32[]{:S(2)}) collective-permute-start(bf16[128,256]{1,0:T(8,128)(2,1)S(1)} %shard_map.200.refs_0_), channel_id=1, source_target_pairs={{0,16},{8,24},{16,0},{24,8},{1,17},{9,25},{17,1},{25,9},{2,18},{10... | collective-permute-start | bytes 196616 | tf_op jit(solution)/shard_map/ppermute | solution.py:52
  89.2 8.2 %collective-permute-start.31 = (bf16[128,256]{1,0:T(8,128)(2,1)S(1)}, bf16[128,256]{1,0:T(8,128)(2,1)S(1)}, u32[]{:S(2)}, u32[]{:S(2)}) collective-permute-start(bf16[128,256]{1,0:T(8,128)(2,1)S(1)} %shard_map.200.refs_0_), channel_id=1, source_target_pairs={{0,17},{1,16},{8,25},{9,24},{16,1},{17,0},{24,9},{25,8},{2,19},{3,... | collective-permute-start | bytes 196616 | tf_op jit(solution)/shard_map/ppermute | solution.py:61
  90.7 6.9 %collective-permute-start.32 = (bf16[128,256]{1,0:T(8,128)(2,1)S(1)}, bf16[128,256]{1,0:T(8,128)(2,1)S(1)}, u32[]{:S(2)}, u32[]{:S(2)}) collective-permute-start(bf16[128,256]{1,0:T(8,128)(2,1)S(1)} %shard_map.200.refs_0_), channel_id=1, source_target_pairs={{0,8},{8,0},{16,24},{24,16},{1,9},{9,1},{17,25},{25,17},{2,10},{10... | collective-permute-start | bytes 196616 | tf_op jit(solution)/shard_map/ppermute | solution.py:52
  95.4 15.4 %collective-permute-start.22 = (bf16[32,4608]{1,0:T(8,128)(2,1)S(1)}, bf16[32,4608]{1,0:T(8,128)(2,1)S(1)}, u32[]{:S(2)}, u32[]{:S(2)}) collective-permute-start(bf16[32,4608]{1,0:T(8,128)(2,1)S(1)} %collective-permute-done.20.refs_3_), channel_id=1, source_target_pairs={{0,1},{1,0},{2,3},{3,2},{4,5},{5,4},{6,7},{7,6},{8,9},{9,8},{10,11... | collective-permute-start | bytes 884744 | tf_op jit(solution)/shard_map/ppermute | solution.py:52
  97.5 23.0 %collective-permute-start.52 = (bf16[64,4608]{1,0:T(8,128)(2,1)S(1)}, bf16[64,4608]{1,0:T(8,128)(2,1)S(1)}, u32[]{:S(2)}, u32[]{:S(2)}) collective-permute-start(bf16[64,4608]{1,0:T(8,128)(2,1)S(1)} %collective-permute-done.16.refs_0_), channel_id=1, source_target_pairs={{0,8},{8,0},{16,24},{24,16},{1,9},{9,1},{17,25},{25,17},{2,10},{10... | collective-permute-start | bytes 1769480 | tf_op jit(solution)/shard_map/ppermute | solution.py:52
  98.2 8.6 %collective-permute-start.11 = (bf16[32,2304]{1,0:T(8,128)(2,1)S(1)}, bf16[32,2304]{1,0:T(8,128)(2,1)S(1)}, u32[]{:S(2)}, u32[]{:S(2)}) collective-permute-start(bf16[32,2304]{1,0:T(8,128)(2,1)S(1)} %shard_map.198), channel_id=1, source_target_pairs={{0,6},{2,4},{4,2},{6,0},{1,7},{3,5},{5,3},{7,1},{8,14},{10,12},{12... | collective-permute-start | bytes 442376 | tf_op jit(solution)/shard_map/ppermute | solution.py:52
  101.7 7.6 %collective-permute-start.9 = (bf16[32,2304]{1,0:T(8,128)(2,1)S(1)}, bf16[32,2304]{1,0:T(8,128)(2,1)S(1)}, u32[]{:S(2)}, u32[]{:S(2)}) collective-permute-start(bf16[32,2304]{1,0:T(8,128)(2,1)S(1)} %shard_map.198), channel_id=1, source_target_pairs={{0,2},{2,0},{4,6},{6,4},{1,3},{3,1},{5,7},{7,5},{8,10},{10,8},{12,... | collective-permute-start | bytes 442376 | tf_op jit(solution)/shard_map/ppermute | solution.py:52
  101.7 19.4 %collective-permute-start.53 = (bf16[64,4608]{1,0:T(8,128)(2,1)S(1)}, bf16[64,4608]{1,0:T(8,128)(2,1)S(1)}, u32[]{:S(2)}, u32[]{:S(2)}) collective-permute-start(bf16[64,4608]{1,0:T(8,128)(2,1)S(1)} %collective-permute-done.51.refs_1_), channel_id=1, source_target_pairs={{0,8},{8,0},{16,24},{24,16},{1,9},{9,1},{17,25},{25,17},{2,10},{10... | collective-permute-start | bytes 1769480 | tf_op jit(solution)/shard_map/ppermute | solution.py:52
  110.9 19.1 %collective-permute-start.17 = (bf16[64,4608]{1,0:T(8,128)(2,1)S(1)}, bf16[64,4608]{1,0:T(8,128)(2,1)S(1)}, u32[]{:S(2)}, u32[]{:S(2)}) collective-permute-start(bf16[64,4608]{1,0:T(8,128)(2,1)S(1)} %collective-permute-done.16.refs_0_), channel_id=1, source_target_pairs={{0,16},{8,24},{16,0},{24,8},{1,17},{9,25},{17,1},{25,9},{2,18},{10... | collective-permute-start | bytes 1769480 | tf_op jit(solution)/shard_map/ppermute | solution.py:52
  111.4 17.2 %collective-permute-start.23 = (bf16[32,4608]{1,0:T(8,128)(2,1)S(1)}, bf16[32,4608]{1,0:T(8,128)(2,1)S(1)}, u32[]{:S(2)}, u32[]{:S(2)}) collective-permute-start(bf16[32,4608]{1,0:T(8,128)(2,1)S(1)} %collective-permute-done.21.refs_4_), channel_id=1, source_target_pairs={{0,1},{1,0},{2,3},{3,2},{4,5},{5,4},{6,7},{7,6},{8,9},{9,8},{10,11... | collective-permute-start | bytes 884744 | tf_op jit(solution)/shard_map/ppermute | solution.py:52
  119.8 20.1 %collective-permute-start.13 = (bf16[128,2304]{1,0:T(8,128)(2,1)S(1)}, bf16[128,2304]{1,0:T(8,128)(2,1)S(1)}, u32[]{:S(2)}, u32[]{:S(2)}) collective-permute-start(bf16[128,2304]{1,0:T(8,128)(2,1)S(1)} %pad_maximum_fusion.refs_0_), channel_id=1, source_target_pairs={{0,1},{1,0},{2,3},{3,2},{4,5},{5,4},{6,7},{7,6},{8,9},{9,8},{10,11... | collective-permute-start | bytes 1769480 | tf_op jit(solution)/shard_map/ppermute | solution.py:52
  120.5 19.9 %collective-permute-start.12 = (bf16[128,2304]{1,0:T(8,128)(2,1)S(1)}, bf16[128,2304]{1,0:T(8,128)(2,1)S(1)}, u32[]{:S(2)}, u32[]{:S(2)}) collective-permute-start(bf16[128,2304]{1,0:T(8,128)(2,1)S(1)} %pad_maximum_fusion.refs_0_), channel_id=1, source_target_pairs={{0,16},{8,24},{16,0},{24,8},{1,17},{9,25},{17,1},{25,9},{2,18},{10... | collective-permute-start | bytes 1769480 | tf_op jit(solution)/shard_map/ppermute | solution.py:52
  121.1 19.4 %collective-permute-start.43 = (bf16[128,2304]{1,0:T(8,128)(2,1)S(1)}, bf16[128,2304]{1,0:T(8,128)(2,1)S(1)}, u32[]{:S(2)}, u32[]{:S(2)}) collective-permute-start(bf16[128,2304]{1,0:T(8,128)(2,1)S(1)} %pad_maximum_fusion.refs_0_), channel_id=1, source_target_pairs={{0,8},{8,0},{16,24},{24,16},{1,9},{9,1},{17,25},{25,17},{2,10},{10... | collective-permute-start | bytes 1769480 | tf_op jit(solution)/shard_map/ppermute | solution.py:52
  128.6 6.9 %collective-permute-start.54 = (bf16[128,512]{1,0:T(8,128)(2,1)S(1)}, bf16[128,512]{1,0:T(8,128)(2,1)S(1)}, u32[]{:S(2)}, u32[]{:S(2)}) collective-permute-start(bf16[128,512]{1,0:T(8,128)(2,1)S(1)} %shard_map.206.attention.refs_0_), channel_id=1, source_target_pairs={{0,1},{1,0},{2,3},{3,2},{4,5},{5,4},{6,7},{7,6},{8,9},{9,8},{10,11... | collective-permute-start | bytes 393224 | tf_op jit(solution)/shard_map/ppermute | solution.py:52
  130.0 9.9 %collective-permute-start.55 = (bf16[128,512]{1,0:T(8,128)(2,1)S(1)}, bf16[128,512]{1,0:T(8,128)(2,1)S(1)}, u32[]{:S(2)}, u32[]{:S(2)}) collective-permute-start(bf16[128,512]{1,0:T(8,128)(2,1)S(1)} %shard_map.206.attention.refs_0_), channel_id=1, source_target_pairs={{0,16},{8,24},{16,0},{24,8},{1,17},{9,25},{17,1},{25,9},{2,18},{10... | collective-permute-start | bytes 393224 | tf_op jit(solution)/shard_map/ppermute | solution.py:52
  140.9 11.0 %collective-permute-start.36 = (bf16[64,4608]{1,0:T(8,128)(2,1)S(1)}, bf16[64,4608]{1,0:T(8,128)(2,1)S(1)}, u32[]{:S(2)}, u32[]{:S(2)}) collective-permute-start(bf16[64,4608]{1,0:T(8,128)(2,1)S(1)} %collective-permute-done.17.refs_0_), channel_id=1, source_target_pairs={{0,8},{8,0},{16,24},{24,16},{1,9},{9,1},{17,25},{25,17},{2,10},{10... | collective-permute-start | bytes 1769480 | tf_op jit(solution)/shard_map/ppermute | solution.py:52
  141.5 22.8 %collective-permute-start.68 = (bf16[128,4608]{1,0:T(8,128)(2,1)S(1)}, bf16[128,4608]{1,0:T(8,128)(2,1)S(1)}, u32[]{:S(2)}, u32[]{:S(2)}) collective-permute-start(bf16[128,4608]{1,0:T(8,128)(2,1)S(1)} %multiply_convert_fusion.refs_0_), channel_id=1, source_target_pairs={{0,8},{8,0},{16,24},{24,16},{1,9},{9,1},{17,25},{25,17},{2,10},{10... | collective-permute-start | bytes 3538952 | tf_op jit(solution)/shard_map/ppermute | solution.py:52
  141.9 9.1 %collective-permute-start.14 = (bf16[64,2304]{1,0:T(8,128)(2,1)S(1)}, bf16[64,2304]{1,0:T(8,128)(2,1)S(1)}, u32[]{:S(2)}, u32[]{:S(2)}) collective-permute-start(bf16[64,2304]{1,0:T(8,128)(2,1)S(1)} %slice.16), channel_id=1, source_target_pairs={{0,16},{8,24},{16,0},{24,8},{1,17},{9,25},{17,1},{25,9},{2,18},{10... | collective-permute-start | bytes 884744 | tf_op jit(solution)/shard_map/ppermute | solution.py:52
  142.4 8.9 %collective-permute-start.15 = (bf16[64,2304]{1,0:T(8,128)(2,1)S(1)}, bf16[64,2304]{1,0:T(8,128)(2,1)S(1)}, u32[]{:S(2)}, u32[]{:S(2)}) collective-permute-start(bf16[64,2304]{1,0:T(8,128)(2,1)S(1)} %slice.17), channel_id=1, source_target_pairs={{0,1},{1,0},{2,3},{3,2},{4,5},{5,4},{6,7},{7,6},{8,9},{9,8},{10,11... | collective-permute-start | bytes 884744 | tf_op jit(solution)/shard_map/ppermute | solution.py:52
  143.4 8.2 %collective-permute-start.42 = (bf16[32,4608]{1,0:T(8,128)(2,1)S(1)}, bf16[32,4608]{1,0:T(8,128)(2,1)S(1)}, u32[]{:S(2)}, u32[]{:S(2)}) collective-permute-start(bf16[32,4608]{1,0:T(8,128)(2,1)S(1)} %collective-permute-done.23.refs_6_), channel_id=1, source_target_pairs={{0,8},{8,0},{16,24},{24,16},{1,9},{9,1},{17,25},{25,17},{2,10},{10... | collective-permute-start | bytes 884744 | tf_op jit(solution)/shard_map/ppermute | solution.py:52
  151.6 9.6 %collective-permute-start.44 = (bf16[128,2304]{1,0:T(8,128)(2,1)S(1)}, bf16[128,2304]{1,0:T(8,128)(2,1)S(1)}, u32[]{:S(2)}, u32[]{:S(2)}) collective-permute-start(bf16[128,2304]{1,0:T(8,128)(2,1)S(1)} %collective-permute-done.12.refs_1_), channel_id=1, source_target_pairs={{0,8},{8,0},{16,24},{24,16},{1,9},{9,1},{17,25},{25,17},{2,10},{10... | collective-permute-start | bytes 1769480 | tf_op jit(solution)/shard_map/ppermute | solution.py:52
  151.9 9.7 %collective-permute-start.45 = (bf16[128,2304]{1,0:T(8,128)(2,1)S(1)}, bf16[128,2304]{1,0:T(8,128)(2,1)S(1)}, u32[]{:S(2)}, u32[]{:S(2)}) collective-permute-start(bf16[128,2304]{1,0:T(8,128)(2,1)S(1)} %collective-permute-done.13.refs_2_), channel_id=1, source_target_pairs={{0,8},{8,0},{16,24},{24,16},{1,9},{9,1},{17,25},{25,17},{2,10},{10... | collective-permute-start | bytes 1769480 | tf_op jit(solution)/shard_map/ppermute | solution.py:52
  152.6 12.9 %collective-permute-start.56 = (bf16[128,512]{1,0:T(8,128)(2,1)S(1)}, bf16[128,512]{1,0:T(8,128)(2,1)S(1)}, u32[]{:S(2)}, u32[]{:S(2)}) collective-permute-start(bf16[128,512]{1,0:T(8,128)(2,1)S(1)} %shard_map.206.attention.refs_0_), channel_id=1, source_target_pairs={{0,17},{1,16},{8,25},{9,24},{16,1},{17,0},{24,9},{25,8},{2,19},{3,... | collective-permute-start | bytes 393224 | tf_op jit(solution)/shard_map/ppermute | solution.py:61
  153.7 13.0 %collective-permute-start.57 = (bf16[128,512]{1,0:T(8,128)(2,1)S(1)}, bf16[128,512]{1,0:T(8,128)(2,1)}, u32[]{:S(2)}, u32[]{:S(2)}) collective-permute-start(bf16[128,512]{1,0:T(8,128)(2,1)S(1)} %shard_map.206.attention.refs_0_), channel_id=1, source_target_pairs={{0,8},{8,0},{16,24},{24,16},{1,9},{9,1},{17,25},{25,17},{2,10},{10... | collective-permute-start | bytes 393224 | tf_op jit(solution)/shard_map/ppermute | solution.py:52
  161.2 10.3 %collective-permute-start.58 = (bf16[128,512]{1,0:T(8,128)(2,1)S(1)}, bf16[128,512]{1,0:T(8,128)(2,1)S(1)}, u32[]{:S(2)}, u32[]{:S(2)}) collective-permute-start(bf16[128,512]{1,0:T(8,128)(2,1)S(1)} %collective-permute-done.54.refs_1_), channel_id=1, source_target_pairs={{0,8},{8,0},{16,24},{24,16},{1,9},{9,1},{17,25},{25,17},{2,10},{10... | collective-permute-start | bytes 393224 | tf_op jit(solution)/shard_map/ppermute | solution.py:52
  161.6 9.9 %collective-permute-start.59 = (bf16[128,512]{1,0:T(8,128)(2,1)S(1)}, bf16[128,512]{1,0:T(8,128)(2,1)S(1)}, u32[]{:S(2)}, u32[]{:S(2)}) collective-permute-start(bf16[128,512]{1,0:T(8,128)(2,1)S(1)} %collective-permute-done.55.refs_2_), channel_id=1, source_target_pairs={{0,8},{8,0},{16,24},{24,16},{1,9},{9,1},{17,25},{25,17},{2,10},{10... | collective-permute-start | bytes 393224 | tf_op jit(solution)/shard_map/ppermute | solution.py:52
  164.3 7.7 %collective-permute-start.61 = (f32[8,128]{1,0:T(8,128)S(1)}, f32[8,128]{1,0:T(8,128)S(1)}, u32[]{:S(2)}, u32[]{:S(2)}) collective-permute-start(f32[8,128]{1,0:T(8,128)S(1)} %shard_map.207.refs_8_), channel_id=1, source_target_pairs={{0,1},{1,0},{2,3},{3,2},{4,5},{5,4},{6,7},{7,6},{8,9},{9,8},{10,11... | collective-permute-start | bytes 12296 | tf_op jit(solution)/shard_map/ppermute | solution.py:52
  171.5 7.3 %collective-permute-start.60 = (bf16[128,512]{1,0:T(8,128)(2,1)S(1)}, bf16[128,512]{1,0:T(8,128)(2,1)S(1)}, u32[]{:S(2)}, u32[]{:S(2)}) collective-permute-start(bf16[128,512]{1,0:T(8,128)(2,1)S(1)} %collective-permute-done.56.refs_3_), channel_id=1, source_target_pairs={{0,8},{8,0},{16,24},{24,16},{1,9},{9,1},{17,25},{25,17},{2,10},{10... | collective-permute-start | bytes 393224 | tf_op jit(solution)/shard_map/ppermute | solution.py:52
  171.5 7.2 %collective-permute-start.64 = (f32[8,128]{1,0:T(8,128)S(1)}, f32[8,128]{1,0:T(8,128)S(1)}, u32[]{:S(2)}, u32[]{:S(2)}) collective-permute-start(f32[8,128]{1,0:T(8,128)S(1)} %shard_map.207.refs_8_), channel_id=1, source_target_pairs={{0,8},{8,0},{16,24},{24,16},{1,9},{9,1},{17,25},{25,17},{2,10},{10... | collective-permute-start | bytes 12296 | tf_op jit(solution)/shard_map/ppermute | solution.py:52
  172.0 6.8 %collective-permute-start.65 = (f32[8,128]{1,0:T(8,128)S(1)}, f32[8,128]{1,0:T(8,128)S(1)}, u32[]{:S(2)}, u32[]{:S(2)}) collective-permute-start(f32[8,128]{1,0:T(8,128)S(1)} %collective-permute-done.61.refs_9_), channel_id=1, source_target_pairs={{0,8},{8,0},{16,24},{24,16},{1,9},{9,1},{17,25},{25,17},{2,10},{10... | collective-permute-start | bytes 12296 | tf_op jit(solution)/shard_map/ppermute | solution.py:52
  (63 other events, 458.8 us)

commit v2 on v1

--- a/solution.py
+++ b/solution.py
@@ -27,7 +27,7 @@
 SMEM = pl.BlockSpec(memory_space=pltpu.SMEM)
 
 
-def kernel_call(body, inputs, in_specs, outputs, scratch=(), flops=1, transcendentals=0):
+def kernel_call(body, inputs, in_specs, outputs, scratch=(), flops=1, transcendentals=0, grant=None):
     moved = sum(a.size * a.dtype.itemsize for a in inputs)
     moved += sum(int(jnp.dtype(o.dtype).itemsize) * o.size for o in outputs)
     return pl.pallas_call(
@@ -36,7 +36,7 @@
         in_specs=in_specs,
         out_specs=[VMEM] * len(outputs),
         scratch_shapes=list(scratch),
-        compiler_params=pltpu.CompilerParams(vmem_limit_bytes=KERNEL_VMEM),
+        compiler_params=pltpu.CompilerParams(vmem_limit_bytes=grant or KERNEL_VMEM),
         cost_estimate=pl.CostEstimate(
             flops=flops, bytes_accessed=moved, transcendentals=transcendentals
         ),
@@ -164,6 +164,17 @@
             )
             d = do[0, at, cols].astype(jnp.float32)
             outs[j][:, cols] = jnp.where(d * code > 0, d, 0.0).astype(jnp.bfloat16)
+
+
+def prepare_body(hidden, before, last, blocks, scaled):
+    x = hidden[...].astype(jnp.float32)
+    _, width = x.shape
+    scale = lax.rsqrt(jnp.sum(x * x, axis=1, keepdims=True) / width + EPSILON)
+    normed = (x * scale * before[...]).astype(jnp.bfloat16)
+    step = blocks.shape[2]
+    for b in range(blocks.shape[0]):
+        blocks[b] = normed[:, b * step : (b + 1) * step]
+    scaled[...] = (x * last[...]).astype(jnp.bfloat16)
 
 
 def base_input_body(place, bq, bkv, out, turned):
@@ -507,7 +518,14 @@
     dp_rest = swap(rest, DP, 1)
     both_mine = swap(dp_mine, TASK, 2)
     shares = [by_task] + [swap(by_task, TENSOR, m) for m in range(1, tensors)]
-    both_rest = [swap(shares[m], DP, 1) for m in range(tensors // 2, tensors)]
+    both_rest = []
+    for m in range(tensors // 2, tensors):
+        if m % 2:
+            start = ((tensor ^ m) % (tensors // 2)) * rows
+            block = lax.dynamic_slice_in_dim(dp_rest, start, rows, 0)
+            both_rest.append(swap(block, TASK, 2))
+        else:
+            both_rest.append(swap(shares[m], DP, 1))
     return [hidden, dp_mine, dp_rest], [both_mine], shares + both_rest
 
 
@@ -543,7 +561,8 @@
         [shape_of((row_count, features), bf16)],
     )[0]
     late = contract(paired(after(late_rows, [attention])), unembedding, f32)
-    column = jnp.concatenate([piece_out] + [swap(piece_out, TENSOR, m) for m in range(1, tensors)], axis=0)
+    shares = after([swap(piece_out, TENSOR, m) for m in range(1, tensors)], [attention])
+    column = jnp.concatenate([piece_out] + shares, axis=0)
     by_task, by_dp = swap(column, TASK, 2), swap(column, DP, 1)
     cut = column.shape[0] // 2
     parts = [
@@ -645,6 +664,7 @@
         [SMEM] * 5 + [VMEM] * 2,
         [shape_of((quarter, 2 * LANES), bf16)] * tasks,
         [pltpu.VMEM((half, LANES), f32)],
+        grant=56 * 2**20,
     )
     got_in = [kept_in[0]] + [swap(kept_in[j], TASK, j) for j in range(1, tasks)]
     kept_out = kernel_call(
@@ -661,10 +681,15 @@
         [pltpu.VMEM((half, LANES), f32)],
     )[0]
 
-    early_hidden, early_place = after([hidden, place], [kept_in[0]])
-    normed = rms_norm(early_hidden.astype(f32), pre_gain).astype(bf16)
+    early_hidden = after([hidden], [kept_in[0]])[0]
     blocks = width // quarter
-    normed = jnp.transpose(normed.reshape(row_count, blocks, quarter), (1, 0, 2))
+    normed, scaled = kernel_call(
+        prepare_body,
+        [early_hidden, pre_gain[None, :], final_gain[None, :]],
+        [VMEM] * 3,
+        [shape_of((blocks, row_count, quarter), bf16), shape_of((row_count, width), bf16)],
+    )
+    early_place = after([place], [scaled])[0]
     group_index = early_place[0] * halves + early_place[1]
     query_positions = group_index * row_count + jnp.arange(row_count, dtype=jnp.int32)
     half_head = LANES // 2
@@ -681,13 +706,15 @@
     where = jnp.concatenate(
         [place, (lax.axis_index((TASK, TENSOR, DP)) * unembedding.shape[0]).astype(jnp.int32)[None]]
     )
-    if low_rank:
-        weight_gain = (post_gain * final_gain)[None, :]
-        rows = [weight_gain, 1.0 / weight_gain, (1.0 / final_gain)[None, :], where]
-    else:
-        rows = [jnp.ones((1, width), f32), where]
-    tied = after(list(got_in) + rows, [normed, cosine, sine])
-    got_in, rows = tied[:tasks], tied[tasks:]
+
+    def row_table(post, last):
+        if not low_rank:
+            return [jnp.ones((1, width), f32), where]
+        both = (post * last)[None, :]
+        return [both, 1.0 / both, (1.0 / last)[None, :], where]
+
+    gains = after([post_gain, final_gain], [scaled])
+    rows = row_table(*gains)
     weight_gain, where = rows[0], rows[-1]
     piece_in = kernel_call(
         merge_input_body,
@@ -702,8 +729,8 @@
     got_out = [kept_out[0]] + [swap(kept_out[j], TASK, j) for j in range(1, tasks)]
     got_out = after(got_out, [b for _, _, b in pieces_in[1:4]])
     if low_rank:
-        scaled = (hidden.astype(f32) * final_gain).astype(bf16)
         early_rows, middle_rows, late_rows = send_hidden(scaled, kept_in[0], tensor)
+        early_rows[:1] = after(early_rows[:1], [cosine, sine] + list(rows))
         base = [contract(paired(early_rows[:1]), unembedding, f32)]
         base.append(contract(paired(early_rows[1:]), unembedding, f32))
     piece_out = kernel_call(

time: 202 us -> 190 us (0.941)
  waiting for transfers between devices: 78.8 us -> 62.3 us
  starting transfers between devices: 56.1 us -> 63 us
  Pallas kernels: 38.2 us -> 42.9 us
  other arithmetic: 6.95 us -> 2.96 us
  local copies, waits for them, and re-layouts: 18.9 us -> 15.7 us
    ppermute x69, waiting for transfers between devices: 75 us -> 50.2 us  [swap(): return lax.ppermute(block, axis, [(i, i ^ mask) for i in range(count)])]
    ppermute x7, waiting for transfers between devices: 3.78 us -> 12.1 us  [swap_two(): return lax.ppermute(block, (TASK, DP), route)]
    ppermute x69, starting transfers between devices: 48.8 us -> 54.1 us  [swap(): return lax.ppermute(block, axis, [(i, i ^ mask) for i in range(count)])]
    convert_element_type x2 -> x0, other arithmetic: 3 us -> none  [the longest x1 2.8 us: on_device(): normed = rms_norm(early_hidden.astype(f32), pre_gain).astype(bf16)]
    pallas_call x12 -> x13, Pallas kernels: 16.2 us -> 18.9 us  [kernel_call(): pl.pallas_call(body, out_shape=outputs, in_specs=in_specs, out_specs=[VME...]
    reshape x1 -> x0, local copies, waits for them, and re-layouts: 2.48 us -> none  [on_device(): normed.reshape(row_count, blocks, quarter)]
  transfers between devices with their start and end apart: 76 -> 76, of which waited for: 24 -> 27; matrix products, arithmetic and copies ran while one was open for 7% -> 2% of each run, Pallas kernels for 16% -> 19%
where the time goes in v2:
time: 190 us
  starting transfers between devices  63 us (33%)
  waiting for transfers between devices  62.3 us (33%)
  Pallas kernels  42.9 us (23%)
  local copies, waits for them, and re-layouts  15.7 us (8%)
  other arithmetic  2.96 us (2%)
  between operations  2.65 us (1%)
    ppermute x69, starting transfers between devices, swap(): return lax.ppermute(block, axis, [(i, i ^ mask) for i in range(count)])  54.1 us
    ppermute x69, waiting for transfers between devices, swap(): return lax.ppermute(block, axis, [(i, i ^ mask) for i in range(count)])  50.2 us
    pallas_call x4, Pallas kernels, contract(): pl.pallas_call(functools.partial(contract_body, step), out_shape=shape_of...  22.6 us
    pallas_call x13, Pallas kernels, kernel_call(): pl.pallas_call(body, out_shape=outputs, in_specs=in_specs, out_specs=[VME...  18.9 us
    unnamed x70, local copies, waits for them, and re-layouts  13.4 us
    ppermute x7, waiting for transfers between devices, swap_two(): return lax.ppermute(block, (TASK, DP), route)  12.1 us
    ppermute x7, starting transfers between devices, swap_two(): return lax.ppermute(block, (TASK, DP), route)  8.88 us
  transfers between devices with their start and end apart: 76, of which 27 were waited for; matrix products, arithmetic and copies ran while one was open for 2% of the time, Pallas kernels for 19%

profile of v2, /device:TPU:0, one launch (start us, length us, event | category | flops | bytes accessed | tf_op | source)
XLA Modules:
  0.0 189.6 jit_solution(11082693943769047770)
XLA Ops:
  1.3 2.6 %shard_map.194 = (bf16[576,256]{1,0:T(8,128)(2,1)}, bf16[576,256]{1,0:T(8,128)(2,1)}, bf16[576,256]{1,0:T(8,128)(2,1)}, bf16[576,256]{1,0:T(8,128)(2,1)}) custom-call(s32[3]{0:T(128)} %pad_add_fusion.1.place, s32[1,2,36]{2,1,0:T(2,128)} %bitcast.27, s32[1,2,1,36]{3,2,1,0:T(1,128)} %bitcast.28, s32[2,36]{1,0:T(2,128)} %bitcast.29, s32[2,1,36]{2,1,0:T(1,128)} %bitcast.30, ...), custom_call_target="tpu_custom_call" | custom-call | flops 1 | bytes 2360460 | tf_op jit(solution)/shard_map/pallas_call | solution.py:33
  4.5 2.6 %collective-permute-start.1 = (bf16[576,256]{1,0:T(8,128)(2,1)}, bf16[576,256]{1,0:T(8,128)(2,1)}, u32[]{:S(2)}, u32[]{:S(2)}) collective-permute-start(bf16[576,256]{1,0:T(8,128)(2,1)} %get-tuple-element.55), channel_id=1, source_target_pairs={{0,16},{8,24},{16,0},{24,8},{1,17},{9,25},{17,1},{25,9},{2,18},{10... | collective-permute-start | bytes 884744 | tf_op jit(solution)/shard_map/ppermute | solution.py:52
  9.7 1.7 collective-permute-start.30
  13.4 1.8 collective-permute-done.1.refs_2_
  15.2 5.9 %collective-permute-done.2.refs_3_ = bf16[576,256]{1,0:T(8,128)(2,1)} collective-permute-done((bf16[576,256]{1,0:T(8,128)(2,1)}, bf16[576,256]{1,0:T(8,128)(2,1)}, u32[]{:S(2)}, u32[]{:S(2)}) %collective-permute-start.2) | collective-permute-done | bytes 294944 | tf_op jit(solution)/shard_map/ppermute | solution.py:52
  21.0 1.6 shard_map.198.refs_0_
  22.7 1.6 collective-permute-start.6
  27.3 4.9 %collective-permute-done.6.refs_1_ = bf16[576,256]{1,0:T(8,128)(2,1)S(1)} collective-permute-done((bf16[576,256]{1,0:T(8,128)(2,1)S(1)}, bf16[576,256]{1,0:T(8,128)(2,1)S(1)}, u32[]{:S(2)}, u32[]{:S(2)}) %collective-permute-start.6) | collective-permute-done | bytes 294944 | tf_op jit(solution)/shard_map/ppermute | solution.py:52
  32.3 1.9 collective-permute-done.7.refs_2_
  34.2 7.1 %collective-permute-done.8.refs_3_ = bf16[576,256]{1,0:T(8,128)(2,1)S(1)} collective-permute-done((bf16[576,256]{1,0:T(8,128)(2,1)S(1)}, bf16[576,256]{1,0:T(8,128)(2,1)S(1)}, u32[]{:S(2)}, u32[]{:S(2)}) %collective-permute-start.8) | collective-permute-done | bytes 294944 | tf_op jit(solution)/shard_map/ppermute | solution.py:61
  43.5 1.8 collective-permute-start.35
  45.3 1.6 collective-permute-start.4
  49.4 2.6 %collective-permute-start.32 = (bf16[32,4608]{1,0:T(8,128)(2,1)}, bf16[32,4608]{1,0:T(8,128)(2,1)}, u32[]{:S(2)}, u32[]{:S(2)}) collective-permute-start(bf16[32,4608]{1,0:T(8,128)(2,1)} %collective-permute-done.30.refs_1_), channel_id=1, source_target_pairs={{0,4},{2,6},{4,0},{6,2},{1,5},{3,7},{5,1},{7,3},{8,12},{10,14},{12... | collective-permute-start | bytes 884744 | tf_op jit(solution)/shard_map/ppermute | solution.py:52
  52.1 1.6 collective-permute-start.31
  54.2 1.6 collective-permute-start.16
  56.4 1.5 shard_map.199
  57.9 1.6 collective-permute-done.28.refs_0_
  59.5 2.6 %collective-permute-start.10 = (bf16[32,2304]{1,0:T(8,128)(2,1)}, bf16[32,2304]{1,0:T(8,128)(2,1)}, u32[]{:S(2)}, u32[]{:S(2)}) collective-permute-start(bf16[32,2304]{1,0:T(8,128)(2,1)} %shard_map.199), channel_id=1, source_target_pairs={{0,4},{2,6},{4,0},{6,2},{1,5},{3,7},{5,1},{7,3},{8,12},{10,14},{12... | collective-permute-start | bytes 442376 | tf_op jit(solution)/shard_map/ppermute | solution.py:52
  62.0 6.9 %collective-permute-done.16.other = bf16[128,128]{1,0:T(8,128)(2,1)S(1)} collective-permute-done((bf16[128,128]{1,0:T(8,128)(2,1)S(1)}, bf16[128,128]{1,0:T(8,128)(2,1)S(1)}, u32[]{:S(2)}, u32[]{:S(2)}) %collective-permute-start.16) | collective-permute-done | bytes 32800 | tf_op jit(solution)/shard_map/ppermute | solution.py:52
  68.9 2.7 %collective-permute-start.11 = (bf16[32,2304]{1,0:T(8,128)(2,1)}, bf16[32,2304]{1,0:T(8,128)(2,1)}, u32[]{:S(2)}, u32[]{:S(2)}) collective-permute-start(bf16[32,2304]{1,0:T(8,128)(2,1)} %shard_map.199), channel_id=1, source_target_pairs={{0,6},{2,4},{4,2},{6,0},{1,7},{3,5},{5,3},{7,1},{8,14},{10,12},{12... | collective-permute-start | bytes 442376 | tf_op jit(solution)/shard_map/ppermute | solution.py:52
  73.5 1.5 collective-permute-start.18
  75.0 1.5 collective-permute-start.19
  78.6 1.9 collective-permute-done.19.refs_3_
  81.8 3.4 %collective-permute-start.33 = (bf16[32,4608]{1,0:T(8,128)(2,1)}, bf16[32,4608]{1,0:T(8,128)(2,1)}, u32[]{:S(2)}, u32[]{:S(2)}) collective-permute-start(bf16[32,4608]{1,0:T(8,128)(2,1)} %collective-permute-done.30.refs_1_), channel_id=1, source_target_pairs={{0,6},{2,4},{4,2},{6,0},{1,7},{3,5},{5,3},{7,1},{8,14},{10,12},{12... | collective-permute-start | bytes 884744 | tf_op jit(solution)/shard_map/ppermute | solution.py:52
  85.9 1.5 collective-permute-start.36
  94.5 1.6 shard_map.202.refs_0_
  96.7 2.4 %collective-permute-start.49 = (bf16[128,128]{1,0:T(8,128)(2,1)S(1)}, bf16[128,128]{1,0:T(8,128)(2,1)S(1)}, u32[]{:S(2)}, u32[]{:S(2)}) collective-permute-start(bf16[128,128]{1,0:T(8,128)(2,1)S(1)} %shard_map.202.refs_0_), channel_id=1, source_target_pairs={{0,2},{2,0},{4,6},{6,4},{1,3},{3,1},{5,7},{7,5},{8,10},{10,8},{12,... | collective-permute-start | bytes 98312 | tf_op jit(solution)/shard_map/ppermute | solution.py:52
  100.2 5.1 %collective-permute-done.34.refs_5_ = bf16[32,4608]{1,0:T(8,128)(2,1)S(1)} collective-permute-done((bf16[32,4608]{1,0:T(8,128)(2,1)}, bf16[32,4608]{1,0:T(8,128)(2,1)S(1)}, u32[]{:S(2)}, u32[]{:S(2)}) %collective-permute-start.34) | collective-permute-done | bytes 294944 | tf_op jit(solution)/shard_map/ppermute | solution.py:52
  105.3 1.5 collective-permute-start.50
  106.7 1.5 collective-permute-start.51
  108.3 1.7 collective-permute-start.25
  110.2 3.3 %copy-done = bf16[896,4608]{1,0:T(8,128)(2,1)S(1)} copy-done((bf16[896,4608]{1,0:T(8,128)(2,1)S(1)}, bf16[896,4608]{1,0:T(8,128)(2,1)}, u32[]{:S(2)}) %copy-start) | copy-done | bytes 8257560
  113.6 5.0 %shard_map.206.refs_17_ = f32[256,896]{1,0:T(8,128)S(1)} custom-call(bf16[896,4608]{1,0:T(8,128)(2,1)S(1)} %copy-done, bf16[64,4608]{1,0:T(8,128)(2,1)S(1)} %collective-permute-done.28.refs_0_, bf16[64,4608]{1,0:T(8,128)(2,1)S(1)} %collective-permute-done.35.refs_1_, bf16[64,4608]{1,0:T(8,128)(2,1)} %collective-permute-done.52.refs_2_, ...), custom_call_target="tpu_custom_call" | custom-call | flops 2113929216 | bytes 11534336 | tf_op jit(solution)/shard_map/pallas_call | solution.py:351
  119.2 1.7 collective-permute-start.54
  121.4 3.8 %collective-permute-done.54.refs_1_ = bf16[128,512]{1,0:T(8,128)(2,1)S(1)} collective-permute-done((bf16[128,512]{1,0:T(8,128)(2,1)S(1)}, bf16[128,512]{1,0:T(8,128)(2,1)S(1)}, u32[]{:S(2)}, u32[]{:S(2)}) %collective-permute-start.54) | collective-permute-done | bytes 131104 | tf_op jit(solution)/shard_map/ppermute | solution.py:52
  131.9 7.0 %collective-permute-done.26.refs_3_ = bf16[64,2304]{1,0:T(8,128)(2,1)S(1)} collective-permute-done((bf16[64,2304]{1,0:T(8,128)(2,1)S(1)}, bf16[64,2304]{1,0:T(8,128)(2,1)S(1)}, u32[]{:S(2)}, u32[]{:S(2)}) %collective-permute-start.26) | collective-permute-done | bytes 294944 | tf_op jit(solution)/shard_map/ppermute | solution.py:52
  140.5 1.7 collective-permute-start.56
  142.2 7.6 %shard_map.203.refs_18_ = f32[512,896]{1,0:T(8,128)S(1)} custom-call(bf16[896,4608]{1,0:T(8,128)(2,1)S(1)} %copy-done, bf16[64,4608]{1,0:T(8,128)(2,1)} %collective-permute-done.29.refs_0_, bf16[32,4608]{1,0:T(8,128)(2,1)} %collective-permute-done.30.refs_1_, bf16[32,4608]{1,0:T(8,128)(2,1)} %collective-permute-done.31.refs_2_, ...), custom_call_target="tpu_custom_call" | custom-call | flops 4227858432 | bytes 14811136 | tf_op jit(solution)/shard_map/pallas_call | solution.py:351
  151.4 1.7 shard_map.208.refs_8_
  154.9 1.7 collective-permute-start.63
  156.6 3.6 %shard_map.209.refs_16_ = f32[256,896]{1,0:T(8,128)S(1)} custom-call(bf16[896,4608]{1,0:T(8,128)(2,1)S(1)} %bitcast.20, bf16[128,4608]{1,0:T(8,128)(2,1)S(1)} %get-tuple-element.85.refs_0_, bf16[128,4608]{1,0:T(8,128)(2,1)S(1)} %collective-permute-done.68.refs_1_), custom_call_target="tpu_custom_call" | custom-call | flops 2113929216 | bytes 11534336 | tf_op jit(solution)/shard_map/pallas_call | solution.py:351
  161.4 6.3 %shard_map.205.mixed = bf16[512,896]{1,0:T(8,128)(2,1)S(1)} custom-call(bf16[896,4608]{1,0:T(8,128)(2,1)S(1)} %bitcast.20, bf16[512,4608]{1,0:T(8,128)(2,1)S(1)} %bitcast.22), custom_call_target="tpu_custom_call" | custom-call | flops 4227858432 | bytes 14811136 | tf_op jit(solution)/shard_map/pallas_call | solution.py:351
  167.8 3.7 %shard_map.210 = f32[2,8,128]{2,1,0:T(8,128)S(1)} custom-call(s32[4]{0:T(128)S(1)} %pad_add_fusion.place, s32[8,128]{1,0:T(8,128)S(1)} %bitcast.24, bf16[512,896]{1,0:T(8,128)(2,1)S(1)} %shard_map.205.mixed, bf16[128,512]{1,0:T(8,128)(2,1)S(1)} %shard_map.207.attention.refs_0_, bf16[128,512]{1,0:T(8,128)(2,1)S(1)} %collective-permute-done.54.refs_1_, ...), custom_call_target="tpu_custom_call" | custom-call | flops 939524096 | bytes 5681168 | tf_op jit(solution)/shard_map/pallas_call | solution.py:33
  171.6 2.6 %collective-permute-start.70 = (f32[2,8,128]{2,1,0:T(8,128)S(1)}, f32[2,8,128]{2,1,0:T(8,128)S(1)}, u32[]{:S(2)}, u32[]{:S(2)}) collective-permute-start(f32[2,8,128]{2,1,0:T(8,128)S(1)} %shard_map.210), channel_id=1, source_target_pairs={{0,4},{2,6},{4,0},{6,2},{1,5},{3,7},{5,1},{7,3},{8,12},{10,14},{12... | collective-permute-start | bytes 24584 | tf_op jit(solution)/shard_map/ppermute | solution.py:52
  174.1 1.8 collective-permute-start.71
  176.2 3.4 %collective-permute-done.71 = f32[2,8,128]{2,1,0:T(8,128)S(1)} collective-permute-done((f32[2,8,128]{2,1,0:T(8,128)S(1)}, f32[2,8,128]{2,1,0:T(8,128)S(1)}, u32[]{:S(2)}, u32[]{:S(2)}) %collective-permute-start.71) | collective-permute-done | bytes 8224 | tf_op jit(solution)/shard_map/ppermute | solution.py:52
  181.6 1.5 collective-permute-start.74
  184.1 2.1 %collective-permute-done.74 = f32[2,8,128]{2,1,0:T(8,128)S(1)} collective-permute-done((f32[2,8,128]{2,1,0:T(8,128)S(1)}, f32[2,8,128]{2,1,0:T(8,128)S(1)}, u32[]{:S(2)}, u32[]{:S(2)}) %collective-permute-start.74) | collective-permute-done | bytes 8224 | tf_op jit(solution)/shard_map/ppermute | solution.py:61
  (214 shorter events, 49.0 us)
Async XLA Ops:
  3.9 9.5 %collective-permute-start = (bf16[576,256]{1,0:T(8,128)(2,1)}, bf16[576,256]{1,0:T(8,128)(2,1)}, u32[]{:S(2)}, u32[]{:S(2)}) collective-permute-start(bf16[576,256]{1,0:T(8,128)(2,1)} %get-tuple-element.54), channel_id=1, source_target_pairs={{0,8},{8,0},{16,24},{24,16},{1,9},{9,1},{17,25},{25,17},{2,10},{10... | collective-permute-start | bytes 884744 | tf_op jit(solution)/shard_map/ppermute | solution.py:52
  4.5 10.7 %collective-permute-start.1 = (bf16[576,256]{1,0:T(8,128)(2,1)}, bf16[576,256]{1,0:T(8,128)(2,1)}, u32[]{:S(2)}, u32[]{:S(2)}) collective-permute-start(bf16[576,256]{1,0:T(8,128)(2,1)} %get-tuple-element.55), channel_id=1, source_target_pairs={{0,16},{8,24},{16,0},{24,8},{1,17},{9,25},{17,1},{25,9},{2,18},{10... | collective-permute-start | bytes 884744 | tf_op jit(solution)/shard_map/ppermute | solution.py:52
  7.0 14.0 %collective-permute-start.2 = (bf16[576,256]{1,0:T(8,128)(2,1)}, bf16[576,256]{1,0:T(8,128)(2,1)}, u32[]{:S(2)}, u32[]{:S(2)}) collective-permute-start(bf16[576,256]{1,0:T(8,128)(2,1)} %get-tuple-element.56), channel_id=1, source_target_pairs={{0,24},{8,16},{16,8},{24,0},{1,25},{9,17},{17,9},{25,1},{2,26},{10... | collective-permute-start | bytes 884744 | tf_op jit(solution)/shard_map/ppermute | solution.py:52
  9.7 33.4 %collective-permute-start.30 = (bf16[32,4608]{1,0:T(8,128)(2,1)}, bf16[32,4608]{1,0:T(8,128)(2,1)}, u32[]{:S(2)}, u32[]{:S(2)}) collective-permute-start(bf16[32,4608]{1,0:T(8,128)(2,1)} %constant_dynamic-slice_fusion.2), channel_id=1, source_target_pairs={{0,16},{8,24},{16,0},{24,8},{1,17},{9,25},{17,1},{25,9},{2,18},{10... | collective-permute-start | bytes 884744 | tf_op jit(solution)/shard_map/ppermute | solution.py:52
  22.7 9.6 %collective-permute-start.6 = (bf16[576,256]{1,0:T(8,128)(2,1)S(1)}, bf16[576,256]{1,0:T(8,128)(2,1)S(1)}, u32[]{:S(2)}, u32[]{:S(2)}) collective-permute-start(bf16[576,256]{1,0:T(8,128)(2,1)S(1)} %shard_map.198.refs_0_), channel_id=1, source_target_pairs={{0,1},{1,0},{2,3},{3,2},{4,5},{5,4},{6,7},{7,6},{8,9},{9,8},{10,11... | collective-permute-start | bytes 884744 | tf_op jit(solution)/shard_map/ppermute | solution.py:52
  24.3 9.9 %collective-permute-start.7 = (bf16[576,256]{1,0:T(8,128)(2,1)S(1)}, bf16[576,256]{1,0:T(8,128)(2,1)S(1)}, u32[]{:S(2)}, u32[]{:S(2)}) collective-permute-start(bf16[576,256]{1,0:T(8,128)(2,1)S(1)} %shard_map.198.refs_0_), channel_id=1, source_target_pairs={{0,16},{8,24},{16,0},{24,8},{1,17},{9,25},{17,1},{25,9},{2,18},{10... | collective-permute-start | bytes 884744 | tf_op jit(solution)/shard_map/ppermute | solution.py:52
  25.7 15.6 %collective-permute-start.8 = (bf16[576,256]{1,0:T(8,128)(2,1)S(1)}, bf16[576,256]{1,0:T(8,128)(2,1)S(1)}, u32[]{:S(2)}, u32[]{:S(2)}) collective-permute-start(bf16[576,256]{1,0:T(8,128)(2,1)S(1)} %shard_map.198.refs_0_), channel_id=1, source_target_pairs={{0,17},{1,16},{8,25},{9,24},{16,1},{17,0},{24,9},{25,8},{2,19},{3,... | collective-permute-start | bytes 884744 | tf_op jit(solution)/shard_map/ppermute | solution.py:61
  27.3 16.3 %collective-permute-start.12 = (bf16[576,256]{1,0:T(8,128)(2,1)S(1)}, bf16[576,256]{1,0:T(8,128)(2,1)S(1)}, u32[]{:S(2)}, u32[]{:S(2)}) collective-permute-start(bf16[576,256]{1,0:T(8,128)(2,1)S(1)} %shard_map.198.refs_0_), channel_id=1, source_target_pairs={{0,8},{8,0},{16,24},{24,16},{1,9},{9,1},{17,25},{25,17},{2,10},{10... | collective-permute-start | bytes 884744 | tf_op jit(solution)/shard_map/ppermute | solution.py:52
  32.3 13.0 %collective-permute-start.13 = (bf16[576,256]{1,0:T(8,128)(2,1)S(1)}, bf16[576,256]{1,0:T(8,128)(2,1)S(1)}, u32[]{:S(2)}, u32[]{:S(2)}) collective-permute-start(bf16[576,256]{1,0:T(8,128)(2,1)S(1)} %collective-permute-done.6.refs_1_), channel_id=1, source_target_pairs={{0,8},{8,0},{16,24},{24,16},{1,9},{9,1},{17,25},{25,17},{2,10},{10... | collective-permute-start | bytes 884744 | tf_op jit(solution)/shard_map/ppermute | solution.py:52
  34.2 11.1 %collective-permute-start.14 = (bf16[576,256]{1,0:T(8,128)(2,1)S(1)}, bf16[576,256]{1,0:T(8,128)(2,1)S(1)}, u32[]{:S(2)}, u32[]{:S(2)}) collective-permute-start(bf16[576,256]{1,0:T(8,128)(2,1)S(1)} %collective-permute-done.7.refs_2_), channel_id=1, source_target_pairs={{0,8},{8,0},{16,24},{24,16},{1,9},{9,1},{17,25},{25,17},{2,10},{10... | collective-permute-start | bytes 884744 | tf_op jit(solution)/shard_map/ppermute | solution.py:52
  43.2 16.3 %collective-permute-start.28 = (bf16[64,4608]{1,0:T(8,128)(2,1)S(1)}, bf16[64,4608]{1,0:T(8,128)(2,1)S(1)}, u32[]{:S(2)}, u32[]{:S(2)}) collective-permute-start(bf16[64,4608]{1,0:T(8,128)(2,1)S(1)} %get-tuple-element.91), channel_id=1, source_target_pairs={{0,1},{1,0},{2,3},{3,2},{4,5},{5,4},{6,7},{7,6},{8,9},{9,8},{10,11... | collective-permute-start | bytes 1769480 | tf_op jit(solution)/shard_map/ppermute | solution.py:52
  43.5 29.5 %collective-permute-start.35 = (bf16[64,4608]{1,0:T(8,128)(2,1)S(1)}, bf16[64,4608]{1,0:T(8,128)(2,1)S(1)}, u32[]{:S(2)}, u32[]{:S(2)}) collective-permute-start(bf16[64,4608]{1,0:T(8,128)(2,1)S(1)} %get-tuple-element.90), channel_id=1, source_target_pairs={{0,1},{1,0},{2,3},{3,2},{4,5},{5,4},{6,7},{7,6},{8,9},{9,8},{10,11... | collective-permute-start | bytes 1769480 | tf_op jit(solution)/shard_map/ppermute | solution.py:52
  46.9 7.3 %collective-permute-start.5 = (bf16[32,2304]{1,0:T(8,128)(2,1)S(1)}, bf16[32,2304]{1,0:T(8,128)(2,1)S(1)}, u32[]{:S(2)}, u32[]{:S(2)}) collective-permute-start(bf16[32,2304]{1,0:T(8,128)(2,1)S(1)} %get-tuple-element.60), channel_id=1, source_target_pairs={{0,24},{8,16},{16,8},{24,0},{1,25},{9,17},{17,9},{25,1},{2,26},{10... | collective-permute-start | bytes 442376 | tf_op jit(solution)/shard_map/ppermute | solution.py:52
  49.4 24.1 %collective-permute-start.32 = (bf16[32,4608]{1,0:T(8,128)(2,1)}, bf16[32,4608]{1,0:T(8,128)(2,1)}, u32[]{:S(2)}, u32[]{:S(2)}) collective-permute-start(bf16[32,4608]{1,0:T(8,128)(2,1)} %collective-permute-done.30.refs_1_), channel_id=1, source_target_pairs={{0,4},{2,6},{4,0},{6,2},{1,5},{3,7},{5,1},{7,3},{8,12},{10,14},{12... | collective-permute-start | bytes 884744 | tf_op jit(solution)/shard_map/ppermute | solution.py:52
  52.1 22.9 %collective-permute-start.31 = (bf16[32,4608]{1,0:T(8,128)(2,1)}, bf16[32,4608]{1,0:T(8,128)(2,1)}, u32[]{:S(2)}, u32[]{:S(2)}) collective-permute-start(bf16[32,4608]{1,0:T(8,128)(2,1)} %collective-permute-done.30.refs_1_), channel_id=1, source_target_pairs={{0,2},{2,0},{4,6},{6,4},{1,3},{3,1},{5,7},{7,5},{8,10},{10,8},{12,... | collective-permute-start | bytes 884744 | tf_op jit(solution)/shard_map/ppermute | solution.py:52
  54.2 14.7 %collective-permute-start.16 = (bf16[128,128]{1,0:T(8,128)(2,1)S(1)}, bf16[128,128]{1,0:T(8,128)(2,1)S(1)}, u32[]{:S(2)}, u32[]{:S(2)}) collective-permute-start(bf16[128,128]{1,0:T(8,128)(2,1)S(1)} %get-tuple-element.68.own), channel_id=1, source_target_pairs={{0,2},{2,0},{4,6},{6,4},{1,3},{3,1},{5,7},{7,5},{8,10},{10,8},{12,... | collective-permute-start | bytes 98312 | tf_op jit(solution)/shard_map/ppermute | solution.py:52
  59.5 17.0 %collective-permute-start.10 = (bf16[32,2304]{1,0:T(8,128)(2,1)}, bf16[32,2304]{1,0:T(8,128)(2,1)}, u32[]{:S(2)}, u32[]{:S(2)}) collective-permute-start(bf16[32,2304]{1,0:T(8,128)(2,1)} %shard_map.199), channel_id=1, source_target_pairs={{0,4},{2,6},{4,0},{6,2},{1,5},{3,7},{5,1},{7,3},{8,12},{10,14},{12... | collective-permute-start | bytes 442376 | tf_op jit(solution)/shard_map/ppermute | solution.py:52
  68.9 7.8 %collective-permute-start.11 = (bf16[32,2304]{1,0:T(8,128)(2,1)}, bf16[32,2304]{1,0:T(8,128)(2,1)}, u32[]{:S(2)}, u32[]{:S(2)}) collective-permute-start(bf16[32,2304]{1,0:T(8,128)(2,1)} %shard_map.199), channel_id=1, source_target_pairs={{0,6},{2,4},{4,2},{6,0},{1,7},{3,5},{5,3},{7,1},{8,14},{10,12},{12... | collective-permute-start | bytes 442376 | tf_op jit(solution)/shard_map/ppermute | solution.py:52
  76.7 8.5 %collective-permute-start.20 = (bf16[128,256]{1,0:T(8,128)(2,1)}, bf16[128,256]{1,0:T(8,128)(2,1)S(1)}, u32[]{:S(2)}, u32[]{:S(2)}) collective-permute-start(bf16[128,256]{1,0:T(8,128)(2,1)} %shard_map.201.refs_0_), channel_id=1, source_target_pairs={{0,8},{8,0},{16,24},{24,16},{1,9},{9,1},{17,25},{25,17},{2,10},{10... | collective-permute-start | bytes 196616 | tf_op jit(solution)/shard_map/ppermute | solution.py:52
  78.0 9.3 %collective-permute-start.21 = (bf16[128,256]{1,0:T(8,128)(2,1)}, bf16[128,256]{1,0:T(8,128)(2,1)S(1)}, u32[]{:S(2)}, u32[]{:S(2)}) collective-permute-start(bf16[128,256]{1,0:T(8,128)(2,1)} %collective-permute-done.17.refs_1_), channel_id=1, source_target_pairs={{0,8},{8,0},{16,24},{24,16},{1,9},{9,1},{17,25},{25,17},{2,10},{10... | collective-permute-start | bytes 196616 | tf_op jit(solution)/shard_map/ppermute | solution.py:52
  78.1 10.4 %collective-permute-start.22 = (bf16[128,256]{1,0:T(8,128)(2,1)}, bf16[128,256]{1,0:T(8,128)(2,1)S(1)}, u32[]{:S(2)}, u32[]{:S(2)}) collective-permute-start(bf16[128,256]{1,0:T(8,128)(2,1)} %collective-permute-done.18.refs_2_), channel_id=1, source_target_pairs={{0,8},{8,0},{16,24},{24,16},{1,9},{9,1},{17,25},{25,17},{2,10},{10... | collective-permute-start | bytes 196616 | tf_op jit(solution)/shard_map/ppermute | solution.py:52
  80.5 8.7 %collective-permute-start.23 = (bf16[128,256]{1,0:T(8,128)(2,1)}, bf16[128,256]{1,0:T(8,128)(2,1)S(1)}, u32[]{:S(2)}, u32[]{:S(2)}) collective-permute-start(bf16[128,256]{1,0:T(8,128)(2,1)} %collective-permute-done.19.refs_3_), channel_id=1, source_target_pairs={{0,8},{8,0},{16,24},{24,16},{1,9},{9,1},{17,25},{25,17},{2,10},{10... | collective-permute-start | bytes 196616 | tf_op jit(solution)/shard_map/ppermute | solution.py:52
  81.8 14.2 %collective-permute-start.33 = (bf16[32,4608]{1,0:T(8,128)(2,1)}, bf16[32,4608]{1,0:T(8,128)(2,1)}, u32[]{:S(2)}, u32[]{:S(2)}) collective-permute-start(bf16[32,4608]{1,0:T(8,128)(2,1)} %collective-permute-done.30.refs_1_), channel_id=1, source_target_pairs={{0,6},{2,4},{4,2},{6,0},{1,7},{3,5},{5,3},{7,1},{8,14},{10,12},{12... | collective-permute-start | bytes 884744 | tf_op jit(solution)/shard_map/ppermute | solution.py:52
  85.9 10.8 %collective-permute-start.36 = (bf16[32,4608]{1,0:T(8,128)(2,1)}, bf16[32,4608]{1,0:T(8,128)(2,1)}, u32[]{:S(2)}, u32[]{:S(2)}) collective-permute-start(bf16[32,4608]{1,0:T(8,128)(2,1)} %constant_dynamic-slice_fusion), channel_id=1, source_target_pairs={{0,16},{8,24},{16,0},{24,8},{1,17},{9,25},{17,1},{25,9},{2,18},{10... | collective-permute-start | bytes 884744 | tf_op jit(solution)/shard_map/ppermute | solution.py:52
  88.0 18.7 %collective-permute-start.29 = (bf16[64,4608]{1,0:T(8,128)(2,1)S(1)}, bf16[64,4608]{1,0:T(8,128)(2,1)}, u32[]{:S(2)}, u32[]{:S(2)}) collective-permute-start(bf16[64,4608]{1,0:T(8,128)(2,1)S(1)} %collective-permute-done.28.refs_0_), channel_id=1, source_target_pairs={{0,16},{8,24},{16,0},{24,8},{1,17},{9,25},{17,1},{25,9},{2,18},{10... | collective-permute-start | bytes 1769480 | tf_op jit(solution)/shard_map/ppermute | solution.py:52
  89.2 20.9 %collective-permute-start.52 = (bf16[64,4608]{1,0:T(8,128)(2,1)S(1)}, bf16[64,4608]{1,0:T(8,128)(2,1)}, u32[]{:S(2)}, u32[]{:S(2)}) collective-permute-start(bf16[64,4608]{1,0:T(8,128)(2,1)S(1)} %collective-permute-done.28.refs_0_), channel_id=1, source_target_pairs={{0,8},{8,0},{16,24},{24,16},{1,9},{9,1},{17,25},{25,17},{2,10},{10... | collective-permute-start | bytes 1769480 | tf_op jit(solution)/shard_map/ppermute | solution.py:52
  89.8 20.4 %collective-permute-start.53 = (bf16[64,4608]{1,0:T(8,128)(2,1)S(1)}, bf16[64,4608]{1,0:T(8,128)(2,1)}, u32[]{:S(2)}, u32[]{:S(2)}) collective-permute-start(bf16[64,4608]{1,0:T(8,128)(2,1)S(1)} %collective-permute-done.35.refs_1_), channel_id=1, source_target_pairs={{0,8},{8,0},{16,24},{24,16},{1,9},{9,1},{17,25},{25,17},{2,10},{10... | collective-permute-start | bytes 1769480 | tf_op jit(solution)/shard_map/ppermute | solution.py:52
  96.1 9.2 %collective-permute-start.34 = (bf16[32,4608]{1,0:T(8,128)(2,1)}, bf16[32,4608]{1,0:T(8,128)(2,1)S(1)}, u32[]{:S(2)}, u32[]{:S(2)}) collective-permute-start(bf16[32,4608]{1,0:T(8,128)(2,1)} %collective-permute-done.32.refs_3_), channel_id=1, source_target_pairs={{0,1},{1,0},{2,3},{3,2},{4,5},{5,4},{6,7},{7,6},{8,9},{9,8},{10,11... | collective-permute-start | bytes 884744 | tf_op jit(solution)/shard_map/ppermute | solution.py:52
  96.7 11.6 %collective-permute-start.49 = (bf16[128,128]{1,0:T(8,128)(2,1)S(1)}, bf16[128,128]{1,0:T(8,128)(2,1)S(1)}, u32[]{:S(2)}, u32[]{:S(2)}) collective-permute-start(bf16[128,128]{1,0:T(8,128)(2,1)S(1)} %shard_map.202.refs_0_), channel_id=1, source_target_pairs={{0,2},{2,0},{4,6},{6,4},{1,3},{3,1},{5,7},{7,5},{8,10},{10,8},{12,... | collective-permute-start | bytes 98312 | tf_op jit(solution)/shard_map/ppermute | solution.py:52
  105.3 13.3 %collective-permute-start.50 = (bf16[128,128]{1,0:T(8,128)(2,1)S(1)}, bf16[128,128]{1,0:T(8,128)(2,1)S(1)}, u32[]{:S(2)}, u32[]{:S(2)}) collective-permute-start(bf16[128,128]{1,0:T(8,128)(2,1)S(1)} %shard_map.202.refs_0_), channel_id=1, source_target_pairs={{0,4},{2,6},{4,0},{6,2},{1,5},{3,7},{5,1},{7,3},{8,12},{10,14},{12... | collective-permute-start | bytes 98312 | tf_op jit(solution)/shard_map/ppermute | solution.py:52
  106.7 11.9 %collective-permute-start.51 = (bf16[128,128]{1,0:T(8,128)(2,1)S(1)}, bf16[128,128]{1,0:T(8,128)(2,1)S(1)}, u32[]{:S(2)}, u32[]{:S(2)}) collective-permute-start(bf16[128,128]{1,0:T(8,128)(2,1)S(1)} %shard_map.202.refs_0_), channel_id=1, source_target_pairs={{0,6},{2,4},{4,2},{6,0},{1,7},{3,5},{5,3},{7,1},{8,14},{10,12},{12... | collective-permute-start | bytes 98312 | tf_op jit(solution)/shard_map/ppermute | solution.py:52
  108.3 20.6 %collective-permute-start.25 = (bf16[128,2304]{1,0:T(8,128)(2,1)S(1)}, bf16[128,2304]{1,0:T(8,128)(2,1)S(1)}, u32[]{:S(2)}, u32[]{:S(2)}) collective-permute-start(bf16[128,2304]{1,0:T(8,128)(2,1)S(1)} %pad_maximum_fusion.refs_0_), channel_id=1, source_target_pairs={{0,1},{1,0},{2,3},{3,2},{4,5},{5,4},{6,7},{7,6},{8,9},{9,8},{10,11... | collective-permute-start | bytes 1769480 | tf_op jit(solution)/shard_map/ppermute | solution.py:52
  110.0 19.3 %collective-permute-start.24 = (bf16[128,2304]{1,0:T(8,128)(2,1)S(1)}, bf16[128,2304]{1,0:T(8,128)(2,1)S(1)}, u32[]{:S(2)}, u32[]{:S(2)}) collective-permute-start(bf16[128,2304]{1,0:T(8,128)(2,1)S(1)} %pad_maximum_fusion.refs_0_), channel_id=1, source_target_pairs={{0,16},{8,24},{16,0},{24,8},{1,17},{9,25},{17,1},{25,9},{2,18},{10... | collective-permute-start | bytes 1769480 | tf_op jit(solution)/shard_map/ppermute | solution.py:52
  110.2 16.3 %collective-permute-start.38 = (bf16[32,4608]{1,0:T(8,128)(2,1)}, bf16[32,4608]{1,0:T(8,128)(2,1)S(1)}, u32[]{:S(2)}, u32[]{:S(2)}) collective-permute-start(bf16[32,4608]{1,0:T(8,128)(2,1)} %collective-permute-done.30.refs_1_), channel_id=1, source_target_pairs={{0,8},{8,0},{16,24},{24,16},{1,9},{9,1},{17,25},{25,17},{2,10},{10... | collective-permute-start | bytes 884744 | tf_op jit(solution)/shard_map/ppermute | solution.py:52
  128.7 10.8 %collective-permute-start.44 = (bf16[128,2304]{1,0:T(8,128)(2,1)S(1)}, bf16[128,2304]{1,0:T(8,128)(2,1)S(1)}, u32[]{:S(2)}, u32[]{:S(2)}) collective-permute-start(bf16[128,2304]{1,0:T(8,128)(2,1)S(1)} %pad_maximum_fusion.refs_0_), channel_id=1, source_target_pairs={{0,8},{8,0},{16,24},{24,16},{1,9},{9,1},{17,25},{25,17},{2,10},{10... | collective-permute-start | bytes 1769480 | tf_op jit(solution)/shard_map/ppermute | solution.py:52
  128.9 11.2 %collective-permute-start.37 = (bf16[64,4608]{1,0:T(8,128)(2,1)}, bf16[64,4608]{1,0:T(8,128)(2,1)S(1)}, u32[]{:S(2)}, u32[]{:S(2)}) collective-permute-start(bf16[64,4608]{1,0:T(8,128)(2,1)} %collective-permute-done.29.refs_0_), channel_id=1, source_target_pairs={{0,8},{8,0},{16,24},{24,16},{1,9},{9,1},{17,25},{25,17},{2,10},{10... | collective-permute-start | bytes 1769480 | tf_op jit(solution)/shard_map/ppermute | solution.py:52
  129.3 23.7 %collective-permute-start.68 = (bf16[128,4608]{1,0:T(8,128)(2,1)S(1)}, bf16[128,4608]{1,0:T(8,128)(2,1)S(1)}, u32[]{:S(2)}, u32[]{:S(2)}) collective-permute-start(bf16[128,4608]{1,0:T(8,128)(2,1)S(1)} %get-tuple-element.85.refs_0_), channel_id=1, source_target_pairs={{0,8},{8,0},{16,24},{24,16},{1,9},{9,1},{17,25},{25,17},{2,10},{10... | collective-permute-start | bytes 3538952 | tf_op jit(solution)/shard_map/ppermute | solution.py:52
  129.6 9.4 %collective-permute-start.26 = (bf16[64,2304]{1,0:T(8,128)(2,1)S(1)}, bf16[64,2304]{1,0:T(8,128)(2,1)S(1)}, u32[]{:S(2)}, u32[]{:S(2)}) collective-permute-start(bf16[64,2304]{1,0:T(8,128)(2,1)S(1)} %slice.16), channel_id=1, source_target_pairs={{0,16},{8,24},{16,0},{24,8},{1,17},{9,25},{17,1},{25,9},{2,18},{10... | collective-permute-start | bytes 884744 | tf_op jit(solution)/shard_map/ppermute | solution.py:52
  130.6 9.0 %collective-permute-start.27 = (bf16[64,2304]{1,0:T(8,128)(2,1)S(1)}, bf16[64,2304]{1,0:T(8,128)(2,1)S(1)}, u32[]{:S(2)}, u32[]{:S(2)}) collective-permute-start(bf16[64,2304]{1,0:T(8,128)(2,1)S(1)} %slice.17), channel_id=1, source_target_pairs={{0,1},{1,0},{2,3},{3,2},{4,5},{5,4},{6,7},{7,6},{8,9},{9,8},{10,11... | collective-permute-start | bytes 884744 | tf_op jit(solution)/shard_map/ppermute | solution.py:52
  139.6 10.3 %collective-permute-start.45 = (bf16[128,2304]{1,0:T(8,128)(2,1)S(1)}, bf16[128,2304]{1,0:T(8,128)(2,1)S(1)}, u32[]{:S(2)}, u32[]{:S(2)}) collective-permute-start(bf16[128,2304]{1,0:T(8,128)(2,1)S(1)} %collective-permute-done.24.refs_1_), channel_id=1, source_target_pairs={{0,8},{8,0},{16,24},{24,16},{1,9},{9,1},{17,25},{25,17},{2,10},{10... | collective-permute-start | bytes 1769480 | tf_op jit(solution)/shard_map/ppermute | solution.py:52
  140.1 10.3 %collective-permute-start.46 = (bf16[128,2304]{1,0:T(8,128)(2,1)S(1)}, bf16[128,2304]{1,0:T(8,128)(2,1)S(1)}, u32[]{:S(2)}, u32[]{:S(2)}) collective-permute-start(bf16[128,2304]{1,0:T(8,128)(2,1)S(1)} %collective-permute-done.25.refs_2_), channel_id=1, source_target_pairs={{0,8},{8,0},{16,24},{24,16},{1,9},{9,1},{17,25},{25,17},{2,10},{10... | collective-permute-start | bytes 1769480 | tf_op jit(solution)/shard_map/ppermute | solution.py:52
  140.5 13.3 %collective-permute-start.56 = (bf16[128,512]{1,0:T(8,128)(2,1)S(1)}, bf16[128,512]{1,0:T(8,128)(2,1)S(1)}, u32[]{:S(2)}, u32[]{:S(2)}) collective-permute-start(bf16[128,512]{1,0:T(8,128)(2,1)S(1)} %shard_map.207.attention.refs_0_), channel_id=1, source_target_pairs={{0,17},{1,16},{8,25},{9,24},{16,1},{17,0},{24,9},{25,8},{2,19},{3,... | collective-permute-start | bytes 393224 | tf_op jit(solution)/shard_map/ppermute | solution.py:61
  142.2 12.7 %collective-permute-start.57 = (bf16[128,512]{1,0:T(8,128)(2,1)S(1)}, bf16[128,512]{1,0:T(8,128)(2,1)}, u32[]{:S(2)}, u32[]{:S(2)}) collective-permute-start(bf16[128,512]{1,0:T(8,128)(2,1)S(1)} %shard_map.207.attention.refs_0_), channel_id=1, source_target_pairs={{0,8},{8,0},{16,24},{24,16},{1,9},{9,1},{17,25},{25,17},{2,10},{10... | collective-permute-start | bytes 393224 | tf_op jit(solution)/shard_map/ppermute | solution.py:52
  149.9 10.3 %collective-permute-start.58 = (bf16[128,512]{1,0:T(8,128)(2,1)S(1)}, bf16[128,512]{1,0:T(8,128)(2,1)S(1)}, u32[]{:S(2)}, u32[]{:S(2)}) collective-permute-start(bf16[128,512]{1,0:T(8,128)(2,1)S(1)} %collective-permute-done.54.refs_1_), channel_id=1, source_target_pairs={{0,8},{8,0},{16,24},{24,16},{1,9},{9,1},{17,25},{25,17},{2,10},{10... | collective-permute-start | bytes 393224 | tf_op jit(solution)/shard_map/ppermute | solution.py:52
  150.4 9.8 %collective-permute-start.59 = (bf16[128,512]{1,0:T(8,128)(2,1)S(1)}, bf16[128,512]{1,0:T(8,128)(2,1)S(1)}, u32[]{:S(2)}, u32[]{:S(2)}) collective-permute-start(bf16[128,512]{1,0:T(8,128)(2,1)S(1)} %collective-permute-done.55.refs_2_), channel_id=1, source_target_pairs={{0,8},{8,0},{16,24},{24,16},{1,9},{9,1},{17,25},{25,17},{2,10},{10... | collective-permute-start | bytes 393224 | tf_op jit(solution)/shard_map/ppermute | solution.py:52
  153.0 7.7 %collective-permute-start.61 = (f32[8,128]{1,0:T(8,128)S(1)}, f32[8,128]{1,0:T(8,128)S(1)}, u32[]{:S(2)}, u32[]{:S(2)}) collective-permute-start(f32[8,128]{1,0:T(8,128)S(1)} %shard_map.208.refs_8_), channel_id=1, source_target_pairs={{0,1},{1,0},{2,3},{3,2},{4,5},{5,4},{6,7},{7,6},{8,9},{9,8},{10,11... | collective-permute-start | bytes 12296 | tf_op jit(solution)/shard_map/ppermute | solution.py:52
  160.2 7.5 %collective-permute-start.60 = (bf16[128,512]{1,0:T(8,128)(2,1)S(1)}, bf16[128,512]{1,0:T(8,128)(2,1)S(1)}, u32[]{:S(2)}, u32[]{:S(2)}) collective-permute-start(bf16[128,512]{1,0:T(8,128)(2,1)S(1)} %collective-permute-done.56.refs_3_), channel_id=1, source_target_pairs={{0,8},{8,0},{16,24},{24,16},{1,9},{9,1},{17,25},{25,17},{2,10},{10... | collective-permute-start | bytes 393224 | tf_op jit(solution)/shard_map/ppermute | solution.py:52
  160.3 7.5 %collective-permute-start.64 = (f32[8,128]{1,0:T(8,128)S(1)}, f32[8,128]{1,0:T(8,128)S(1)}, u32[]{:S(2)}, u32[]{:S(2)}) collective-permute-start(f32[8,128]{1,0:T(8,128)S(1)} %shard_map.208.refs_8_), channel_id=1, source_target_pairs={{0,8},{8,0},{16,24},{24,16},{1,9},{9,1},{17,25},{25,17},{2,10},{10... | collective-permute-start | bytes 12296 | tf_op jit(solution)/shard_map/ppermute | solution.py:52
  (63 other events, 453.9 us)
